TPU v7x, 32 devices: a whole 2x2x4 slice. The times are simulated.
32 devices in a mesh: group: 2 (over x), ctx: 16 (over z, y, core).
Axes of the slice: x: 2, y: 2, z: 4, core: 2. Of those that a mesh axis runs over, the one named last changes fastest.
Arguments:
- hyena_qkv: bfloat16 [4096, 3, 2048], P(('group', 'ctx')), parts along dimension 0, may hold values from -6 to 6
- short_weight: float32 [3, 3, 2048], replicated, may hold values from -3.5 to 3.5
- filter_rate: float32 [128, 16], replicated, as said below
- filter_residue: float32 [128, 16], replicated, may hold values from -4 to 4
- attn_qkv: bfloat16 [4096, 3, 2048], P(('group', 'ctx')), parts along dimension 0, may hold values from -6 to 6
- doc_lengths: int32 [8], P('group'), parts along dimension 0, may hold values from 1 to 897, 2048 in all
Outputs:
- hyena_out: bfloat16 [4096, 2048], P(('group', 'ctx')), parts along dimension 0
- attn_out: bfloat16 [4096, 2048], P(('group', 'ctx')), parts along dimension 0
There are 2 independent parts, one for each index of `group`. A program takes and returns all parts, laid end to end along the dimension named above; an argument that names none is the same for every part. Nothing has to cross between parts.
Inputs may be any that keep to these rules, and one draw needn't show every extreme that they name: `filter_rate`: every rate is positive and at most 1/30. `doc_lengths`: the lengths sum to 2048 and the longest is exactly 897.
All inputs are finite; a program needn't handle non-finite values.
Results may differ from a plain program's by a relative error of at most 0.0054.
Values may be sent and summed in bfloat16 or wider, within the bound.
No kernel may reach another device: no remote copies, remote signals or barrier semaphores. Data moves between devices by JAX's collectives and lax.ppermute only.
A program may use at most 128 MiB of HBM per device.

v0:
```python
import functools
import math

import jax
import jax.numpy as jnp
from jax import lax
from jax.experimental import pallas as pl
from jax.experimental.pallas import tpu as pltpu
from jax.sharding import PartitionSpec as P


HEAD = 128
LANES = 128
TURNS = 1
EDGE = 8
ROW = 4


F32 = jnp.float32
BF16 = jnp.bfloat16


def flip(value, axis, bit):
    count = lax.axis_size(axis)
    return lax.ppermute(value, axis, [(at, at ^ bit) for at in range(count)])


def side_of(at):
    return at // 2 % 2


def ahead(value, axis, steps, bit=0, first=0, side=None):
    count = lax.axis_size(axis)
    pairs = [
        (at, (at + steps) ^ bit)
        for at in range(first, count - steps)
        if side is None or side_of(at) == side
    ]
    return lax.ppermute(value, axis, pairs)


def spot():
    index = lax.axis_index("ctx")
    return index & 1, lax.shift_right_logical(index, 1) & 1, index & (ROW - 1), index // ROW


ALL_VMEM = 67043328


def limits(mib):
    return pltpu.CompilerParams(vmem_limit_bytes=mib << 20)


def cost(flops, moved, exps=0):
    return pl.CostEstimate(flops=flops, bytes_accessed=moved, transcendentals=exps)


VMEM = pl.BlockSpec(memory_space=pltpu.VMEM)
SMEM = pl.BlockSpec(memory_space=pltpu.SMEM)
ANY = pl.BlockSpec(memory_space=pl.ANY)
HBM = pl.BlockSpec(memory_space=pltpu.HBM)


def same_filter(modes, width, terms, lanes):
    row_at = lax.broadcasted_iota(jnp.int32, (terms, lanes), 0)
    lane_at = lax.broadcasted_iota(jnp.int32, (terms, lanes), 1)
    kept = None
    for g in range(terms // modes):
        both = (
            (row_at >= g * modes)
            & (row_at < (g + 1) * modes)
            & (lane_at >= g * width)
            & (lane_at < (g + 1) * width)
        )
        kept = both if kept is None else kept | both
    return kept


def feature(x, halo, w_ref, stream, at):
    here = x.astype(F32)
    halo = halo.astype(F32)
    edge = halo.shape[0]
    row_at = lax.broadcasted_iota(jnp.int32, here.shape, 0)
    one = jnp.where(row_at == 0, halo[edge - 1 :], pltpu.roll(here, 1, 0))
    two = jnp.where(row_at == 1, halo[edge - 1 :], pltpu.roll(here, 2, 0))
    two = jnp.where(row_at == 0, halo[edge - 2 : edge - 1], two)
    tap = [w_ref[n, stream : stream + 1, at] for n in range(3)]
    return tap[0] * here + tap[1] * one + tap[2] * two


def of_step(table_ref):
    groups = table_ref.shape[1]
    return pltpu.roll(table_ref[...], groups - pl.program_id(0) * (groups // STEPS), 1)


def down(table, part, filters, lanes):
    columns = [table[:, part * filters + g : part * filters + g + 1] for g in range(filters)]
    return jnp.concatenate([jnp.broadcast_to(c, (c.shape[0], lanes)) for c in columns], axis=0)


def hyena_ends_body(
    filters, x_ref, halo_ref, w_ref, rate_ref, res_ref, mixed_ref, keep_ref, away_ref, wide_ref, gain_ref, all_s
):
    rows = x_ref.shape[1]
    modes, groups = rate_ref.shape
    parts = groups // STEPS // filters
    terms = filters * modes
    lanes = x_ref.shape[2] // parts
    width = lanes // filters
    rates = of_step(rate_ref)
    coeffs = of_step(res_ref) * jnp.sqrt(2.0 * rates / modes)
    lag = (rows - 1 - lax.broadcasted_iota(jnp.int32, (terms, rows), 1)).astype(F32)
    own = same_filter(modes, width, terms, lanes)
    pick = lambda matrix: jnp.sum(jnp.where(own, matrix, 0.0).reshape(filters, modes, lanes), axis=0)
    step = pl.program_id(0)
    for part in range(parts):
        at = slice(part * lanes, (part + 1) * lanes)
        key, value = (feature(x_ref[n, :, at], halo_ref[n, :, at], w_ref, n, at) for n in (1, 2))
        mixed = (key * value).astype(BF16)
        mixed_ref[:, at] = mixed
        rate = down(rates, part, filters, rows)
        powers = jnp.exp(-rate * lag)
        high = powers.astype(BF16)
        low = (powers - high.astype(F32)).astype(BF16)
        ends = jnp.dot(high, mixed, preferred_element_type=F32) + jnp.dot(
            low, mixed, preferred_element_type=F32
        )
        all_s[0, step, :, at] = pick(ends)
        all_s[1, step, :, at] = pick(rate)
        all_s[2, step, :, at] = pick(down(coeffs, part, filters, rows))

    @pl.when(step == STEPS - 1)
    def _():
        core = spot()[0]
        half = STEPS // 2
        for n in range(half):
            at = slice(n * parts * lanes, (n + 1) * parts * lanes)
            away_ref[:, at] = all_s[0, (1 - core) * half + n]
            for table, out in enumerate((keep_ref, wide_ref, gain_ref)):
                out[:, at] = all_s[table, core * half + n]


STEPS = 4


def hyena_ends(streams, halo, short_weight, rates, residues):
    _, rows, channels = streams.shape
    edge = halo.shape[1]
    modes, groups = rates.shape
    filters = groups * LANES // channels
    terms = filters * modes
    wide = channels // STEPS
    lead = lambda n: (0, 0, n)
    whole = lambda n: (0, 0)
    half = (modes, channels // 2)
    return pl.pallas_call(
        functools.partial(hyena_ends_body, filters),
        grid=(STEPS,),
        in_specs=[
            pl.BlockSpec((3, rows, wide), lead),
            pl.BlockSpec((3, edge, wide), lead),
            pl.BlockSpec((3, 3, wide), lead),
            pl.BlockSpec((modes, groups), whole),
            pl.BlockSpec((modes, groups), whole),
        ],
        out_specs=[pl.BlockSpec((rows, wide), lambda n: (0, n))] + [pl.BlockSpec(half, whole)] * 4,
        out_shape=[jax.ShapeDtypeStruct((rows, channels), BF16)] + [jax.ShapeDtypeStruct(half, F32)] * 4,
        scratch_shapes=[pltpu.VMEM((3, STEPS, modes, wide), F32)],
        compiler_params=limits(16),
        cost_estimate=cost(4 * rows * terms * channels, 8 * rows * channels),
        name="hyena_ends",
    )(streams, halo, short_weight, rates, residues)


def hyena_near_body(
    filters, x_ref, halo_ref, w_ref, mixed_ref, rate_ref, res_ref, near_ref, q_ref, high_ref, low_ref, taps_s, u_s
):
    rows = mixed_ref.shape[0]
    modes, groups = rate_ref.shape
    parts = groups // STEPS // filters
    terms = filters * modes
    lanes = mixed_ref.shape[1] // parts
    width = lanes // filters
    rates = of_step(rate_ref)
    coeffs = of_step(res_ref) * jnp.sqrt(2.0 * rates / modes)
    row_at = lax.broadcasted_iota(jnp.int32, (rows, lanes), 0)
    lane_at = lax.broadcasted_iota(jnp.int32, (rows, lanes), 1)
    lag = (rows - 1 - lax.broadcasted_iota(jnp.int32, (terms, rows), 1)).astype(F32)
    ahead_lag = (1 + lax.broadcasted_iota(jnp.int32, (terms, rows), 1)).astype(F32)
    zero = jnp.zeros((rows, lanes), BF16)
    for part in range(parts):
        at = slice(part * lanes, (part + 1) * lanes)
        mixed = mixed_ref[:, at]
        rate = down(rates, part, filters, rows)
        powers = down(coeffs, part, filters, rows) * jnp.exp(-rate * lag)
        backward = jnp.sum(powers.reshape(filters, modes, rows), axis=1)
        for g in range(filters):
            spread = jnp.broadcast_to(backward[g : g + 1], (rows, rows))
            shifted = pltpu.roll(spread, 1, 1, stride=1, stride_axis=0)
            kept = jnp.where(lane_at <= row_at, shifted, 0.0)
            taps_s[part, :, g * rows : (g + 1) * rows] = kept.astype(BF16)
            mine = (lane_at >= g * width) & (lane_at < (g + 1) * width)
            u_s[part, g * rows : (g + 1) * rows, :] = jnp.where(mine, mixed, zero)
        near_ref[:, at] = jnp.dot(taps_s[part], u_s[part], preferred_element_type=F32)
        q_ref[:, at] = feature(x_ref[0, :, at], halo_ref[0, :, at], w_ref, 0, at)
        decays = jnp.exp(-rate * ahead_lag).T
        here = slice(part * terms, (part + 1) * terms)
        high = decays.astype(BF16)
        high_ref[:, here] = high
        low_ref[:, here] = (decays - high.astype(F32)).astype(BF16)


def hyena_near(streams, halo, short_weight, mixed, rates, residues):
    rows, channels = mixed.shape
    edge = halo.shape[1]
    modes, groups = rates.shape
    lanes = LANES
    filters = groups * lanes // channels
    terms = filters * modes
    parts = groups // STEPS // filters
    wide = channels // STEPS
    by_block = lambda n: (0, n)
    lead = lambda n: (0, 0, n)
    whole = lambda n: (0, 0)
    return pl.pallas_call(
        functools.partial(hyena_near_body, filters),
        grid=(STEPS,),
        in_specs=[
            pl.BlockSpec((1, rows, wide), lead),
            pl.BlockSpec((1, edge, wide), lead),
            pl.BlockSpec((3, 3, wide), lead),
            pl.BlockSpec((rows, wide), by_block),
            pl.BlockSpec((modes, groups), whole),
            pl.BlockSpec((modes, groups), whole),
        ],
        out_specs=[pl.BlockSpec((rows, wide), by_block)] * 2 + [pl.BlockSpec((rows, parts * terms), by_block)] * 2,
        out_shape=[jax.ShapeDtypeStruct((rows, channels), F32)] * 2
        + [jax.ShapeDtypeStruct((rows, groups * modes), BF16)] * 2,
        scratch_shapes=[
            pltpu.VMEM((parts, rows, filters * rows), BF16),
            pltpu.VMEM((parts, filters * rows, lanes), BF16),
        ],
        compiler_params=limits(16),
        cost_estimate=cost(2 * rows * rows * filters * channels, 12 * rows * channels),
        name="hyena_near",
    )(streams, halo, short_weight, mixed, rates, residues)


def hyena_out_body(modes, near_ref, q_ref, high_ref, low_ref, keep_ref, back_ref, out_ref):
    wide = near_ref.shape[1]
    terms = high_ref.shape[1] * LANES // wide
    filters = terms // modes
    own = same_filter(modes, LANES // filters, terms, LANES)
    mine = pl.program_id(0) // (STEPS // 2) == spot()[0]
    for part in range(wide // LANES):
        at = slice(part * LANES, (part + 1) * LANES)
        here = slice(part * terms, (part + 1) * terms)
        carried = jnp.where(mine, keep_ref[:, at], back_ref[:, at])
        carried = jnp.where(own, jnp.concatenate([carried] * filters, axis=0), 0.0)
        c_high = carried.astype(BF16)
        c_low = (carried - c_high.astype(F32)).astype(BF16)
        high, low = high_ref[:, here], low_ref[:, here]
        far = (
            jnp.dot(high, c_high, preferred_element_type=F32)
            + jnp.dot(low, c_high, preferred_element_type=F32)
            + jnp.dot(high, c_low, preferred_element_type=F32)
        )
        out_ref[:, at] = (q_ref[:, at] * (near_ref[:, at] + far)).astype(BF16)


def hyena_finish(near, query, high, low, keep, back):
    rows, channels = near.shape
    modes = keep.shape[0]
    wide = channels // STEPS
    by_block = lambda n: (0, n)
    by_half = lambda n: (0, n % (STEPS // 2))
    return pl.pallas_call(
        functools.partial(hyena_out_body, modes),
        grid=(STEPS,),
        in_specs=[
            pl.BlockSpec((rows, wide), by_block),
            pl.BlockSpec((rows, wide), by_block),
            pl.BlockSpec((rows, high.shape[1] // STEPS), by_block),
            pl.BlockSpec((rows, high.shape[1] // STEPS), by_block),
            pl.BlockSpec((modes, wide), by_half),
            pl.BlockSpec((modes, wide), by_half),
        ],
        out_specs=pl.BlockSpec((rows, wide), by_block),
        out_shape=jax.ShapeDtypeStruct((rows, channels), BF16),
        compiler_params=limits(16),
        cost_estimate=cost(6 * rows * high.size, 10 * rows * channels),
        name="hyena_finish",
    )(near, query, high, low, keep, back)


def small(body, *operands, outs=1):
    def kernel(*refs):
        made = body(*(ref[...] for ref in refs[: len(operands)]))
        for ref, value in zip(refs[len(operands) :], made if outs > 1 else (made,)):
            ref[...] = value

    shape = pltpu.VMEM(operands[0].shape, operands[0].dtype)
    made = pl.pallas_call(
        kernel,
        in_specs=[VMEM] * len(operands),
        out_specs=[VMEM] * outs,
        out_shape=[shape] * outs,
        compiler_params=limits(4),
        cost_estimate=cost(operands[0].size, 4 * operands[0].size),
    )(*operands)
    return made if outs > 1 else made[0]


def scan_states(keep, away, rate, gain, rows):
    count = lax.axis_size("ctx") // ROW
    decay = lambda blocks, rate: jnp.exp(-rate * float(rows * blocks))

    def both(mine, theirs, rate):
        first = spot()[0] == 0
        even = jnp.where(first, mine, theirs)
        return decay(1, rate) * even + jnp.where(first, theirs, mine), even

    theirs = flip(away, "ctx", 1)
    chip, even = small(both, keep, theirs, rate, outs=2)

    def whole(mine, other, rate):
        first = spot()[1] == 0
        left = jnp.where(first, mine, other)
        return decay(2, rate) * left + jnp.where(first, other, mine), left

    other = flip(chip, "ctx", 2)
    total, left = small(whole, chip, other, rate, outs=2)
    before = ahead(total, "ctx", ROW)
    reach = 2
    while reach < count:
        upto = small(lambda total, before, rate: total + decay(ROW, rate) * before, total, before, rate)
        earlier = ahead(upto, "ctx", ROW * reach)
        reach *= 2
        if reach < count:
            before = small(
                lambda before, earlier, rate: before + decay(ROW * (reach // 2 - 1), rate) * earlier,
                before,
                earlier,
                rate,
            )

    def last(before, earlier, left, even, rate, gain):
        before = before + decay(ROW * (reach // 2 - 1), rate) * earlier
        core, side, _, _ = spot()
        before = jnp.where(side == 0, before, decay(2, rate) * before + left)
        second = decay(1, rate) * before + even
        return (
            gain * jnp.where(core == 0, before, second),
            gain * jnp.where(core == 0, second, before),
        )

    if count == 2:
        earlier = jnp.zeros_like(before)
    if count > 1:
        mine, away = small(last, before, earlier, left, even, rate, gain, outs=2)
    return mine, flip(away, "ctx", 1)


def lanes_from(start, size):
    return pl.ds(pl.multiple_of(start * size, size), size)


def front_body(attn, hyena, theirs_ref, edge_ref, sems):
    rows, half = theirs_ref.shape[1:]
    away = attn.at[:, :, lanes_from(1 - spot()[0], half)]
    edge = hyena.at[:, rows - EDGE : rows, :]
    copies = [
        pltpu.make_async_copy(away, theirs_ref, sems.at[0]),
        pltpu.make_async_copy(edge, edge_ref, sems.at[1]),
    ]
    for copy in copies:
        copy.start()
    for copy in copies:
        copy.wait()


def front(attn, hyena):
    count, rows, channels = attn.shape
    return pl.pallas_call(
        front_body,
        in_specs=[HBM, HBM],
        out_specs=[VMEM, VMEM],
        out_shape=[
            pltpu.VMEM((count, rows, channels // 2), attn.dtype),
            pltpu.VMEM((count, EDGE, channels), hyena.dtype),
        ],
        scratch_shapes=[pltpu.SemaphoreType.DMA((2,))],
        compiler_params=pltpu.CompilerParams(vmem_limit_bytes=ALL_VMEM - (26 << 17)),
        cost_estimate=cost(0, 4 * count * rows * channels // 2),
        name="front",
    )(attn, hyena)


def pack_body(first, streams_ref, theirs_ref, *outs):
    core, side, _, _ = spot()
    slots = (0, 1) if first == 0 else (1 - core, core)
    quarter = theirs_ref.shape[2] // 2
    for out, away in zip(outs, (0, 1)[-len(outs) :]):
        to = 1 - side if away else side
        for stream in range(first, 3):
            out[slots[0], stream - first] = streams_ref[stream, :, lanes_from(2 * core + to, quarter)]
            out[slots[1], stream - first] = theirs_ref[stream, :, lanes_from(to, quarter)]


def pack(streams, theirs, first, amount):
    _, rows, half = theirs.shape
    shape = pltpu.VMEM((2, 3 - first, rows, half // 2), BF16)
    return pl.pallas_call(
        functools.partial(pack_body, first),
        in_specs=[VMEM, VMEM],
        out_specs=[VMEM] * amount,
        out_shape=[shape] * amount,
        compiler_params=limits(10),
        cost_estimate=cost(0, 8 * amount * rows * half),
        name="pack",
    )(streams, theirs)


def odd_body(wanted, pairs, out_ref, sem):
    @pl.when(spot()[1] == wanted)
    def _():
        copy = pltpu.make_async_copy(pairs.at[0:1], out_ref, sem)
        copy.start()
        copy.wait()


def odd(pairs, wanted):
    return pl.pallas_call(
        functools.partial(odd_body, wanted),
        in_specs=[ANY],
        out_specs=VMEM,
        out_shape=pltpu.VMEM((1,) + pairs.shape[1:], pairs.dtype),
        scratch_shapes=[pltpu.SemaphoreType.DMA],
        compiler_params=limits(4),
        cost_estimate=cost(0, pairs.size * 2),
        name="odd",
    )(pairs)


def contig_start(docs_ref, position):
    first = jnp.zeros_like(position)
    bound = jnp.int32(0)
    for n in range(docs_ref.shape[0]):
        bound = bound + docs_ref[n]
        first = jnp.where(position >= bound, bound, first)
    return first


def row_part(streams, theirs, swap, slot, stream, head, quarter):
    core, side, _, _ = spot()
    if slot < 2:
        start = (side if slot else 2 * core + side) * quarter + head * HEAD
        lanes = pl.ds(pl.multiple_of(start, HEAD), HEAD)
        return theirs[stream, :, lanes] if slot else streams[stream, :, lanes]
    return swap[slot - 2, stream, :, head * HEAD : (head + 1) * HEAD]


SCALE = math.log2(math.e) / math.sqrt(HEAD)


CHUNK = 32


def softmax_group(queries, keys, values, bias, turn, s_s, p_s, keep):
    tall, rows = queries.shape[0], keys[0].shape[0]
    width = len(keys) * rows
    for n in range(0, len(keys), 2):
        s_s[turn, 0:tall, n * rows : (n + 2) * rows] = lax.dot_general(
            queries,
            jnp.concatenate(keys[n : n + 2], axis=0),
            (((1,), (1,)), ((), ())),
            preferred_element_type=F32,
        )
    for m in range(0, tall, CHUNK):
        some = slice(m, m + CHUNK)
        top = None
        parts = []
        for n in range(0, width, LANES):
            part = s_s[turn, some, n : n + LANES] + bias[some, n : n + LANES]
            parts.append(part)
            top = part if top is None else jnp.maximum(top, part)
        top = jnp.broadcast_to(jnp.max(top, axis=1, keepdims=True), (CHUNK, LANES))
        below = jnp.zeros((CHUNK, LANES), F32)
        for n, part in enumerate(parts):
            weight = jnp.exp2((part - top) * SCALE)
            below = below + weight
            p_s[turn, some, n * LANES : (n + 1) * LANES] = weight.astype(BF16)
        keep(m, top, jnp.broadcast_to(jnp.sum(below, axis=1, keepdims=True), (CHUNK, LANES)))
    return jnp.dot(
        p_s[turn, 0:tall, 0:width], jnp.concatenate(values, axis=0), preferred_element_type=F32
    )


def attend_body(docs_ref, streams, theirs, swap, own, cross, acc_ref, m_ref, l_ref, bias_s, s_s, p_s):
    _, side, place, row = spot()
    rows, quarter = own.shape[2:]
    base = row * (ROW * rows)
    part = functools.partial(row_part, streams, theirs, swap, quarter=quarter)

    def run(first_pair, second_pair):
        for group, (asking, seen) in enumerate(((first_pair, first_pair), (second_pair, (0, 1, 2, 3)))):
            starts = [base + (2 * (side if old else 1 - side) + 1 - n - ROW) * rows for old in (1, 0) for n in (0, 1)]
            starts += [base + (place ^ slot) * rows for slot in seen]
            for at, slot in enumerate(asking):
                position = base + (place ^ slot) * rows + lax.broadcasted_iota(jnp.int32, (rows, 1), 0)
                first = contig_start(docs_ref, position)
                for n, start in enumerate(starts):
                    token = start + lax.broadcasted_iota(jnp.int32, (rows, rows), 1)
                    bias_s[group, at * rows : (at + 1) * rows, n * rows : (n + 1) * rows] = jnp.where(
                        (token >= first) & (token <= position), 0.0, -jnp.inf
                    )
            for head in range(quarter // HEAD):
                lanes = slice(head * HEAD, (head + 1) * HEAD)
                olds = lambda kind: [old[n, kind, :, lanes] for old in (own, cross) for n in (0, 1)]

                def keep(m, top, below):
                    out = slice(asking[0] * rows + m, asking[0] * rows + m + CHUNK)
                    m_ref[out, lanes] = top
                    l_ref[out, lanes] = below

                acc_ref[asking[0] * rows : (asking[1] + 1) * rows, lanes] = softmax_group(
                    jnp.concatenate([part(slot, 0, head) for slot in asking], axis=0),
                    olds(0) + [part(slot, 1, head) for slot in seen],
                    olds(1) + [part(slot, 2, head) for slot in seen],
                    bias_s.at[group],
                    head % 2,
                    s_s,
                    p_s,
                    keep,
                )

    @pl.when(side == 0)
    def _():
        run((0, 1), (2, 3))

    @pl.when(side == 1)
    def _():
        run((2, 3), (0, 1))


def attend(doc_lengths, streams, theirs, swap, own, cross):
    _, _, rows, quarter = own.shape
    heads = quarter // HEAD
    return pl.pallas_call(
        attend_body,
        in_specs=[SMEM] + [VMEM] * 5,
        out_specs=[VMEM] * 3,
        out_shape=[
            jax.ShapeDtypeStruct((ROW * rows, quarter), F32),
        ]
        * 3,
        scratch_shapes=[
            pltpu.VMEM((2, 2 * rows, 2 * ROW * rows), F32),
            pltpu.VMEM((2, 2 * rows, 2 * ROW * rows), F32),
            pltpu.VMEM((2, 2 * rows, 2 * ROW * rows), BF16),
        ],
        compiler_params=limits(20),
        cost_estimate=cost(26 * 4 * rows * rows * quarter, 14 * ROW * rows * quarter, 26 * heads * rows * rows),
        name="attend",
    )(doc_lengths, streams, theirs, swap, own, cross)


def attend_last_body(heads, docs_ref, streams, theirs, swap, *refs):
    cross_l, own_s, own_l, cross_s, acc_ref, m_ref, l_ref = refs[:7]
    outs = refs[7:]
    _, side, place, row = spot()
    rows, quarter = acc_ref.shape[0] // ROW, acc_ref.shape[1]
    base = row * (ROW * rows)

    def run(early, late, large, small):
        for asking, blocks in ((early, ((small, 0), (large, 1), (large, 0))), (late, ((large, 0),))):
            width = len(blocks) * rows
            here = slice(asking[0] * rows, (asking[1] + 1) * rows)
            token = base - (ROW + len(blocks)) * rows + lax.broadcasted_iota(jnp.int32, (rows, width), 1)
            allowed = []
            for slot in asking:
                position = base + (place ^ slot) * rows + lax.broadcasted_iota(jnp.int32, (rows, 1), 0)
                allowed.append((token >= contig_start(docs_ref, position)).astype(jnp.int32))
            allowed = jnp.concatenate(allowed, axis=0) != 0
            lanes_of = [slice(head * HEAD, (head + 1) * HEAD) for head in heads]
            stack = lambda kind, lanes: jnp.concatenate([ref[n, kind, :, lanes] for ref, n in blocks], axis=0)
            scores = [
                lax.dot_general(
                    jnp.concatenate(
                        [row_part(streams, theirs, swap, slot, 0, head, quarter) for slot in asking], axis=0
                    ),
                    stack(0, lanes_of[head - heads[0]]),
                    (((1,), (1,)), ((), ())),
                    preferred_element_type=F32,
                )
                for head in heads
            ]
            scores = [jnp.where(allowed, score, -jnp.inf) for score in scores]
            tops = [
                jnp.maximum(m_ref[here, lanes], jnp.max(score, axis=1, keepdims=True))
                for lanes, score in zip(lanes_of, scores)
            ]
            weights = [
                jnp.exp2((score - jnp.concatenate([top] * len(blocks), axis=1)) * SCALE)
                for score, top in zip(scores, tops)
            ]
            for lanes, top, weight in zip(lanes_of, tops, weights):
                fade = jnp.exp2((m_ref[here, lanes] - top) * SCALE)
                share = 1.0 / (l_ref[here, lanes] * fade + jnp.sum(weight, axis=1, keepdims=True))
                more = jnp.dot(weight.astype(BF16), stack(1, lanes), preferred_element_type=F32)
                made = ((acc_ref[here, lanes] * fade + more) * share).astype(BF16)
                put = slice(lanes.start - heads[0] * HEAD, lanes.stop - heads[0] * HEAD)
                for n, slot in enumerate(asking):
                    outs[slot][:, put] = made[n * rows : (n + 1) * rows]

    @pl.when(side == 0)
    def _():
        run((0, 1), (2, 3), cross_l, own_s)

    @pl.when(side == 1)
    def _():
        run((2, 3), (0, 1), own_l, cross_s)


def attend_last(heads, doc_lengths, streams, theirs, swap, olds, acc, top, below):
    rows = acc.shape[0] // ROW
    lanes = len(heads) * HEAD
    return pl.pallas_call(
        functools.partial(attend_last_body, heads),
        in_specs=[SMEM] + [VMEM] * 10,
        out_specs=[VMEM] * ROW,
        out_shape=[jax.ShapeDtypeStruct((rows, lanes), BF16)] * ROW,
        compiler_params=limits(16),
        cost_estimate=cost(32 * rows * rows * lanes, 48 * rows * lanes, 8 * len(heads) * rows * rows),
        name="attend_last",
    )(doc_lengths, streams, theirs, swap, *olds, acc, top, below)


def assemble_body(*refs):
    place = spot()[2]
    *pieces, out_ref = refs
    turns = len(pieces) // ROW
    lanes = pieces[0].shape[1]
    for n, piece in enumerate(pieces):
        maker = place ^ (n % ROW)
        which = 2 * (maker & 1) + lax.shift_right_logical(maker, 1)
        out_ref[:, lanes_from(which * turns + n // ROW, lanes)] = piece[...]


def assemble(pieces):
    rows, lanes = pieces[0].shape
    return pl.pallas_call(
        assemble_body,
        in_specs=[VMEM] * len(pieces),
        out_specs=VMEM,
        out_shape=jax.ShapeDtypeStruct((rows, len(pieces) * lanes), BF16),
        compiler_params=limits(6),
        cost_estimate=cost(0, 4 * rows * lanes * len(pieces)),
        name="assemble",
    )(*pieces)


def on_device(hyena_qkv, short_weight, filter_rate, filter_residue, attn_qkv, doc_lengths):
    rows = attn_qkv.shape[0]
    inner = hyena_qkv.transpose(1, 0, 2)
    streams = attn_qkv.transpose(1, 0, 2)
    rates, residues = filter_rate.T, filter_residue.T
    theirs, edge = front(streams, inner)

    theirs = flip(theirs, "ctx", 1)
    edge = ahead(edge, "ctx", 1)
    own, cross = pack(streams, theirs, 1, 2)
    cross = ahead(cross, "ctx", ROW, 2)
    own = ahead(own, "ctx", ROW)
    (swap,) = pack(streams, theirs, 0, 1)
    swap = flip(swap, "ctx", 2)
    olds = (
        ahead(cross, "ctx", ROW, 0, ROW, 0),
        ahead(odd(own, 0), "ctx", ROW, 0, ROW, 0),
        ahead(own, "ctx", ROW, 0, ROW, 1),
        ahead(odd(cross, 1), "ctx", ROW, 0, ROW, 1),
    )

    mixed, keep, away, wide, gain = hyena_ends(inner, edge, short_weight, rates, residues)
    near, query, high, low = hyena_near(inner, edge, short_weight, mixed, rates, residues)
    keep, back = scan_states(keep, away, wide, gain, rows)
    hyena_out = hyena_finish(near, query, high, low, keep, back)

    acc, top, below = attend(doc_lengths, streams, theirs, swap, own, cross)
    pieces = []
    heads = acc.shape[1] // HEAD
    for turn in range(TURNS):
        these = range(turn * heads // TURNS, (turn + 1) * heads // TURNS)
        made = attend_last(these, doc_lengths, streams, theirs, swap, olds, acc, top, below)
        pieces.append(made[0])
        pieces += [flip(made[n], "ctx", n) for n in range(1, ROW)]
    attn_out = assemble(pieces)
    return (hyena_out, attn_out)


def solution(mesh):
    in_specs = (
        P(("group", "ctx"), None, None),
        P(),
        P(),
        P(),
        P(("group", "ctx"), None, None),
        P("group"),
    )
    out_specs = (P(("group", "ctx"), None), P(("group", "ctx"), None))
    return jax.shard_map(on_device, mesh=mesh, in_specs=in_specs, out_specs=out_specs, check_vma=False)
```

profile of v0, /device:TPU:0, one launch (start us, length us, event | category | flops | bytes accessed | tf_op | source)
XLA Modules:
  0.0 81.2 jit_solution(6666490989395298872)
XLA Ops:
  0.6 1.3 %front.1 = (bf16[3,128,1024]{2,1,0:T(8,128)(2,1)S(1)}, bf16[3,8,2048]{2,1,0:T(8,128)(2,1)S(1)}) custom-call(bf16[3,128,2048]{2,1,0:T(8,128)(2,1)} %bitcast.4, bf16[3,128,2048]{2,1,0:T(8,128)(2,1)} %bitcast.9), custom_call_target="tpu_custom_call" | custom-call | bytes 1572864 | tf_op jit(solution)/shard_map/front/pallas_call | solution.py:384
  1.9 0.6 collective-permute-start.6
  2.5 1.9 %collective-permute-done.6.theirs_ref.theirs = bf16[3,128,1024]{2,1,0:T(8,128)(2,1)S(1)} collective-permute-done((bf16[3,128,1024]{2,1,0:T(8,128)(2,1)S(1)}, bf16[3,128,1024]{2,1,0:T(8,128)(2,1)S(1)}, u32[]{:S(2)}, u32[]{:S(2)}) %collective-permute-start.6) | collective-permute-done | bytes 786464 | tf_op jit(solution)/shard_map/ppermute | solution.py:25
  4.4 0.1 pack.3
  4.5 4.9 %collective-permute-start.10 = (bf16[2,2,128,512]{3,2,1,0:T(8,128)(2,1)S(1)}, bf16[2,2,128,512]{3,2,1,0:T(8,128)(2,1)S(1)}, u32[]{:S(2)}, u32[]{:S(2)}) collective-permute-start(bf16[2,2,128,512]{3,2,1,0:T(8,128)(2,1)S(1)} %get-tuple-element.46), channel_id=1, source_target_pairs={{0,4},{1,5},{2,6},{3,7},{4,8},{5,9},{6,10},{7,11},{8,12},{9,13},{1... | collective-permute-start | bytes 1572872 | tf_op jit(solution)/shard_map/ppermute | solution.py:39
  9.4 4.6 %collective-permute-start.8 = (bf16[2,2,128,512]{3,2,1,0:T(8,128)(2,1)S(1)}, bf16[2,2,128,512]{3,2,1,0:T(8,128)(2,1)S(1)}, u32[]{:S(2)}, u32[]{:S(2)}) collective-permute-start(bf16[2,2,128,512]{3,2,1,0:T(8,128)(2,1)S(1)} %get-tuple-element.45), channel_id=1, source_target_pairs={{0,6},{1,7},{2,4},{3,5},{4,10},{5,11},{6,8},{7,9},{8,14},{9,15},{1... | collective-permute-start | bytes 1572872 | tf_op jit(solution)/shard_map/ppermute | solution.py:39
  14.0 0.1 pack.2
  14.1 0.6 collective-permute-start.7
  14.6 1.3 %collective-permute-start = (bf16[3,8,2048]{2,1,0:T(8,128)(2,1)S(1)}, bf16[3,8,2048]{2,1,0:T(8,128)(2,1)S(1)}, u32[]{:S(2)}, u32[]{:S(2)}) collective-permute-start(bf16[3,8,2048]{2,1,0:T(8,128)(2,1)S(1)} %get-tuple-element.28), channel_id=1, source_target_pairs={{0,1},{1,2},{2,3},{3,4},{4,5},{5,6},{6,7},{7,8},{8,9},{9,10},{10,1... | collective-permute-start | bytes 294920 | tf_op jit(solution)/shard_map/ppermute | solution.py:39
  15.9 5.7 %collective-permute-done.10.pairs.own = bf16[2,2,128,512]{3,2,1,0:T(8,128)(2,1)S(1)} collective-permute-done((bf16[2,2,128,512]{3,2,1,0:T(8,128)(2,1)S(1)}, bf16[2,2,128,512]{3,2,1,0:T(8,128)(2,1)S(1)}, u32[]{:S(2)}, u32[]{:S(2)}) %collective-permute-start.10) | collective-permute-done | bytes 524320 | tf_op jit(solution)/shard_map/ppermute | solution.py:39
  21.6 0.7 collective-permute-start.12
  22.3 9.8 %collective-permute-done.8.pairs.cross = bf16[2,2,128,512]{3,2,1,0:T(8,128)(2,1)S(1)} collective-permute-done((bf16[2,2,128,512]{3,2,1,0:T(8,128)(2,1)S(1)}, bf16[2,2,128,512]{3,2,1,0:T(8,128)(2,1)S(1)}, u32[]{:S(2)}, u32[]{:S(2)}) %collective-permute-start.8) | collective-permute-done | bytes 524320 | tf_op jit(solution)/shard_map/ppermute | solution.py:39
  32.1 0.7 collective-permute-start.9
  32.8 2.3 %hyena_ends.1 = (bf16[128,2048]{1,0:T(8,128)(2,1)S(1)}, f32[16,1024]{1,0:T(8,128)S(1)}, f32[16,1024]{1,0:T(8,128)S(1)}, f32[16,1024]{1,0:T(8,128)S(1)}, f32[16,1024]{1,0:T(8,128)S(1)}) custom-call(bf16[3,128,2048]{2,1,0:T(8,128)(2,1)S(1)} %bitcast.10, bf16[3,8,2048]{2,1,0:T(8,128)(2,1)S(1)} %collective-permute-done.halo_ref, f32[3,3,2048]{2,1,0:T(4,128)S(1)} %copy-done.2, ...), custom_call_target="tpu_custom_call" | custom-call | flops 134217728 | bytes 2097152 | tf_op jit(solution)/shard_map/hyena_ends/pallas_call | solution.py:156
  35.2 0.1 collective-permute-start.1
  35.2 1.2 %collective-permute-done.1.refs_1_ = f32[16,1024]{1,0:T(8,128)S(1)} collective-permute-done((f32[16,1024]{1,0:T(8,128)S(1)}, f32[16,1024]{1,0:T(8,128)S(1)}, u32[]{:S(2)}, u32[]{:S(2)}) %collective-permute-start.1) | collective-permute-done | bytes 65568 | tf_op jit(solution)/shard_map/ppermute | solution.py:25
  36.5 2.4 %collective-permute-start.2 = (f32[16,1024]{1,0:T(8,128)S(1)}, f32[16,1024]{1,0:T(8,128)S(1)}, u32[]{:S(2)}, u32[]{:S(2)}) collective-permute-start(f32[16,1024]{1,0:T(8,128)S(1)} %get-tuple-element.37.refs_0_), channel_id=1, source_target_pairs={{0,2},{1,3},{2,0},{3,1},{4,6},{5,7},{6,4},{7,5},{8,10},{9,11},{10,... | collective-permute-start | bytes 196616 | tf_op jit(solution)/shard_map/ppermute | solution.py:25
  38.9 2.4 %collective-permute-done.2.refs_1_ = f32[16,1024]{1,0:T(8,128)S(1)} collective-permute-done((f32[16,1024]{1,0:T(8,128)S(1)}, f32[16,1024]{1,0:T(8,128)S(1)}, u32[]{:S(2)}, u32[]{:S(2)}) %collective-permute-start.2) | collective-permute-done | bytes 65568 | tf_op jit(solution)/shard_map/ppermute | solution.py:25
  41.4 13.9 %collective-permute-start.3 = (f32[16,1024]{1,0:T(8,128)S(1)}, f32[16,1024]{1,0:T(8,128)S(1)}, u32[]{:S(2)}, u32[]{:S(2)}) collective-permute-start(f32[16,1024]{1,0:T(8,128)S(1)} %get-tuple-element.38.refs_0_), channel_id=1, source_target_pairs={{0,4},{1,5},{2,6},{3,7},{4,8},{5,9},{6,10},{7,11},{8,12},{9,13},{1... | collective-permute-start | bytes 196616 | tf_op jit(solution)/shard_map/ppermute | solution.py:39
  55.3 0.7 collective-permute-start.11
  56.0 1.1 %collective-permute-done.3.refs_1_.refs_0_ = f32[16,1024]{1,0:T(8,128)S(1)} collective-permute-done((f32[16,1024]{1,0:T(8,128)S(1)}, f32[16,1024]{1,0:T(8,128)S(1)}, u32[]{:S(2)}, u32[]{:S(2)}) %collective-permute-start.3) | collective-permute-done | bytes 65568 | tf_op jit(solution)/shard_map/ppermute | solution.py:39
  57.2 0.7 collective-permute-start.13
  57.9 4.5 %collective-permute-start.4 = (f32[16,1024]{1,0:T(8,128)S(1)}, f32[16,1024]{1,0:T(8,128)S(1)}, u32[]{:S(2)}, u32[]{:S(2)}) collective-permute-start(f32[16,1024]{1,0:T(8,128)S(1)} %shard_map.79), channel_id=1, source_target_pairs={{0,8},{1,9},{2,10},{3,11},{4,12},{5,13},{6,14},{7,15},{16,24},{17,... | collective-permute-start | bytes 196616 | tf_op jit(solution)/shard_map/ppermute | solution.py:39
  62.3 4.9 %attend.1 = (f32[512,512]{1,0:T(8,128)S(1)}, f32[512,512]{1,0:T(8,128)S(1)}, f32[512,512]{1,0:T(8,128)S(1)}) custom-call(s32[4]{0:T(128)S(1)} %copy-done.5, bf16[3,128,2048]{2,1,0:T(8,128)(2,1)S(1)} %bitcast.7, bf16[3,128,1024]{2,1,0:T(8,128)(2,1)S(1)} %collective-permute-done.6.theirs_ref.theirs, bf16[2,3,128,512]{3,2,1,0:T(8,128)(2,1)S(1)} %collective-permute-done.7.swap, ...), custom_call_target="tpu_custom_call" | custom-call | flops 872415232 | bytes 3670016 | tf_op jit(solution)/shard_map/attend/pallas_call | solution.py:549
  67.2 2.1 %attend_last.1 = (bf16[128,512]{1,0:T(8,128)(2,1)S(1)}, bf16[128,512]{1,0:T(8,128)(2,1)S(1)}, bf16[128,512]{1,0:T(8,128)(2,1)S(1)}, bf16[128,512]{1,0:T(8,128)(2,1)S(1)}) custom-call(s32[4]{0:T(128)S(1)} %copy-done.5, bf16[3,128,2048]{2,1,0:T(8,128)(2,1)S(1)} %bitcast.8, bf16[3,128,1024]{2,1,0:T(8,128)(2,1)S(1)} %collective-permute-done.6.theirs_ref.theirs, ...), custom_call_target="tpu_custom_call" | custom-call | flops 268435456 | bytes 3145728 | tf_op jit(solution)/shard_map/attend_last/pallas_call | solution.py:628
  69.4 0.1 collective-permute-start.14
  69.4 3.1 %collective-permute-start.15 = (bf16[128,512]{1,0:T(8,128)(2,1)S(1)}, bf16[128,512]{1,0:T(8,128)(2,1)S(1)}, u32[]{:S(2)}, u32[]{:S(2)}) collective-permute-start(bf16[128,512]{1,0:T(8,128)(2,1)S(1)} %get-tuple-element.52), channel_id=1, source_target_pairs={{0,2},{1,3},{2,0},{3,1},{4,6},{5,7},{6,4},{7,5},{8,10},{9,11},{10,... | collective-permute-start | bytes 393224 | tf_op jit(solution)/shard_map/ppermute | solution.py:25
  72.5 0.1 shard_map.80
  72.6 0.2 collective-permute-start.5
  72.8 5.1 %hyena_near.1 = (f32[128,2048]{1,0:T(8,128)S(1)}, f32[128,2048]{1,0:T(8,128)S(1)}, bf16[128,2048]{1,0:T(8,128)(2,1)S(1)}, bf16[128,2048]{1,0:T(8,128)(2,1)S(1)}) custom-call(bf16[3,128,2048]{2,1,0:T(8,128)(2,1)S(1)} %bitcast.11, bf16[3,8,2048]{2,1,0:T(8,128)(2,1)S(1)} %collective-permute-done.halo_ref, f32[3,3,2048]{2,1,0:T(4,128)S(1)} %copy-done.2, ...), custom_call_target="tpu_custom_call" | custom-call | flops 536870912 | bytes 3145728 | tf_op jit(solution)/shard_map/hyena_near/pallas_call | solution.py:225
  77.9 2.4 %hyena_finish.1 = bf16[128,2048]{1,0:T(8,128)(2,1)} custom-call(f32[128,2048]{1,0:T(8,128)S(1)} %get-tuple-element.30.near_ref, f32[128,2048]{1,0:T(8,128)S(1)} %get-tuple-element.31.q_ref, bf16[128,2048]{1,0:T(8,128)(2,1)S(1)} %get-tuple-element.32.high_ref, bf16[128,2048]{1,0:T(8,128)(2,1)S(1)} %get-tuple-element.33.low_ref, ...), custom_call_target="tpu_custom_call" | custom-call | flops 201326592 | bytes 2621440 | tf_op jit(solution)/shard_map/hyena_finish/pallas_call | solution.py:277
  80.3 0.8 %assemble.1 = bf16[128,2048]{1,0:T(8,128)(2,1)} custom-call(bf16[128,512]{1,0:T(8,128)(2,1)S(1)} %get-tuple-element.50.refs_0_, bf16[128,512]{1,0:T(8,128)(2,1)S(1)} %collective-permute-done.14.refs_1_, bf16[128,512]{1,0:T(8,128)(2,1)S(1)} %collective-permute-done.15.refs_2_, bf16[128,512]{1,0:T(8,128)(2,1)S(1)} %collective-permute-done.16.refs_3_), custom_call_target="tpu_custom_call" | custom-call | bytes 1048576 | tf_op jit(solution)/shard_map/assemble/pallas_call | solution.py:652
  (29 shorter events, 0.2 us)
Async XLA Ops:
  0.6 3.8 %copy-start = (bf16[128,3,2048]{2,0,1:T(8,128)(2,1)S(1)}, bf16[128,3,2048]{2,0,1:T(8,128)(2,1)}, u32[]{:S(2)}) copy-start(bf16[128,3,2048]{2,0,1:T(8,128)(2,1)} %param.10) | copy-start | bytes 4718596
  1.9 2.5 %collective-permute-start.6 = (bf16[3,128,1024]{2,1,0:T(8,128)(2,1)S(1)}, bf16[3,128,1024]{2,1,0:T(8,128)(2,1)S(1)}, u32[]{:S(2)}, u32[]{:S(2)}) collective-permute-start(bf16[3,128,1024]{2,1,0:T(8,128)(2,1)S(1)} %get-tuple-element.44), channel_id=1, source_target_pairs={{0,1},{1,0},{2,3},{3,2},{4,5},{5,4},{6,7},{7,6},{8,9},{9,8},{10,11... | collective-permute-start | bytes 2359304 | tf_op jit(solution)/shard_map/ppermute | solution.py:25
  4.5 17.1 %collective-permute-start.10 = (bf16[2,2,128,512]{3,2,1,0:T(8,128)(2,1)S(1)}, bf16[2,2,128,512]{3,2,1,0:T(8,128)(2,1)S(1)}, u32[]{:S(2)}, u32[]{:S(2)}) collective-permute-start(bf16[2,2,128,512]{3,2,1,0:T(8,128)(2,1)S(1)} %get-tuple-element.46), channel_id=1, source_target_pairs={{0,4},{1,5},{2,6},{3,7},{4,8},{5,9},{6,10},{7,11},{8,12},{9,13},{1... | collective-permute-start | bytes 1572872 | tf_op jit(solution)/shard_map/ppermute | solution.py:39
  9.4 23.4 %copy-start.1 = (bf16[128,3,2048]{2,0,1:T(8,128)(2,1)S(1)}, bf16[128,3,2048]{2,0,1:T(8,128)(2,1)}, u32[]{:S(2)}) copy-start(bf16[128,3,2048]{2,0,1:T(8,128)(2,1)} %param.6) | copy-start | bytes 4718596
  9.4 23.4 %copy-start.2 = (f32[3,3,2048]{2,1,0:T(4,128)S(1)}, f32[3,3,2048]{2,1,0:T(4,128)}, u32[]{:S(2)}) copy-start(f32[3,3,2048]{2,1,0:T(4,128)} %w_ref.3) | copy-start | bytes 221188
  9.4 23.4 %copy-start.3 = (f32[128,16]{0,1:T(8,128)S(1)}, f32[128,16]{0,1:T(8,128)}, u32[]{:S(2)}) copy-start(f32[128,16]{0,1:T(8,128)} %param.8) | copy-start | bytes 24580
  9.4 23.4 %copy-start.4 = (f32[128,16]{0,1:T(8,128)S(1)}, f32[128,16]{0,1:T(8,128)}, u32[]{:S(2)}) copy-start(f32[128,16]{0,1:T(8,128)} %param.9) | copy-start | bytes 24580
  9.4 22.7 %collective-permute-start.8 = (bf16[2,2,128,512]{3,2,1,0:T(8,128)(2,1)S(1)}, bf16[2,2,128,512]{3,2,1,0:T(8,128)(2,1)S(1)}, u32[]{:S(2)}, u32[]{:S(2)}) collective-permute-start(bf16[2,2,128,512]{3,2,1,0:T(8,128)(2,1)S(1)} %get-tuple-element.45), channel_id=1, source_target_pairs={{0,6},{1,7},{2,4},{3,5},{4,10},{5,11},{6,8},{7,9},{8,14},{9,15},{1... | collective-permute-start | bytes 1572872 | tf_op jit(solution)/shard_map/ppermute | solution.py:39
  14.1 43.8 %collective-permute-start.7 = (bf16[2,3,128,512]{3,2,1,0:T(8,128)(2,1)S(1)}, bf16[2,3,128,512]{3,2,1,0:T(8,128)(2,1)S(1)}, u32[]{:S(2)}, u32[]{:S(2)}) collective-permute-start(bf16[2,3,128,512]{3,2,1,0:T(8,128)(2,1)S(1)} %pack.2), channel_id=1, source_target_pairs={{0,2},{1,3},{2,0},{3,1},{4,6},{5,7},{6,4},{7,5},{8,10},{9,11},{10,... | collective-permute-start | bytes 2359304 | tf_op jit(solution)/shard_map/ppermute | solution.py:25
  14.6 18.1 %collective-permute-start = (bf16[3,8,2048]{2,1,0:T(8,128)(2,1)S(1)}, bf16[3,8,2048]{2,1,0:T(8,128)(2,1)S(1)}, u32[]{:S(2)}, u32[]{:S(2)}) collective-permute-start(bf16[3,8,2048]{2,1,0:T(8,128)(2,1)S(1)} %get-tuple-element.28), channel_id=1, source_target_pairs={{0,1},{1,2},{2,3},{3,4},{4,5},{5,6},{6,7},{7,8},{8,9},{9,10},{10,1... | collective-permute-start | bytes 294920 | tf_op jit(solution)/shard_map/ppermute | solution.py:39
  21.6 45.6 %collective-permute-start.12 = (bf16[2,2,128,512]{3,2,1,0:T(8,128)(2,1)S(1)}, bf16[2,2,128,512]{3,2,1,0:T(8,128)(2,1)S(1)}, u32[]{:S(2)}, u32[]{:S(2)}) collective-permute-start(bf16[2,2,128,512]{3,2,1,0:T(8,128)(2,1)S(1)} %collective-permute-done.10.pairs.own), channel_id=1, source_target_pairs={{6,10},{7,11},{10,14},{11,15},{22,26},{23,27},{26,30},{27,31}} | collective-permute-start | bytes 1572872 | tf_op jit(solution)/shard_map/ppermute | solution.py:39
  32.1 35.2 %collective-permute-start.9 = (bf16[2,2,128,512]{3,2,1,0:T(8,128)(2,1)S(1)}, bf16[2,2,128,512]{3,2,1,0:T(8,128)(2,1)S(1)}, u32[]{:S(2)}, u32[]{:S(2)}) collective-permute-start(bf16[2,2,128,512]{3,2,1,0:T(8,128)(2,1)S(1)} %collective-permute-done.8.pairs.cross), channel_id=1, source_target_pairs={{4,8},{5,9},{8,12},{9,13},{20,24},{21,25},{24,28},{25,29}} | collective-permute-start | bytes 1572872 | tf_op jit(solution)/shard_map/ppermute | solution.py:39
  32.8 29.5 %copy-start.5 = (s32[4]{0:T(128)S(1)}, s32[4]{0:T(128)}, u32[]{:S(2)}) copy-start(s32[4]{0:T(128)} %docs_ref.3) | copy-start | bytes 52
  35.2 1.3 %collective-permute-start.1 = (f32[16,1024]{1,0:T(8,128)S(1)}, f32[16,1024]{1,0:T(8,128)S(1)}, u32[]{:S(2)}, u32[]{:S(2)}) collective-permute-start(f32[16,1024]{1,0:T(8,128)S(1)} %get-tuple-element.35), channel_id=1, source_target_pairs={{0,1},{1,0},{2,3},{3,2},{4,5},{5,4},{6,7},{7,6},{8,9},{9,8},{10,11... | collective-permute-start | bytes 196616 | tf_op jit(solution)/shard_map/ppermute | solution.py:25
  36.5 4.8 %collective-permute-start.2 = (f32[16,1024]{1,0:T(8,128)S(1)}, f32[16,1024]{1,0:T(8,128)S(1)}, u32[]{:S(2)}, u32[]{:S(2)}) collective-permute-start(f32[16,1024]{1,0:T(8,128)S(1)} %get-tuple-element.37.refs_0_), channel_id=1, source_target_pairs={{0,2},{1,3},{2,0},{3,1},{4,6},{5,7},{6,4},{7,5},{8,10},{9,11},{10,... | collective-permute-start | bytes 196616 | tf_op jit(solution)/shard_map/ppermute | solution.py:25
  41.4 15.8 %collective-permute-start.3 = (f32[16,1024]{1,0:T(8,128)S(1)}, f32[16,1024]{1,0:T(8,128)S(1)}, u32[]{:S(2)}, u32[]{:S(2)}) collective-permute-start(f32[16,1024]{1,0:T(8,128)S(1)} %get-tuple-element.38.refs_0_), channel_id=1, source_target_pairs={{0,4},{1,5},{2,6},{3,7},{4,8},{5,9},{6,10},{7,11},{8,12},{9,13},{1... | collective-permute-start | bytes 196616 | tf_op jit(solution)/shard_map/ppermute | solution.py:39
  55.3 11.9 %collective-permute-start.11 = (bf16[1,2,128,512]{3,2,1,0:T(8,128)(2,1)S(1)}, bf16[1,2,128,512]{3,2,1,0:T(8,128)(2,1)S(1)}, u32[]{:S(2)}, u32[]{:S(2)}) collective-permute-start(bf16[1,2,128,512]{3,2,1,0:T(8,128)(2,1)S(1)} %odd.2), channel_id=1, source_target_pairs={{4,8},{5,9},{8,12},{9,13},{20,24},{21,25},{24,28},{25,29}} | collective-permute-start | bytes 786440 | tf_op jit(solution)/shard_map/ppermute | solution.py:39
  57.2 10.1 %collective-permute-start.13 = (bf16[1,2,128,512]{3,2,1,0:T(8,128)(2,1)S(1)}, bf16[1,2,128,512]{3,2,1,0:T(8,128)(2,1)S(1)}, u32[]{:S(2)}, u32[]{:S(2)}) collective-permute-start(bf16[1,2,128,512]{3,2,1,0:T(8,128)(2,1)S(1)} %odd.3), channel_id=1, source_target_pairs={{6,10},{7,11},{10,14},{11,15},{22,26},{23,27},{26,30},{27,31}} | collective-permute-start | bytes 786440 | tf_op jit(solution)/shard_map/ppermute | solution.py:39
  57.9 14.7 %collective-permute-start.4 = (f32[16,1024]{1,0:T(8,128)S(1)}, f32[16,1024]{1,0:T(8,128)S(1)}, u32[]{:S(2)}, u32[]{:S(2)}) collective-permute-start(f32[16,1024]{1,0:T(8,128)S(1)} %shard_map.79), channel_id=1, source_target_pairs={{0,8},{1,9},{2,10},{3,11},{4,12},{5,13},{6,14},{7,15},{16,24},{17,... | collective-permute-start | bytes 196616 | tf_op jit(solution)/shard_map/ppermute | solution.py:39
  69.4 11.0 %collective-permute-start.14 = (bf16[128,512]{1,0:T(8,128)(2,1)S(1)}, bf16[128,512]{1,0:T(8,128)(2,1)S(1)}, u32[]{:S(2)}, u32[]{:S(2)}) collective-permute-start(bf16[128,512]{1,0:T(8,128)(2,1)S(1)} %get-tuple-element.51), channel_id=1, source_target_pairs={{0,1},{1,0},{2,3},{3,2},{4,5},{5,4},{6,7},{7,6},{8,9},{9,8},{10,11... | collective-permute-start | bytes 393224 | tf_op jit(solution)/shard_map/ppermute | solution.py:25
  69.4 10.9 %collective-permute-start.15 = (bf16[128,512]{1,0:T(8,128)(2,1)S(1)}, bf16[128,512]{1,0:T(8,128)(2,1)S(1)}, u32[]{:S(2)}, u32[]{:S(2)}) collective-permute-start(bf16[128,512]{1,0:T(8,128)(2,1)S(1)} %get-tuple-element.52), channel_id=1, source_target_pairs={{0,2},{1,3},{2,0},{3,1},{4,6},{5,7},{6,4},{7,5},{8,10},{9,11},{10,... | collective-permute-start | bytes 393224 | tf_op jit(solution)/shard_map/ppermute | solution.py:25
  72.5 7.8 %collective-permute-start.16 = (bf16[128,512]{1,0:T(8,128)(2,1)S(1)}, bf16[128,512]{1,0:T(8,128)(2,1)S(1)}, u32[]{:S(2)}, u32[]{:S(2)}) collective-permute-start(bf16[128,512]{1,0:T(8,128)(2,1)S(1)} %get-tuple-element.53), channel_id=1, source_target_pairs={{0,3},{1,2},{2,1},{3,0},{4,7},{5,6},{6,5},{7,4},{8,11},{9,10},{10,... | collective-permute-start | bytes 393224 | tf_op jit(solution)/shard_map/ppermute | solution.py:25
  72.6 5.3 %collective-permute-start.5 = (f32[16,1024]{1,0:T(8,128)S(1)}, f32[16,1024]{1,0:T(8,128)S(1)}, u32[]{:S(2)}, u32[]{:S(2)}) collective-permute-start(f32[16,1024]{1,0:T(8,128)S(1)} %get-tuple-element.43), channel_id=1, source_target_pairs={{0,1},{1,0},{2,3},{3,2},{4,5},{5,4},{6,7},{7,6},{8,9},{9,8},{10,11... | collective-permute-start | bytes 196616 | tf_op jit(solution)/shard_map/ppermute | solution.py:25
where the time goes:
time: 81.5 us; the launch traced here: 81.2 us
  starting transfers between devices  38.8 us (48%)
  waiting for transfers between devices  22.2 us (27%)
  Pallas kernels  19.2 us (24%)
  between operations  0.96 us (1%)
    ppermute x9, starting transfers between devices, ahead(): return lax.ppermute(value, axis, pairs)  31.8 us
    ppermute x9, waiting for transfers between devices, ahead(): return lax.ppermute(value, axis, pairs)  16.6 us
    ppermute x8, starting transfers between devices, flip(): return lax.ppermute(value, axis, [(at, at ^ bit) for at in range(count)])  6.99 us
    ppermute x8, waiting for transfers between devices, flip(): return lax.ppermute(value, axis, [(at, at ^ bit) for at in range(count)])  5.58 us
    pallas_call x1, Pallas kernels, hyena_near(): pl.pallas_call(functools.partial(hyena_near_body, filters), grid=(STEPS,)...  5.05 us
    pallas_call x1, Pallas kernels, attend(): pl.pallas_call(attend_body, in_specs=[SMEM] + [VMEM] * 5, out_specs=[VMEM...  4.85 us
    pallas_call x1, Pallas kernels, hyena_finish(): pl.pallas_call(functools.partial(hyena_out_body, modes), grid=(STEPS,), i...  2.44 us
    pallas_call x1, Pallas kernels, hyena_ends(): pl.pallas_call(functools.partial(hyena_ends_body, filters), grid=(STEPS,)...  2.32 us
  transfers between devices with their start and end apart: 17, of which 6 were waited for; matrix products, arithmetic and copies ran while one was open for 0% of the time, Pallas kernels for 21%

commit v1 on v0

--- a/solution.py
+++ b/solution.py
@@ -11,7 +11,6 @@
 
 HEAD = 128
 LANES = 128
-TURNS = 1
 EDGE = 8
 ROW = 4
 
@@ -565,15 +564,28 @@
     )(doc_lengths, streams, theirs, swap, own, cross)
 
 
-def attend_last_body(heads, docs_ref, streams, theirs, swap, *refs):
-    cross_l, own_s, own_l, cross_s, acc_ref, m_ref, l_ref = refs[:7]
-    outs = refs[7:]
+def merge(scores, values, past, below, total):
+    top = jnp.maximum(past, jnp.max(scores, axis=1, keepdims=True))
+    fade = jnp.exp2((past - top) * SCALE)
+    weight = jnp.exp2((scores - jnp.concatenate([top] * (scores.shape[1] // LANES), axis=1)) * SCALE)
+    below = below * fade + jnp.sum(weight, axis=1, keepdims=True)
+    total = total * fade + jnp.dot(weight.astype(BF16), values, preferred_element_type=F32)
+    return top, below, total
+
+
+def product(queries, keys):
+    return lax.dot_general(queries, keys, (((1,), (1,)), ((), ())), preferred_element_type=F32)
+
+
+def attend_mid_body(docs_ref, streams, theirs, swap, cross_l, own_l, acc_ref, m_ref, l_ref, *refs):
+    outs, (acc_out, m_out, l_out, q_out) = refs[:ROW], refs[ROW:]
     _, side, place, row = spot()
     rows, quarter = acc_ref.shape[0] // ROW, acc_ref.shape[1]
     base = row * (ROW * rows)
-
-    def run(early, late, large, small):
-        for asking, blocks in ((early, ((small, 0), (large, 1), (large, 0))), (late, ((large, 0),))):
+    all_lanes = [slice(n, n + HEAD) for n in range(0, quarter, HEAD)]
+
+    def run(early, late, large):
+        for asking, blocks in ((early, (1, 0)), (late, (0,))):
             width = len(blocks) * rows
             here = slice(asking[0] * rows, (asking[1] + 1) * rows)
             token = base - (ROW + len(blocks)) * rows + lax.broadcasted_iota(jnp.int32, (rows, width), 1)
@@ -582,82 +594,129 @@
                 position = base + (place ^ slot) * rows + lax.broadcasted_iota(jnp.int32, (rows, 1), 0)
                 allowed.append((token >= contig_start(docs_ref, position)).astype(jnp.int32))
             allowed = jnp.concatenate(allowed, axis=0) != 0
-            lanes_of = [slice(head * HEAD, (head + 1) * HEAD) for head in heads]
-            stack = lambda kind, lanes: jnp.concatenate([ref[n, kind, :, lanes] for ref, n in blocks], axis=0)
-            scores = [
-                lax.dot_general(
-                    jnp.concatenate(
-                        [row_part(streams, theirs, swap, slot, 0, head, quarter) for slot in asking], axis=0
-                    ),
-                    stack(0, lanes_of[head - heads[0]]),
-                    (((1,), (1,)), ((), ())),
-                    preferred_element_type=F32,
+            stack = lambda kind, lanes: jnp.concatenate([large[n, kind, :, lanes] for n in blocks], axis=0)
+            queries = [
+                jnp.concatenate([row_part(streams, theirs, swap, slot, 0, head, quarter) for slot in asking], axis=0)
+                for head in range(len(all_lanes))
+            ]
+            scores = [product(query, stack(0, lanes)) for query, lanes in zip(queries, all_lanes)]
+            scores = [jnp.where(allowed, score, -jnp.inf) for score in scores]
+            for lanes, query, score in zip(all_lanes, queries, scores):
+                top, below, total = merge(
+                    score, stack(1, lanes), m_ref[here, lanes], l_ref[here, lanes], acc_ref[here, lanes]
                 )
-                for head in heads
-            ]
-            scores = [jnp.where(allowed, score, -jnp.inf) for score in scores]
-            tops = [
-                jnp.maximum(m_ref[here, lanes], jnp.max(score, axis=1, keepdims=True))
-                for lanes, score in zip(lanes_of, scores)
-            ]
-            weights = [
-                jnp.exp2((score - jnp.concatenate([top] * len(blocks), axis=1)) * SCALE)
-                for score, top in zip(scores, tops)
-            ]
-            for lanes, top, weight in zip(lanes_of, tops, weights):
-                fade = jnp.exp2((m_ref[here, lanes] - top) * SCALE)
-                share = 1.0 / (l_ref[here, lanes] * fade + jnp.sum(weight, axis=1, keepdims=True))
-                more = jnp.dot(weight.astype(BF16), stack(1, lanes), preferred_element_type=F32)
-                made = ((acc_ref[here, lanes] * fade + more) * share).astype(BF16)
-                put = slice(lanes.start - heads[0] * HEAD, lanes.stop - heads[0] * HEAD)
+                made = (total * (1.0 / below)).astype(BF16)
                 for n, slot in enumerate(asking):
-                    outs[slot][:, put] = made[n * rows : (n + 1) * rows]
+                    outs[slot][:, lanes] = made[n * rows : (n + 1) * rows]
+                if asking is early:
+                    m_out[:, lanes], l_out[:, lanes], acc_out[:, lanes] = top, below, total
+                    q_out[:, lanes] = query
 
     @pl.when(side == 0)
     def _():
-        run((0, 1), (2, 3), cross_l, own_s)
+        run((0, 1), (2, 3), cross_l)
 
     @pl.when(side == 1)
     def _():
-        run((2, 3), (0, 1), own_l, cross_s)
-
-
-def attend_last(heads, doc_lengths, streams, theirs, swap, olds, acc, top, below):
-    rows = acc.shape[0] // ROW
-    lanes = len(heads) * HEAD
-    return pl.pallas_call(
-        functools.partial(attend_last_body, heads),
-        in_specs=[SMEM] + [VMEM] * 10,
-        out_specs=[VMEM] * ROW,
-        out_shape=[jax.ShapeDtypeStruct((rows, lanes), BF16)] * ROW,
+        run((2, 3), (0, 1), own_l)
+
+
+def attend_mid(doc_lengths, streams, theirs, swap, cross_l, own_l, acc, top, below):
+    rows, quarter = acc.shape[0] // ROW, acc.shape[1]
+    pair = jax.ShapeDtypeStruct((2 * rows, quarter), F32)
+    return pl.pallas_call(
+        attend_mid_body,
+        in_specs=[SMEM] + [VMEM] * 8,
+        out_specs=[VMEM] * (ROW + 4),
+        out_shape=[jax.ShapeDtypeStruct((rows, quarter), BF16)] * ROW
+        + [pair] * 3
+        + [jax.ShapeDtypeStruct((2 * rows, quarter), BF16)],
         compiler_params=limits(16),
-        cost_estimate=cost(32 * rows * rows * lanes, 48 * rows * lanes, 8 * len(heads) * rows * rows),
+        cost_estimate=cost(24 * rows * rows * quarter, 48 * rows * quarter, 24 * rows * rows),
+        name="attend_mid",
+    )(doc_lengths, streams, theirs, swap, cross_l, own_l, acc, top, below)
+
+
+def attend_last_body(docs_ref, own_s, cross_s, acc_ref, m_ref, l_ref, q_ref, out_ref):
+    core, side, _, row = spot()
+    rows, quarter = out_ref.shape
+    base = row * (ROW * rows)
+    here = pl.ds(pl.multiple_of(core * rows, rows), rows)
+    position = base + lax.broadcasted_iota(jnp.int32, (rows, 1), 0)
+    token = base - (2 * ROW - 1) * rows + lax.broadcasted_iota(jnp.int32, (rows, rows), 1)
+    allowed = token >= contig_start(docs_ref, position)
+
+    def run(odd_block):
+        all_lanes = [slice(n, n + HEAD) for n in range(0, quarter, HEAD)]
+        scores = [product(q_ref[here, lanes], odd_block[0, 0, :, lanes]) for lanes in all_lanes]
+        for lanes, score in zip(all_lanes, scores):
+            _, below, total = merge(
+                jnp.where(allowed, score, -jnp.inf),
+                odd_block[0, 1, :, lanes],
+                m_ref[here, lanes],
+                l_ref[here, lanes],
+                acc_ref[here, lanes],
+            )
+            out_ref[:, lanes] = (total * (1.0 / below)).astype(BF16)
+
+    @pl.when(side == 0)
+    def _():
+        run(own_s)
+
+    @pl.when(side == 1)
+    def _():
+        run(cross_s)
+
+
+def attend_last(doc_lengths, own_s, cross_s, acc, top, below, queries):
+    rows, quarter = acc.shape[0] // 2, acc.shape[1]
+    return pl.pallas_call(
+        attend_last_body,
+        in_specs=[SMEM] + [VMEM] * 6,
+        out_specs=VMEM,
+        out_shape=jax.ShapeDtypeStruct((rows, quarter), BF16),
+        compiler_params=limits(16),
+        cost_estimate=cost(4 * rows * rows * quarter, 16 * rows * quarter, 4 * rows * rows),
         name="attend_last",
-    )(doc_lengths, streams, theirs, swap, *olds, acc, top, below)
+    )(doc_lengths, own_s, cross_s, acc, top, below, queries)
 
 
 def assemble_body(*refs):
     place = spot()[2]
     *pieces, out_ref = refs
-    turns = len(pieces) // ROW
-    lanes = pieces[0].shape[1]
-    for n, piece in enumerate(pieces):
-        maker = place ^ (n % ROW)
-        which = 2 * (maker & 1) + lax.shift_right_logical(maker, 1)
-        out_ref[:, lanes_from(which * turns + n // ROW, lanes)] = piece[...]
-
-
-def assemble(pieces):
-    rows, lanes = pieces[0].shape
+    quarter = pieces[0].shape[1]
+
+    def run(chosen):
+        for slot, piece in enumerate(chosen):
+            maker = place ^ slot
+            which = 2 * (maker & 1) + lax.shift_right_logical(maker, 1)
+            out_ref[:, lanes_from(which, quarter)] = piece[...]
+
+    @pl.when(place == 0)
+    def _():
+        run(pieces[ROW:])
+
+    @pl.when(place != 0)
+    def _():
+        run(pieces[:ROW])
+
+
+def assemble(soon, late):
+    rows, quarter = soon[0].shape
     return pl.pallas_call(
         assemble_body,
-        in_specs=[VMEM] * len(pieces),
+        in_specs=[VMEM] * (2 * ROW),
         out_specs=VMEM,
-        out_shape=jax.ShapeDtypeStruct((rows, len(pieces) * lanes), BF16),
+        out_shape=jax.ShapeDtypeStruct((rows, ROW * quarter), BF16),
         compiler_params=limits(6),
-        cost_estimate=cost(0, 4 * rows * lanes * len(pieces)),
+        cost_estimate=cost(0, 16 * rows * quarter),
         name="assemble",
-    )(*pieces)
+    )(*soon, *late)
+
+
+def to_first(value, axis, place):
+    count = lax.axis_size(axis)
+    return lax.ppermute(value, axis, [(at, at - place) for at in range(place, count, ROW)])
 
 
 def on_device(hyena_qkv, short_weight, filter_rate, filter_residue, attn_qkv, doc_lengths):
@@ -687,14 +746,12 @@
     hyena_out = hyena_finish(near, query, high, low, keep, back)
 
     acc, top, below = attend(doc_lengths, streams, theirs, swap, own, cross)
-    pieces = []
-    heads = acc.shape[1] // HEAD
-    for turn in range(TURNS):
-        these = range(turn * heads // TURNS, (turn + 1) * heads // TURNS)
-        made = attend_last(these, doc_lengths, streams, theirs, swap, olds, acc, top, below)
-        pieces.append(made[0])
-        pieces += [flip(made[n], "ctx", n) for n in range(1, ROW)]
-    attn_out = assemble(pieces)
+    cross_l, own_s, own_l, cross_s = olds
+    *made, acc, top, below, queries = attend_mid(doc_lengths, streams, theirs, swap, cross_l, own_l, acc, top, below)
+    soon = [made[0]] + [flip(made[n], "ctx", n) for n in range(1, ROW)]
+    first = attend_last(doc_lengths, own_s, cross_s, acc, top, below, queries)
+    late = [first] + [to_first(first, "ctx", n) for n in range(1, ROW)]
+    attn_out = assemble(soon, late)
     return (hyena_out, attn_out)
 
 

time: 81.5 us -> 94.9 us (1.16)
  the two profiles are of different devices: /device:TPU:0 before, /device:TPU:1 now
where the time goes in v1:
time: 94.9 us; the launch traced here: 94.5 us
  starting transfers between devices  47.7 us (50%)
  waiting for transfers between devices  25.7 us (27%)
  Pallas kernels  20.1 us (21%)
  between operations  0.97 us (1%)
    ppermute x9, starting transfers between devices, ahead(): return lax.ppermute(value, axis, pairs)  34.3 us
    ppermute x9, waiting for transfers between devices, ahead(): return lax.ppermute(value, axis, pairs)  19.9 us
    ppermute x8, starting transfers between devices, flip(): return lax.ppermute(value, axis, [(at, at ^ bit) for at in range(count)])  9.14 us
    ppermute x8, waiting for transfers between devices, flip(): return lax.ppermute(value, axis, [(at, at ^ bit) for at in range(count)])  5.83 us
    pallas_call x1, Pallas kernels, hyena_near(): pl.pallas_call(functools.partial(hyena_near_body, filters), grid=(STEPS,)...  5.08 us
    pallas_call x1, Pallas kernels, attend(): pl.pallas_call(attend_body, in_specs=[SMEM] + [VMEM] * 5, out_specs=[VMEM...  4.88 us
    ppermute x3, starting transfers between devices, to_first(): lax.ppermute(value, axis, [(at, at - place) for at in range(place, count,...  4.29 us
    pallas_call x1, Pallas kernels, hyena_finish(): pl.pallas_call(functools.partial(hyena_out_body, modes), grid=(STEPS,), i...  2.44 us
  transfers between devices with their start and end apart: 20, of which 7 were waited for; matrix products, arithmetic and copies ran while one was open for 0% of the time, Pallas kernels for 19%

profile of v1, /device:TPU:1, one launch (start us, length us, event | category | flops | bytes accessed | tf_op | source)
XLA Modules:
  0.0 94.5 jit_solution(14948680072382358361)
XLA Ops:
  0.6 1.3 %front.1 = (bf16[3,128,1024]{2,1,0:T(8,128)(2,1)S(1)}, bf16[3,8,2048]{2,1,0:T(8,128)(2,1)S(1)}) custom-call(bf16[3,128,2048]{2,1,0:T(8,128)(2,1)} %bitcast.4, bf16[3,128,2048]{2,1,0:T(8,128)(2,1)} %bitcast.9), custom_call_target="tpu_custom_call" | custom-call | bytes 1572864 | tf_op jit(solution)/shard_map/front/pallas_call | solution.py:383
  2.0 2.3 %collective-permute-done.6.theirs_ref.theirs = bf16[3,128,1024]{2,1,0:T(8,128)(2,1)S(1)} collective-permute-done((bf16[3,128,1024]{2,1,0:T(8,128)(2,1)S(1)}, bf16[3,128,1024]{2,1,0:T(8,128)(2,1)S(1)}, u32[]{:S(2)}, u32[]{:S(2)}) %collective-permute-start.6) | collective-permute-done | bytes 786464 | tf_op jit(solution)/shard_map/ppermute | solution.py:24
  4.4 5.3 %collective-permute-start.8 = (bf16[2,2,128,512]{3,2,1,0:T(8,128)(2,1)S(1)}, bf16[2,2,128,512]{3,2,1,0:T(8,128)(2,1)S(1)}, u32[]{:S(2)}, u32[]{:S(2)}) collective-permute-start(bf16[2,2,128,512]{3,2,1,0:T(8,128)(2,1)S(1)} %get-tuple-element.49), channel_id=1, source_target_pairs={{0,6},{1,7},{2,4},{3,5},{4,10},{5,11},{6,8},{7,9},{8,14},{9,15},{1... | collective-permute-start | bytes 1572872 | tf_op jit(solution)/shard_map/ppermute | solution.py:38
  9.7 3.3 %collective-permute-start.10 = (bf16[2,2,128,512]{3,2,1,0:T(8,128)(2,1)S(1)}, bf16[2,2,128,512]{3,2,1,0:T(8,128)(2,1)S(1)}, u32[]{:S(2)}, u32[]{:S(2)}) collective-permute-start(bf16[2,2,128,512]{3,2,1,0:T(8,128)(2,1)S(1)} %get-tuple-element.50), channel_id=1, source_target_pairs={{0,4},{1,5},{2,6},{3,7},{4,8},{5,9},{6,10},{7,11},{8,12},{9,13},{1... | collective-permute-start | bytes 1572872 | tf_op jit(solution)/shard_map/ppermute | solution.py:38
  13.1 0.3 collective-permute-start.7
  13.4 7.1 %collective-permute-done.8.cross.pairs = bf16[2,2,128,512]{3,2,1,0:T(8,128)(2,1)S(1)} collective-permute-done((bf16[2,2,128,512]{3,2,1,0:T(8,128)(2,1)S(1)}, bf16[2,2,128,512]{3,2,1,0:T(8,128)(2,1)S(1)}, u32[]{:S(2)}, u32[]{:S(2)}) %collective-permute-start.8) | collective-permute-done | bytes 524320 | tf_op jit(solution)/shard_map/ppermute | solution.py:38
  20.6 0.7 collective-permute-start.9
  21.3 10.5 %collective-permute-done.10.own.pairs = bf16[2,2,128,512]{3,2,1,0:T(8,128)(2,1)S(1)} collective-permute-done((bf16[2,2,128,512]{3,2,1,0:T(8,128)(2,1)S(1)}, bf16[2,2,128,512]{3,2,1,0:T(8,128)(2,1)S(1)}, u32[]{:S(2)}, u32[]{:S(2)}) %collective-permute-start.10) | collective-permute-done | bytes 524320 | tf_op jit(solution)/shard_map/ppermute | solution.py:38
  31.8 0.7 collective-permute-start.11
  32.5 3.2 %collective-permute-start = (bf16[3,8,2048]{2,1,0:T(8,128)(2,1)S(1)}, bf16[3,8,2048]{2,1,0:T(8,128)(2,1)S(1)}, u32[]{:S(2)}, u32[]{:S(2)}) collective-permute-start(bf16[3,8,2048]{2,1,0:T(8,128)(2,1)S(1)} %get-tuple-element.32), channel_id=1, source_target_pairs={{0,1},{1,2},{2,3},{3,4},{4,5},{5,6},{6,7},{7,8},{8,9},{9,10},{10,1... | collective-permute-start | bytes 294920 | tf_op jit(solution)/shard_map/ppermute | solution.py:38
  35.8 1.6 %collective-permute-done.halo_ref = bf16[3,8,2048]{2,1,0:T(8,128)(2,1)S(1)} collective-permute-done((bf16[3,8,2048]{2,1,0:T(8,128)(2,1)S(1)}, bf16[3,8,2048]{2,1,0:T(8,128)(2,1)S(1)}, u32[]{:S(2)}, u32[]{:S(2)}) %collective-permute-start) | collective-permute-done | bytes 98336 | tf_op jit(solution)/shard_map/ppermute | solution.py:38
  37.4 2.3 %hyena_ends.1 = (bf16[128,2048]{1,0:T(8,128)(2,1)S(1)}, f32[16,1024]{1,0:T(8,128)S(1)}, f32[16,1024]{1,0:T(8,128)S(1)}, f32[16,1024]{1,0:T(8,128)S(1)}, f32[16,1024]{1,0:T(8,128)S(1)}) custom-call(bf16[3,128,2048]{2,1,0:T(8,128)(2,1)S(1)} %bitcast.10, bf16[3,8,2048]{2,1,0:T(8,128)(2,1)S(1)} %collective-permute-done.halo_ref, f32[3,3,2048]{2,1,0:T(4,128)S(1)} %copy-done.2, ...), custom_call_target="tpu_custom_call" | custom-call | flops 134217728 | bytes 2097152 | tf_op jit(solution)/shard_map/hyena_ends/pallas_call | solution.py:155
  39.8 1.2 %collective-permute-done.1.refs_1_ = f32[16,1024]{1,0:T(8,128)S(1)} collective-permute-done((f32[16,1024]{1,0:T(8,128)S(1)}, f32[16,1024]{1,0:T(8,128)S(1)}, u32[]{:S(2)}, u32[]{:S(2)}) %collective-permute-start.1) | collective-permute-done | bytes 65568 | tf_op jit(solution)/shard_map/ppermute | solution.py:24
  41.1 3.2 %collective-permute-start.2 = (f32[16,1024]{1,0:T(8,128)S(1)}, f32[16,1024]{1,0:T(8,128)S(1)}, u32[]{:S(2)}, u32[]{:S(2)}) collective-permute-start(f32[16,1024]{1,0:T(8,128)S(1)} %get-tuple-element.41.refs_0_), channel_id=1, source_target_pairs={{0,2},{1,3},{2,0},{3,1},{4,6},{5,7},{6,4},{7,5},{8,10},{9,11},{10,... | collective-permute-start | bytes 196616 | tf_op jit(solution)/shard_map/ppermute | solution.py:24
  44.3 2.3 %collective-permute-done.2.refs_1_ = f32[16,1024]{1,0:T(8,128)S(1)} collective-permute-done((f32[16,1024]{1,0:T(8,128)S(1)}, f32[16,1024]{1,0:T(8,128)S(1)}, u32[]{:S(2)}, u32[]{:S(2)}) %collective-permute-start.2) | collective-permute-done | bytes 65568 | tf_op jit(solution)/shard_map/ppermute | solution.py:24
  46.6 11.0 %collective-permute-start.3 = (f32[16,1024]{1,0:T(8,128)S(1)}, f32[16,1024]{1,0:T(8,128)S(1)}, u32[]{:S(2)}, u32[]{:S(2)}) collective-permute-start(f32[16,1024]{1,0:T(8,128)S(1)} %get-tuple-element.42.refs_0_), channel_id=1, source_target_pairs={{0,4},{1,5},{2,6},{3,7},{4,8},{5,9},{6,10},{7,11},{8,12},{9,13},{1... | collective-permute-start | bytes 196616 | tf_op jit(solution)/shard_map/ppermute | solution.py:38
  57.6 0.7 collective-permute-start.16
  58.4 0.5 collective-permute-done.3.refs_1_.refs_0_
  58.9 0.7 collective-permute-start.15
  59.6 8.7 %collective-permute-start.4 = (f32[16,1024]{1,0:T(8,128)S(1)}, f32[16,1024]{1,0:T(8,128)S(1)}, u32[]{:S(2)}, u32[]{:S(2)}) collective-permute-start(f32[16,1024]{1,0:T(8,128)S(1)} %shard_map.79), channel_id=1, source_target_pairs={{0,8},{1,9},{2,10},{3,11},{4,12},{5,13},{6,14},{7,15},{16,24},{17,... | collective-permute-start | bytes 196616 | tf_op jit(solution)/shard_map/ppermute | solution.py:38
  68.4 4.9 %attend.1 = (f32[512,512]{1,0:T(8,128)S(1)}, f32[512,512]{1,0:T(8,128)S(1)}, f32[512,512]{1,0:T(8,128)S(1)}) custom-call(s32[4]{0:T(128)S(1)} %copy-done.5, bf16[3,128,2048]{2,1,0:T(8,128)(2,1)S(1)} %bitcast.7, bf16[3,128,1024]{2,1,0:T(8,128)(2,1)S(1)} %collective-permute-done.6.theirs_ref.theirs, bf16[2,3,128,512]{3,2,1,0:T(8,128)(2,1)S(1)} %collective-permute-done.7.swap, ...), custom_call_target="tpu_custom_call" | custom-call | flops 872415232 | bytes 3670016 | tf_op jit(solution)/shard_map/attend/pallas_call | solution.py:548
  73.3 1.9 %attend_mid.1 = (bf16[128,512]{1,0:T(8,128)(2,1)S(1)}, bf16[128,512]{1,0:T(8,128)(2,1)S(1)}, bf16[128,512]{1,0:T(8,128)(2,1)S(1)}, bf16[128,512]{1,0:T(8,128)(2,...) custom-call(s32[4]{0:T(128)S(1)} %copy-done.5, ...), custom_call_target="tpu_custom_call" | custom-call | flops 201326592 | bytes 3145728 | tf_op jit(solution)/shard_map/attend_mid/pallas_call | solution.py:627
  75.2 3.3 %collective-permute-start.12 = (bf16[128,512]{1,0:T(8,128)(2,1)S(1)}, bf16[128,512]{1,0:T(8,128)(2,1)S(1)}, u32[]{:S(2)}, u32[]{:S(2)}) collective-permute-start(bf16[128,512]{1,0:T(8,128)(2,1)S(1)} %get-tuple-element.55), channel_id=1, source_target_pairs={{0,1},{1,0},{2,3},{3,2},{4,5},{5,4},{6,7},{7,6},{8,9},{9,8},{10,11... | collective-permute-start | bytes 393224 | tf_op jit(solution)/shard_map/ppermute | solution.py:24
  78.5 0.1 collective-permute-start.5
  78.7 2.0 %collective-permute-start.14 = (bf16[128,512]{1,0:T(8,128)(2,1)S(1)}, bf16[128,512]{1,0:T(8,128)(2,1)S(1)}, u32[]{:S(2)}, u32[]{:S(2)}) collective-permute-start(bf16[128,512]{1,0:T(8,128)(2,1)S(1)} %get-tuple-element.57), channel_id=1, source_target_pairs={{0,3},{1,2},{2,1},{3,0},{4,7},{5,6},{6,5},{7,4},{8,11},{9,10},{10,... | collective-permute-start | bytes 393224 | tf_op jit(solution)/shard_map/ppermute | solution.py:24
  80.7 1.0 %attend_last.1.refs_4_ = bf16[128,512]{1,0:T(8,128)(2,1)S(1)} custom-call(s32[4]{0:T(128)S(1)} %copy-done.5, bf16[1,2,128,512]{3,2,1,0:T(8,128)(2,1)S(1)} %collective-permute-done.15.own_s, bf16[1,2,128,512]{3,2,1,0:T(8,128)(2,1)S(1)} %collective-permute-done.16.cross_s, f32[256,512]{1,0:T(8,128)S(1)} %get-tuple-element.58.acc_ref, ...), custom_call_target="tpu_custom_call" | custom-call | flops 33554432 | bytes 1048576 | tf_op jit(solution)/shard_map/attend_last/pallas_call | solution.py:673
  81.8 0.7 collective-permute-start.19
  82.5 0.7 collective-permute-start.18
  83.1 3.0 %collective-permute-start.17 = (bf16[128,512]{1,0:T(8,128)(2,1)S(1)}, bf16[128,512]{1,0:T(8,128)(2,1)S(1)}, u32[]{:S(2)}, u32[]{:S(2)}) collective-permute-start(bf16[128,512]{1,0:T(8,128)(2,1)S(1)} %attend_last.1.refs_4_), channel_id=1, source_target_pairs={{1,0},{5,4},{9,8},{13,12},{17,16},{21,20},{25,24},{29,28}} | collective-permute-start | bytes 393224 | tf_op jit(solution)/shard_map/ppermute | solution.py:719
  86.1 5.1 %hyena_near.1 = (f32[128,2048]{1,0:T(8,128)S(1)}, f32[128,2048]{1,0:T(8,128)S(1)}, bf16[128,2048]{1,0:T(8,128)(2,1)S(1)}, bf16[128,2048]{1,0:T(8,128)(2,1)S(1)}) custom-call(bf16[3,128,2048]{2,1,0:T(8,128)(2,1)S(1)} %bitcast.11, bf16[3,8,2048]{2,1,0:T(8,128)(2,1)S(1)} %collective-permute-done.halo_ref, f32[3,3,2048]{2,1,0:T(4,128)S(1)} %copy-done.2, ...), custom_call_target="tpu_custom_call" | custom-call | flops 536870912 | bytes 3145728 | tf_op jit(solution)/shard_map/hyena_near/pallas_call | solution.py:224
  91.2 2.4 %hyena_finish.1 = bf16[128,2048]{1,0:T(8,128)(2,1)} custom-call(f32[128,2048]{1,0:T(8,128)S(1)} %get-tuple-element.34.near_ref, f32[128,2048]{1,0:T(8,128)S(1)} %get-tuple-element.35.q_ref, bf16[128,2048]{1,0:T(8,128)(2,1)S(1)} %get-tuple-element.36.high_ref, bf16[128,2048]{1,0:T(8,128)(2,1)S(1)} %get-tuple-element.37.low_ref, ...), custom_call_target="tpu_custom_call" | custom-call | flops 201326592 | bytes 2621440 | tf_op jit(solution)/shard_map/hyena_finish/pallas_call | solution.py:276
  93.7 0.8 assemble.1
  (36 shorter events, 0.6 us)
Async XLA Ops:
  0.6 3.7 %copy-start = (bf16[128,3,2048]{2,0,1:T(8,128)(2,1)S(1)}, bf16[128,3,2048]{2,0,1:T(8,128)(2,1)}, u32[]{:S(2)}) copy-start(bf16[128,3,2048]{2,0,1:T(8,128)(2,1)} %param.10) | copy-start | bytes 4718596
  1.9 2.4 %collective-permute-start.6 = (bf16[3,128,1024]{2,1,0:T(8,128)(2,1)S(1)}, bf16[3,128,1024]{2,1,0:T(8,128)(2,1)S(1)}, u32[]{:S(2)}, u32[]{:S(2)}) collective-permute-start(bf16[3,128,1024]{2,1,0:T(8,128)(2,1)S(1)} %get-tuple-element.48), channel_id=1, source_target_pairs={{0,1},{1,0},{2,3},{3,2},{4,5},{5,4},{6,7},{7,6},{8,9},{9,8},{10,11... | collective-permute-start | bytes 2359304 | tf_op jit(solution)/shard_map/ppermute | solution.py:24
  4.4 16.2 %collective-permute-start.8 = (bf16[2,2,128,512]{3,2,1,0:T(8,128)(2,1)S(1)}, bf16[2,2,128,512]{3,2,1,0:T(8,128)(2,1)S(1)}, u32[]{:S(2)}, u32[]{:S(2)}) collective-permute-start(bf16[2,2,128,512]{3,2,1,0:T(8,128)(2,1)S(1)} %get-tuple-element.49), channel_id=1, source_target_pairs={{0,6},{1,7},{2,4},{3,5},{4,10},{5,11},{6,8},{7,9},{8,14},{9,15},{1... | collective-permute-start | bytes 1572872 | tf_op jit(solution)/shard_map/ppermute | solution.py:38
  9.7 27.7 %copy-start.1 = (bf16[128,3,2048]{2,0,1:T(8,128)(2,1)S(1)}, bf16[128,3,2048]{2,0,1:T(8,128)(2,1)}, u32[]{:S(2)}) copy-start(bf16[128,3,2048]{2,0,1:T(8,128)(2,1)} %param.6) | copy-start | bytes 4718596
  9.7 27.7 %copy-start.2 = (f32[3,3,2048]{2,1,0:T(4,128)S(1)}, f32[3,3,2048]{2,1,0:T(4,128)}, u32[]{:S(2)}) copy-start(f32[3,3,2048]{2,1,0:T(4,128)} %w_ref.3) | copy-start | bytes 221188
  9.7 27.7 %copy-start.3 = (f32[128,16]{0,1:T(8,128)S(1)}, f32[128,16]{0,1:T(8,128)}, u32[]{:S(2)}) copy-start(f32[128,16]{0,1:T(8,128)} %param.8) | copy-start | bytes 24580
  9.7 27.7 %copy-start.4 = (f32[128,16]{0,1:T(8,128)S(1)}, f32[128,16]{0,1:T(8,128)}, u32[]{:S(2)}) copy-start(f32[128,16]{0,1:T(8,128)} %param.9) | copy-start | bytes 24580
  9.7 22.1 %collective-permute-start.10 = (bf16[2,2,128,512]{3,2,1,0:T(8,128)(2,1)S(1)}, bf16[2,2,128,512]{3,2,1,0:T(8,128)(2,1)S(1)}, u32[]{:S(2)}, u32[]{:S(2)}) collective-permute-start(bf16[2,2,128,512]{3,2,1,0:T(8,128)(2,1)S(1)} %get-tuple-element.50), channel_id=1, source_target_pairs={{0,4},{1,5},{2,6},{3,7},{4,8},{5,9},{6,10},{7,11},{8,12},{9,13},{1... | collective-permute-start | bytes 1572872 | tf_op jit(solution)/shard_map/ppermute | solution.py:38
  13.1 46.5 %collective-permute-start.7 = (bf16[2,3,128,512]{3,2,1,0:T(8,128)(2,1)S(1)}, bf16[2,3,128,512]{3,2,1,0:T(8,128)(2,1)S(1)}, u32[]{:S(2)}, u32[]{:S(2)}) collective-permute-start(bf16[2,3,128,512]{3,2,1,0:T(8,128)(2,1)S(1)} %pack.2), channel_id=1, source_target_pairs={{0,2},{1,3},{2,0},{3,1},{4,6},{5,7},{6,4},{7,5},{8,10},{9,11},{10,... | collective-permute-start | bytes 2359304 | tf_op jit(solution)/shard_map/ppermute | solution.py:24
  20.6 52.7 %collective-permute-start.9 = (bf16[2,2,128,512]{3,2,1,0:T(8,128)(2,1)S(1)}, bf16[2,2,128,512]{3,2,1,0:T(8,128)(2,1)S(1)}, u32[]{:S(2)}, u32[]{:S(2)}) collective-permute-start(bf16[2,2,128,512]{3,2,1,0:T(8,128)(2,1)S(1)} %collective-permute-done.8.cross.pairs), channel_id=1, source_target_pairs={{4,8},{5,9},{8,12},{9,13},{20,24},{21,25},{24,28},{25,29}} | collective-permute-start | bytes 1572872 | tf_op jit(solution)/shard_map/ppermute | solution.py:38
  31.8 41.4 %collective-permute-start.11 = (bf16[2,2,128,512]{3,2,1,0:T(8,128)(2,1)S(1)}, bf16[2,2,128,512]{3,2,1,0:T(8,128)(2,1)S(1)}, u32[]{:S(2)}, u32[]{:S(2)}) collective-permute-start(bf16[2,2,128,512]{3,2,1,0:T(8,128)(2,1)S(1)} %collective-permute-done.10.own.pairs), channel_id=1, source_target_pairs={{6,10},{7,11},{10,14},{11,15},{22,26},{23,27},{26,30},{27,31}} | collective-permute-start | bytes 1572872 | tf_op jit(solution)/shard_map/ppermute | solution.py:38
  32.5 4.9 %collective-permute-start = (bf16[3,8,2048]{2,1,0:T(8,128)(2,1)S(1)}, bf16[3,8,2048]{2,1,0:T(8,128)(2,1)S(1)}, u32[]{:S(2)}, u32[]{:S(2)}) collective-permute-start(bf16[3,8,2048]{2,1,0:T(8,128)(2,1)S(1)} %get-tuple-element.32), channel_id=1, source_target_pairs={{0,1},{1,2},{2,3},{3,4},{4,5},{5,6},{6,7},{7,8},{8,9},{9,10},{10,1... | collective-permute-start | bytes 294920 | tf_op jit(solution)/shard_map/ppermute | solution.py:38
  37.4 31.0 %copy-start.5 = (s32[4]{0:T(128)S(1)}, s32[4]{0:T(128)}, u32[]{:S(2)}) copy-start(s32[4]{0:T(128)} %docs_ref.5) | copy-start | bytes 52
  39.7 1.3 %collective-permute-start.1 = (f32[16,1024]{1,0:T(8,128)S(1)}, f32[16,1024]{1,0:T(8,128)S(1)}, u32[]{:S(2)}, u32[]{:S(2)}) collective-permute-start(f32[16,1024]{1,0:T(8,128)S(1)} %get-tuple-element.39), channel_id=1, source_target_pairs={{0,1},{1,0},{2,3},{3,2},{4,5},{5,4},{6,7},{7,6},{8,9},{9,8},{10,11... | collective-permute-start | bytes 196616 | tf_op jit(solution)/shard_map/ppermute | solution.py:24
  41.1 5.5 %collective-permute-start.2 = (f32[16,1024]{1,0:T(8,128)S(1)}, f32[16,1024]{1,0:T(8,128)S(1)}, u32[]{:S(2)}, u32[]{:S(2)}) collective-permute-start(f32[16,1024]{1,0:T(8,128)S(1)} %get-tuple-element.41.refs_0_), channel_id=1, source_target_pairs={{0,2},{1,3},{2,0},{3,1},{4,6},{5,7},{6,4},{7,5},{8,10},{9,11},{10,... | collective-permute-start | bytes 196616 | tf_op jit(solution)/shard_map/ppermute | solution.py:24
  46.6 12.3 %collective-permute-start.3 = (f32[16,1024]{1,0:T(8,128)S(1)}, f32[16,1024]{1,0:T(8,128)S(1)}, u32[]{:S(2)}, u32[]{:S(2)}) collective-permute-start(f32[16,1024]{1,0:T(8,128)S(1)} %get-tuple-element.42.refs_0_), channel_id=1, source_target_pairs={{0,4},{1,5},{2,6},{3,7},{4,8},{5,9},{6,10},{7,11},{8,12},{9,13},{1... | collective-permute-start | bytes 196616 | tf_op jit(solution)/shard_map/ppermute | solution.py:38
  57.6 21.0 %collective-permute-start.16 = (bf16[1,2,128,512]{3,2,1,0:T(8,128)(2,1)S(1)}, bf16[1,2,128,512]{3,2,1,0:T(8,128)(2,1)S(1)}, u32[]{:S(2)}, u32[]{:S(2)}) collective-permute-start(bf16[1,2,128,512]{3,2,1,0:T(8,128)(2,1)S(1)} %odd.3), channel_id=1, source_target_pairs={{6,10},{7,11},{10,14},{11,15},{22,26},{23,27},{26,30},{27,31}} | collective-permute-start | bytes 786440 | tf_op jit(solution)/shard_map/ppermute | solution.py:38
  58.9 21.8 %collective-permute-start.15 = (bf16[1,2,128,512]{3,2,1,0:T(8,128)(2,1)S(1)}, bf16[1,2,128,512]{3,2,1,0:T(8,128)(2,1)S(1)}, u32[]{:S(2)}, u32[]{:S(2)}) collective-permute-start(bf16[1,2,128,512]{3,2,1,0:T(8,128)(2,1)S(1)} %odd.2), channel_id=1, source_target_pairs={{4,8},{5,9},{8,12},{9,13},{20,24},{21,25},{24,28},{25,29}} | collective-permute-start | bytes 786440 | tf_op jit(solution)/shard_map/ppermute | solution.py:38
  59.6 18.8 %collective-permute-start.4 = (f32[16,1024]{1,0:T(8,128)S(1)}, f32[16,1024]{1,0:T(8,128)S(1)}, u32[]{:S(2)}, u32[]{:S(2)}) collective-permute-start(f32[16,1024]{1,0:T(8,128)S(1)} %shard_map.79), channel_id=1, source_target_pairs={{0,8},{1,9},{2,10},{3,11},{4,12},{5,13},{6,14},{7,15},{16,24},{17,... | collective-permute-start | bytes 196616 | tf_op jit(solution)/shard_map/ppermute | solution.py:38
  75.2 7.9 %collective-permute-start.12 = (bf16[128,512]{1,0:T(8,128)(2,1)S(1)}, bf16[128,512]{1,0:T(8,128)(2,1)S(1)}, u32[]{:S(2)}, u32[]{:S(2)}) collective-permute-start(bf16[128,512]{1,0:T(8,128)(2,1)S(1)} %get-tuple-element.55), channel_id=1, source_target_pairs={{0,1},{1,0},{2,3},{3,2},{4,5},{5,4},{6,7},{7,6},{8,9},{9,8},{10,11... | collective-permute-start | bytes 393224 | tf_op jit(solution)/shard_map/ppermute | solution.py:24
  78.5 3.9 %collective-permute-start.5 = (f32[16,1024]{1,0:T(8,128)S(1)}, f32[16,1024]{1,0:T(8,128)S(1)}, u32[]{:S(2)}, u32[]{:S(2)}) collective-permute-start(f32[16,1024]{1,0:T(8,128)S(1)} %get-tuple-element.47), channel_id=1, source_target_pairs={{0,1},{1,0},{2,3},{3,2},{4,5},{5,4},{6,7},{7,6},{8,9},{9,8},{10,11... | collective-permute-start | bytes 196616 | tf_op jit(solution)/shard_map/ppermute | solution.py:24
  78.6 15.0 %collective-permute-start.13 = (bf16[128,512]{1,0:T(8,128)(2,1)S(1)}, bf16[128,512]{1,0:T(8,128)(2,1)S(1)}, u32[]{:S(2)}, u32[]{:S(2)}) collective-permute-start(bf16[128,512]{1,0:T(8,128)(2,1)S(1)} %get-tuple-element.56), channel_id=1, source_target_pairs={{0,2},{1,3},{2,0},{3,1},{4,6},{5,7},{6,4},{7,5},{8,10},{9,11},{10,... | collective-permute-start | bytes 393224 | tf_op jit(solution)/shard_map/ppermute | solution.py:24
  78.7 14.9 %collective-permute-start.14 = (bf16[128,512]{1,0:T(8,128)(2,1)S(1)}, bf16[128,512]{1,0:T(8,128)(2,1)S(1)}, u32[]{:S(2)}, u32[]{:S(2)}) collective-permute-start(bf16[128,512]{1,0:T(8,128)(2,1)S(1)} %get-tuple-element.57), channel_id=1, source_target_pairs={{0,3},{1,2},{2,1},{3,0},{4,7},{5,6},{6,5},{7,4},{8,11},{9,10},{10,... | collective-permute-start | bytes 393224 | tf_op jit(solution)/shard_map/ppermute | solution.py:24
  81.8 11.9 %collective-permute-start.19 = (bf16[128,512]{1,0:T(8,128)(2,1)S(1)}, bf16[128,512]{1,0:T(8,128)(2,1)S(1)}, u32[]{:S(2)}, u32[]{:S(2)}) collective-permute-start(bf16[128,512]{1,0:T(8,128)(2,1)S(1)} %attend_last.1.refs_4_), channel_id=1, source_target_pairs={{3,0},{7,4},{11,8},{15,12},{19,16},{23,20},{27,24},{31,28}} | collective-permute-start | bytes 393224 | tf_op jit(solution)/shard_map/ppermute | solution.py:719
  82.5 11.2 %collective-permute-start.18 = (bf16[128,512]{1,0:T(8,128)(2,1)S(1)}, bf16[128,512]{1,0:T(8,128)(2,1)S(1)}, u32[]{:S(2)}, u32[]{:S(2)}) collective-permute-start(bf16[128,512]{1,0:T(8,128)(2,1)S(1)} %attend_last.1.refs_4_), channel_id=1, source_target_pairs={{2,0},{6,4},{10,8},{14,12},{18,16},{22,20},{26,24},{30,28}} | collective-permute-start | bytes 393224 | tf_op jit(solution)/shard_map/ppermute | solution.py:719
  83.1 10.5 %collective-permute-start.17 = (bf16[128,512]{1,0:T(8,128)(2,1)S(1)}, bf16[128,512]{1,0:T(8,128)(2,1)S(1)}, u32[]{:S(2)}, u32[]{:S(2)}) collective-permute-start(bf16[128,512]{1,0:T(8,128)(2,1)S(1)} %attend_last.1.refs_4_), channel_id=1, source_target_pairs={{1,0},{5,4},{9,8},{13,12},{17,16},{21,20},{25,24},{29,28}} | collective-permute-start | bytes 393224 | tf_op jit(solution)/shard_map/ppermute | solution.py:719

commit v2 on v0

--- a/solution.py
+++ b/solution.py
@@ -11,7 +11,6 @@
 
 HEAD = 128
 LANES = 128
-TURNS = 1
 EDGE = 8
 ROW = 4
 
@@ -565,15 +564,18 @@
     )(doc_lengths, streams, theirs, swap, own, cross)
 
 
-def attend_last_body(heads, docs_ref, streams, theirs, swap, *refs):
+def attend_last_body(pair, docs_ref, streams, theirs, swap, *refs):
     cross_l, own_s, own_l, cross_s, acc_ref, m_ref, l_ref = refs[:7]
     outs = refs[7:]
     _, side, place, row = spot()
     rows, quarter = acc_ref.shape[0] // ROW, acc_ref.shape[1]
     base = row * (ROW * rows)
+    heads = range(quarter // HEAD)
 
     def run(early, late, large, small):
         for asking, blocks in ((early, ((small, 0), (large, 1), (large, 0))), (late, ((large, 0),))):
+            if asking != pair:
+                continue
             width = len(blocks) * rows
             here = slice(asking[0] * rows, (asking[1] + 1) * rows)
             token = base - (ROW + len(blocks)) * rows + lax.broadcasted_iota(jnp.int32, (rows, width), 1)
@@ -589,7 +591,7 @@
                     jnp.concatenate(
                         [row_part(streams, theirs, swap, slot, 0, head, quarter) for slot in asking], axis=0
                     ),
-                    stack(0, lanes_of[head - heads[0]]),
+                    stack(0, lanes_of[head]),
                     (((1,), (1,)), ((), ())),
                     preferred_element_type=F32,
                 )
@@ -609,9 +611,8 @@
                 share = 1.0 / (l_ref[here, lanes] * fade + jnp.sum(weight, axis=1, keepdims=True))
                 more = jnp.dot(weight.astype(BF16), stack(1, lanes), preferred_element_type=F32)
                 made = ((acc_ref[here, lanes] * fade + more) * share).astype(BF16)
-                put = slice(lanes.start - heads[0] * HEAD, lanes.stop - heads[0] * HEAD)
-                for n, slot in enumerate(asking):
-                    outs[slot][:, put] = made[n * rows : (n + 1) * rows]
+                for n, out in enumerate(outs):
+                    out[:, lanes] = made[n * rows : (n + 1) * rows]
 
     @pl.when(side == 0)
     def _():
@@ -622,16 +623,15 @@
         run((2, 3), (0, 1), own_l, cross_s)
 
 
-def attend_last(heads, doc_lengths, streams, theirs, swap, olds, acc, top, below):
-    rows = acc.shape[0] // ROW
-    lanes = len(heads) * HEAD
-    return pl.pallas_call(
-        functools.partial(attend_last_body, heads),
+def attend_last(pair, doc_lengths, streams, theirs, swap, olds, acc, top, below):
+    rows, quarter = acc.shape[0] // ROW, acc.shape[1]
+    return pl.pallas_call(
+        functools.partial(attend_last_body, pair),
         in_specs=[SMEM] + [VMEM] * 10,
-        out_specs=[VMEM] * ROW,
-        out_shape=[jax.ShapeDtypeStruct((rows, lanes), BF16)] * ROW,
+        out_specs=[VMEM] * 2,
+        out_shape=[jax.ShapeDtypeStruct((rows, quarter), BF16)] * 2,
         compiler_params=limits(16),
-        cost_estimate=cost(32 * rows * rows * lanes, 48 * rows * lanes, 8 * len(heads) * rows * rows),
+        cost_estimate=cost(16 * rows * rows * quarter, 24 * rows * quarter, 16 * rows * rows),
         name="attend_last",
     )(doc_lengths, streams, theirs, swap, *olds, acc, top, below)
 
@@ -687,14 +687,13 @@
     hyena_out = hyena_finish(near, query, high, low, keep, back)
 
     acc, top, below = attend(doc_lengths, streams, theirs, swap, own, cross)
-    pieces = []
-    heads = acc.shape[1] // HEAD
-    for turn in range(TURNS):
-        these = range(turn * heads // TURNS, (turn + 1) * heads // TURNS)
-        made = attend_last(these, doc_lengths, streams, theirs, swap, olds, acc, top, below)
-        pieces.append(made[0])
-        pieces += [flip(made[n], "ctx", n) for n in range(1, ROW)]
-    attn_out = assemble(pieces)
+    last = lambda pair: attend_last(pair, doc_lengths, streams, theirs, swap, olds, acc, top, below)
+    far2, far3 = last((2, 3))
+    far2 = flip(far2, "ctx", 2)
+    far3 = flip(far3, "ctx", 3)
+    kept, near1 = last((0, 1))
+    near1 = flip(near1, "ctx", 1)
+    attn_out = assemble([kept, near1, far2, far3])
     return (hyena_out, attn_out)
 
 

time: 81.5 us -> 82.8 us (1.016)
    pallas_call x1 -> x2, Pallas kernels: 2.11 us -> 2.79 us  [attend_last(): pl.pallas_call(functools.partial(attend_last_body, pair), in_specs=[SMEM]...]
where the time goes in v2:
time: 82.8 us; the launch traced here: 82.5 us
  starting transfers between devices  39.4 us (48%)
  waiting for transfers between devices  22.2 us (27%)
  Pallas kernels  19.9 us (24%)
  between operations  0.96 us (1%)
    ppermute x9, starting transfers between devices, ahead(): return lax.ppermute(value, axis, pairs)  31.8 us
    ppermute x9, waiting for transfers between devices, ahead(): return lax.ppermute(value, axis, pairs)  16.6 us
    ppermute x8, starting transfers between devices, flip(): return lax.ppermute(value, axis, [(at, at ^ bit) for at in range(count)])  7.58 us
    ppermute x8, waiting for transfers between devices, flip(): return lax.ppermute(value, axis, [(at, at ^ bit) for at in range(count)])  5.58 us
    pallas_call x1, Pallas kernels, hyena_near(): pl.pallas_call(functools.partial(hyena_near_body, filters), grid=(STEPS,)...  5.05 us
    pallas_call x1, Pallas kernels, attend(): pl.pallas_call(attend_body, in_specs=[SMEM] + [VMEM] * 5, out_specs=[VMEM...  4.86 us
    pallas_call x2, Pallas kernels, attend_last(): pl.pallas_call(functools.partial(attend_last_body, pair), in_specs=[SMEM]...  2.79 us
    pallas_call x1, Pallas kernels, hyena_finish(): pl.pallas_call(functools.partial(hyena_out_body, modes), grid=(STEPS,), i...  2.43 us
  transfers between devices with their start and end apart: 17, of which 6 were waited for; matrix products, arithmetic and copies ran while one was open for 0% of the time, Pallas kernels for 21%

profile of v2, /device:TPU:0, one launch (start us, length us, event | category | flops | bytes accessed | tf_op | source)
XLA Modules:
  0.0 82.5 jit_solution(9470193733990605622)
XLA Ops:
  0.6 1.3 %front.1 = (bf16[3,128,1024]{2,1,0:T(8,128)(2,1)S(1)}, bf16[3,8,2048]{2,1,0:T(8,128)(2,1)S(1)}) custom-call(bf16[3,128,2048]{2,1,0:T(8,128)(2,1)} %bitcast.4, bf16[3,128,2048]{2,1,0:T(8,128)(2,1)} %bitcast.10), custom_call_target="tpu_custom_call" | custom-call | bytes 1572864 | tf_op jit(solution)/shard_map/front/pallas_call | solution.py:383
  1.9 0.6 collective-permute-start.6
  2.5 1.9 %collective-permute-done.6.theirs_ref.theirs = bf16[3,128,1024]{2,1,0:T(8,128)(2,1)S(1)} collective-permute-done((bf16[3,128,1024]{2,1,0:T(8,128)(2,1)S(1)}, bf16[3,128,1024]{2,1,0:T(8,128)(2,1)S(1)}, u32[]{:S(2)}, u32[]{:S(2)}) %collective-permute-start.6) | collective-permute-done | bytes 786464 | tf_op jit(solution)/shard_map/ppermute | solution.py:24
  4.4 0.1 pack.3
  4.5 4.9 %collective-permute-start.10 = (bf16[2,2,128,512]{3,2,1,0:T(8,128)(2,1)S(1)}, bf16[2,2,128,512]{3,2,1,0:T(8,128)(2,1)S(1)}, u32[]{:S(2)}, u32[]{:S(2)}) collective-permute-start(bf16[2,2,128,512]{3,2,1,0:T(8,128)(2,1)S(1)} %get-tuple-element.46), channel_id=1, source_target_pairs={{0,4},{1,5},{2,6},{3,7},{4,8},{5,9},{6,10},{7,11},{8,12},{9,13},{1... | collective-permute-start | bytes 1572872 | tf_op jit(solution)/shard_map/ppermute | solution.py:38
  9.4 4.6 %collective-permute-start.8 = (bf16[2,2,128,512]{3,2,1,0:T(8,128)(2,1)S(1)}, bf16[2,2,128,512]{3,2,1,0:T(8,128)(2,1)S(1)}, u32[]{:S(2)}, u32[]{:S(2)}) collective-permute-start(bf16[2,2,128,512]{3,2,1,0:T(8,128)(2,1)S(1)} %get-tuple-element.45), channel_id=1, source_target_pairs={{0,6},{1,7},{2,4},{3,5},{4,10},{5,11},{6,8},{7,9},{8,14},{9,15},{1... | collective-permute-start | bytes 1572872 | tf_op jit(solution)/shard_map/ppermute | solution.py:38
  14.0 0.1 pack.2
  14.1 0.6 collective-permute-start.7
  14.6 1.3 %collective-permute-start = (bf16[3,8,2048]{2,1,0:T(8,128)(2,1)S(1)}, bf16[3,8,2048]{2,1,0:T(8,128)(2,1)S(1)}, u32[]{:S(2)}, u32[]{:S(2)}) collective-permute-start(bf16[3,8,2048]{2,1,0:T(8,128)(2,1)S(1)} %get-tuple-element.28), channel_id=1, source_target_pairs={{0,1},{1,2},{2,3},{3,4},{4,5},{5,6},{6,7},{7,8},{8,9},{9,10},{10,1... | collective-permute-start | bytes 294920 | tf_op jit(solution)/shard_map/ppermute | solution.py:38
  15.9 5.7 %collective-permute-done.10.pairs.own = bf16[2,2,128,512]{3,2,1,0:T(8,128)(2,1)S(1)} collective-permute-done((bf16[2,2,128,512]{3,2,1,0:T(8,128)(2,1)S(1)}, bf16[2,2,128,512]{3,2,1,0:T(8,128)(2,1)S(1)}, u32[]{:S(2)}, u32[]{:S(2)}) %collective-permute-start.10) | collective-permute-done | bytes 524320 | tf_op jit(solution)/shard_map/ppermute | solution.py:38
  21.6 0.7 collective-permute-start.12
  22.3 9.8 %collective-permute-done.8.pairs.cross = bf16[2,2,128,512]{3,2,1,0:T(8,128)(2,1)S(1)} collective-permute-done((bf16[2,2,128,512]{3,2,1,0:T(8,128)(2,1)S(1)}, bf16[2,2,128,512]{3,2,1,0:T(8,128)(2,1)S(1)}, u32[]{:S(2)}, u32[]{:S(2)}) %collective-permute-start.8) | collective-permute-done | bytes 524320 | tf_op jit(solution)/shard_map/ppermute | solution.py:38
  32.1 0.7 collective-permute-start.9
  32.8 2.3 %hyena_ends.1 = (bf16[128,2048]{1,0:T(8,128)(2,1)S(1)}, f32[16,1024]{1,0:T(8,128)S(1)}, f32[16,1024]{1,0:T(8,128)S(1)}, f32[16,1024]{1,0:T(8,128)S(1)}, f32[16,1024]{1,0:T(8,128)S(1)}) custom-call(bf16[3,128,2048]{2,1,0:T(8,128)(2,1)S(1)} %bitcast.11, bf16[3,8,2048]{2,1,0:T(8,128)(2,1)S(1)} %collective-permute-done.halo_ref, f32[3,3,2048]{2,1,0:T(4,128)S(1)} %copy-done.2, ...), custom_call_target="tpu_custom_call" | custom-call | flops 134217728 | bytes 2097152 | tf_op jit(solution)/shard_map/hyena_ends/pallas_call | solution.py:155
  35.2 0.1 collective-permute-start.1
  35.2 1.2 %collective-permute-done.1.refs_1_ = f32[16,1024]{1,0:T(8,128)S(1)} collective-permute-done((f32[16,1024]{1,0:T(8,128)S(1)}, f32[16,1024]{1,0:T(8,128)S(1)}, u32[]{:S(2)}, u32[]{:S(2)}) %collective-permute-start.1) | collective-permute-done | bytes 65568 | tf_op jit(solution)/shard_map/ppermute | solution.py:24
  36.5 2.4 %collective-permute-start.2 = (f32[16,1024]{1,0:T(8,128)S(1)}, f32[16,1024]{1,0:T(8,128)S(1)}, u32[]{:S(2)}, u32[]{:S(2)}) collective-permute-start(f32[16,1024]{1,0:T(8,128)S(1)} %get-tuple-element.37.refs_0_), channel_id=1, source_target_pairs={{0,2},{1,3},{2,0},{3,1},{4,6},{5,7},{6,4},{7,5},{8,10},{9,11},{10,... | collective-permute-start | bytes 196616 | tf_op jit(solution)/shard_map/ppermute | solution.py:24
  38.9 2.4 %collective-permute-done.2.refs_1_ = f32[16,1024]{1,0:T(8,128)S(1)} collective-permute-done((f32[16,1024]{1,0:T(8,128)S(1)}, f32[16,1024]{1,0:T(8,128)S(1)}, u32[]{:S(2)}, u32[]{:S(2)}) %collective-permute-start.2) | collective-permute-done | bytes 65568 | tf_op jit(solution)/shard_map/ppermute | solution.py:24
  41.4 13.9 %collective-permute-start.3 = (f32[16,1024]{1,0:T(8,128)S(1)}, f32[16,1024]{1,0:T(8,128)S(1)}, u32[]{:S(2)}, u32[]{:S(2)}) collective-permute-start(f32[16,1024]{1,0:T(8,128)S(1)} %get-tuple-element.38.refs_0_), channel_id=1, source_target_pairs={{0,4},{1,5},{2,6},{3,7},{4,8},{5,9},{6,10},{7,11},{8,12},{9,13},{1... | collective-permute-start | bytes 196616 | tf_op jit(solution)/shard_map/ppermute | solution.py:38
  55.3 0.7 collective-permute-start.11
  56.0 1.1 %collective-permute-done.3.refs_1_.refs_0_ = f32[16,1024]{1,0:T(8,128)S(1)} collective-permute-done((f32[16,1024]{1,0:T(8,128)S(1)}, f32[16,1024]{1,0:T(8,128)S(1)}, u32[]{:S(2)}, u32[]{:S(2)}) %collective-permute-start.3) | collective-permute-done | bytes 65568 | tf_op jit(solution)/shard_map/ppermute | solution.py:38
  57.2 0.7 collective-permute-start.13
  57.9 4.5 %collective-permute-start.4 = (f32[16,1024]{1,0:T(8,128)S(1)}, f32[16,1024]{1,0:T(8,128)S(1)}, u32[]{:S(2)}, u32[]{:S(2)}) collective-permute-start(f32[16,1024]{1,0:T(8,128)S(1)} %shard_map.79), channel_id=1, source_target_pairs={{0,8},{1,9},{2,10},{3,11},{4,12},{5,13},{6,14},{7,15},{16,24},{17,... | collective-permute-start | bytes 196616 | tf_op jit(solution)/shard_map/ppermute | solution.py:38
  62.4 4.9 %attend.1 = (f32[512,512]{1,0:T(8,128)S(1)}, f32[512,512]{1,0:T(8,128)S(1)}, f32[512,512]{1,0:T(8,128)S(1)}) custom-call(s32[4]{0:T(128)S(1)} %copy-done.5, bf16[3,128,2048]{2,1,0:T(8,128)(2,1)S(1)} %bitcast.7, bf16[3,128,1024]{2,1,0:T(8,128)(2,1)S(1)} %collective-permute-done.6.theirs_ref.theirs, bf16[2,3,128,512]{3,2,1,0:T(8,128)(2,1)S(1)} %collective-permute-done.7.swap, ...), custom_call_target="tpu_custom_call" | custom-call | flops 872415232 | bytes 3670016 | tf_op jit(solution)/shard_map/attend/pallas_call | solution.py:548
  67.3 1.1 %attend_last.3 = (bf16[128,512]{1,0:T(8,128)(2,1)S(1)}, bf16[128,512]{1,0:T(8,128)(2,1)S(1)}) custom-call(s32[4]{0:T(128)S(1)} %copy-done.5, bf16[3,128,2048]{2,1,0:T(8,128)(2,1)S(1)} %bitcast.8, bf16[3,128,1024]{2,1,0:T(8,128)(2,1)S(1)} %collective-permute-done.6.theirs_ref.theirs, bf16[2,3,128,512]{3,2,1,0:T(8,128)(2,1)S(1)} %collective-permute-done.7.swap, ...), custom_call_target="tpu_custom_call" | custom-call | flops 134217728 | bytes 1572864 | tf_op jit(solution)/shard_map/attend_last/pallas_call | solution.py:628
  68.4 3.3 %collective-permute-start.15 = (bf16[128,512]{1,0:T(8,128)(2,1)S(1)}, bf16[128,512]{1,0:T(8,128)(2,1)S(1)}, u32[]{:S(2)}, u32[]{:S(2)}) collective-permute-start(bf16[128,512]{1,0:T(8,128)(2,1)S(1)} %get-tuple-element.52), channel_id=1, source_target_pairs={{0,2},{1,3},{2,0},{3,1},{4,6},{5,7},{6,4},{7,5},{8,10},{9,11},{10,... | collective-permute-start | bytes 393224 | tf_op jit(solution)/shard_map/ppermute | solution.py:24
  71.8 1.6 %attend_last.2 = (bf16[128,512]{1,0:T(8,128)(2,1)S(1)}, bf16[128,512]{1,0:T(8,128)(2,1)S(1)}) custom-call(s32[4]{0:T(128)S(1)} %copy-done.5, bf16[3,128,2048]{2,1,0:T(8,128)(2,1)S(1)} %bitcast.9, bf16[3,128,1024]{2,1,0:T(8,128)(2,1)S(1)} %collective-permute-done.6.theirs_ref.theirs, bf16[2,3,128,512]{3,2,1,0:T(8,128)(2,1)S(1)} %collective-permute-done.7.swap, ...), custom_call_target="tpu_custom_call" | custom-call | flops 134217728 | bytes 1572864 | tf_op jit(solution)/shard_map/attend_last/pallas_call | solution.py:628
  73.4 0.3 collective-permute-start.14
  73.7 0.4 collective-permute-start.5
  74.1 5.1 %hyena_near.1 = (f32[128,2048]{1,0:T(8,128)S(1)}, f32[128,2048]{1,0:T(8,128)S(1)}, bf16[128,2048]{1,0:T(8,128)(2,1)S(1)}, bf16[128,2048]{1,0:T(8,128)(2,1)S(1)}) custom-call(bf16[3,128,2048]{2,1,0:T(8,128)(2,1)S(1)} %bitcast.12, bf16[3,8,2048]{2,1,0:T(8,128)(2,1)S(1)} %collective-permute-done.halo_ref, f32[3,3,2048]{2,1,0:T(4,128)S(1)} %copy-done.2, ...), custom_call_target="tpu_custom_call" | custom-call | flops 536870912 | bytes 3145728 | tf_op jit(solution)/shard_map/hyena_near/pallas_call | solution.py:224
  79.2 2.4 %hyena_finish.1 = bf16[128,2048]{1,0:T(8,128)(2,1)} custom-call(f32[128,2048]{1,0:T(8,128)S(1)} %get-tuple-element.30.near_ref, f32[128,2048]{1,0:T(8,128)S(1)} %get-tuple-element.31.q_ref, bf16[128,2048]{1,0:T(8,128)(2,1)S(1)} %get-tuple-element.32.high_ref, bf16[128,2048]{1,0:T(8,128)(2,1)S(1)} %get-tuple-element.33.low_ref, ...), custom_call_target="tpu_custom_call" | custom-call | flops 201326592 | bytes 2621440 | tf_op jit(solution)/shard_map/hyena_finish/pallas_call | solution.py:276
  81.6 0.8 %assemble.1 = bf16[128,2048]{1,0:T(8,128)(2,1)} custom-call(bf16[128,512]{1,0:T(8,128)(2,1)S(1)} %get-tuple-element.50.refs_0_, bf16[128,512]{1,0:T(8,128)(2,1)S(1)} %collective-permute-done.14.refs_1_, bf16[128,512]{1,0:T(8,128)(2,1)S(1)} %collective-permute-done.15.refs_2_, bf16[128,512]{1,0:T(8,128)(2,1)S(1)} %collective-permute-done.16.refs_3_), custom_call_target="tpu_custom_call" | custom-call | bytes 1048576 | tf_op jit(solution)/shard_map/assemble/pallas_call | solution.py:652
  (30 shorter events, 0.3 us)
Async XLA Ops:
  0.6 3.8 %copy-start = (bf16[128,3,2048]{2,0,1:T(8,128)(2,1)S(1)}, bf16[128,3,2048]{2,0,1:T(8,128)(2,1)}, u32[]{:S(2)}) copy-start(bf16[128,3,2048]{2,0,1:T(8,128)(2,1)} %param.10) | copy-start | bytes 4718596
  1.9 2.5 %collective-permute-start.6 = (bf16[3,128,1024]{2,1,0:T(8,128)(2,1)S(1)}, bf16[3,128,1024]{2,1,0:T(8,128)(2,1)S(1)}, u32[]{:S(2)}, u32[]{:S(2)}) collective-permute-start(bf16[3,128,1024]{2,1,0:T(8,128)(2,1)S(1)} %get-tuple-element.44), channel_id=1, source_target_pairs={{0,1},{1,0},{2,3},{3,2},{4,5},{5,4},{6,7},{7,6},{8,9},{9,8},{10,11... | collective-permute-start | bytes 2359304 | tf_op jit(solution)/shard_map/ppermute | solution.py:24
  4.5 17.1 %collective-permute-start.10 = (bf16[2,2,128,512]{3,2,1,0:T(8,128)(2,1)S(1)}, bf16[2,2,128,512]{3,2,1,0:T(8,128)(2,1)S(1)}, u32[]{:S(2)}, u32[]{:S(2)}) collective-permute-start(bf16[2,2,128,512]{3,2,1,0:T(8,128)(2,1)S(1)} %get-tuple-element.46), channel_id=1, source_target_pairs={{0,4},{1,5},{2,6},{3,7},{4,8},{5,9},{6,10},{7,11},{8,12},{9,13},{1... | collective-permute-start | bytes 1572872 | tf_op jit(solution)/shard_map/ppermute | solution.py:38
  9.4 23.4 %copy-start.1 = (bf16[128,3,2048]{2,0,1:T(8,128)(2,1)S(1)}, bf16[128,3,2048]{2,0,1:T(8,128)(2,1)}, u32[]{:S(2)}) copy-start(bf16[128,3,2048]{2,0,1:T(8,128)(2,1)} %param.6) | copy-start | bytes 4718596
  9.4 23.4 %copy-start.2 = (f32[3,3,2048]{2,1,0:T(4,128)S(1)}, f32[3,3,2048]{2,1,0:T(4,128)}, u32[]{:S(2)}) copy-start(f32[3,3,2048]{2,1,0:T(4,128)} %w_ref.3) | copy-start | bytes 221188
  9.4 23.4 %copy-start.3 = (f32[128,16]{0,1:T(8,128)S(1)}, f32[128,16]{0,1:T(8,128)}, u32[]{:S(2)}) copy-start(f32[128,16]{0,1:T(8,128)} %param.8) | copy-start | bytes 24580
  9.4 23.4 %copy-start.4 = (f32[128,16]{0,1:T(8,128)S(1)}, f32[128,16]{0,1:T(8,128)}, u32[]{:S(2)}) copy-start(f32[128,16]{0,1:T(8,128)} %param.9) | copy-start | bytes 24580
  9.4 22.7 %collective-permute-start.8 = (bf16[2,2,128,512]{3,2,1,0:T(8,128)(2,1)S(1)}, bf16[2,2,128,512]{3,2,1,0:T(8,128)(2,1)S(1)}, u32[]{:S(2)}, u32[]{:S(2)}) collective-permute-start(bf16[2,2,128,512]{3,2,1,0:T(8,128)(2,1)S(1)} %get-tuple-element.45), channel_id=1, source_target_pairs={{0,6},{1,7},{2,4},{3,5},{4,10},{5,11},{6,8},{7,9},{8,14},{9,15},{1... | collective-permute-start | bytes 1572872 | tf_op jit(solution)/shard_map/ppermute | solution.py:38
  14.1 43.8 %collective-permute-start.7 = (bf16[2,3,128,512]{3,2,1,0:T(8,128)(2,1)S(1)}, bf16[2,3,128,512]{3,2,1,0:T(8,128)(2,1)S(1)}, u32[]{:S(2)}, u32[]{:S(2)}) collective-permute-start(bf16[2,3,128,512]{3,2,1,0:T(8,128)(2,1)S(1)} %pack.2), channel_id=1, source_target_pairs={{0,2},{1,3},{2,0},{3,1},{4,6},{5,7},{6,4},{7,5},{8,10},{9,11},{10,... | collective-permute-start | bytes 2359304 | tf_op jit(solution)/shard_map/ppermute | solution.py:24
  14.6 18.1 %collective-permute-start = (bf16[3,8,2048]{2,1,0:T(8,128)(2,1)S(1)}, bf16[3,8,2048]{2,1,0:T(8,128)(2,1)S(1)}, u32[]{:S(2)}, u32[]{:S(2)}) collective-permute-start(bf16[3,8,2048]{2,1,0:T(8,128)(2,1)S(1)} %get-tuple-element.28), channel_id=1, source_target_pairs={{0,1},{1,2},{2,3},{3,4},{4,5},{5,6},{6,7},{7,8},{8,9},{9,10},{10,1... | collective-permute-start | bytes 294920 | tf_op jit(solution)/shard_map/ppermute | solution.py:38
  21.6 45.6 %collective-permute-start.12 = (bf16[2,2,128,512]{3,2,1,0:T(8,128)(2,1)S(1)}, bf16[2,2,128,512]{3,2,1,0:T(8,128)(2,1)S(1)}, u32[]{:S(2)}, u32[]{:S(2)}) collective-permute-start(bf16[2,2,128,512]{3,2,1,0:T(8,128)(2,1)S(1)} %collective-permute-done.10.pairs.own), channel_id=1, source_target_pairs={{6,10},{7,11},{10,14},{11,15},{22,26},{23,27},{26,30},{27,31}} | collective-permute-start | bytes 1572872 | tf_op jit(solution)/shard_map/ppermute | solution.py:38
  32.1 35.2 %collective-permute-start.9 = (bf16[2,2,128,512]{3,2,1,0:T(8,128)(2,1)S(1)}, bf16[2,2,128,512]{3,2,1,0:T(8,128)(2,1)S(1)}, u32[]{:S(2)}, u32[]{:S(2)}) collective-permute-start(bf16[2,2,128,512]{3,2,1,0:T(8,128)(2,1)S(1)} %collective-permute-done.8.pairs.cross), channel_id=1, source_target_pairs={{4,8},{5,9},{8,12},{9,13},{20,24},{21,25},{24,28},{25,29}} | collective-permute-start | bytes 1572872 | tf_op jit(solution)/shard_map/ppermute | solution.py:38
  32.8 29.5 %copy-start.5 = (s32[4]{0:T(128)S(1)}, s32[4]{0:T(128)}, u32[]{:S(2)}) copy-start(s32[4]{0:T(128)} %docs_ref.5) | copy-start | bytes 52
  35.2 1.3 %collective-permute-start.1 = (f32[16,1024]{1,0:T(8,128)S(1)}, f32[16,1024]{1,0:T(8,128)S(1)}, u32[]{:S(2)}, u32[]{:S(2)}) collective-permute-start(f32[16,1024]{1,0:T(8,128)S(1)} %get-tuple-element.35), channel_id=1, source_target_pairs={{0,1},{1,0},{2,3},{3,2},{4,5},{5,4},{6,7},{7,6},{8,9},{9,8},{10,11... | collective-permute-start | bytes 196616 | tf_op jit(solution)/shard_map/ppermute | solution.py:24
  36.5 4.8 %collective-permute-start.2 = (f32[16,1024]{1,0:T(8,128)S(1)}, f32[16,1024]{1,0:T(8,128)S(1)}, u32[]{:S(2)}, u32[]{:S(2)}) collective-permute-start(f32[16,1024]{1,0:T(8,128)S(1)} %get-tuple-element.37.refs_0_), channel_id=1, source_target_pairs={{0,2},{1,3},{2,0},{3,1},{4,6},{5,7},{6,4},{7,5},{8,10},{9,11},{10,... | collective-permute-start | bytes 196616 | tf_op jit(solution)/shard_map/ppermute | solution.py:24
  41.4 15.8 %collective-permute-start.3 = (f32[16,1024]{1,0:T(8,128)S(1)}, f32[16,1024]{1,0:T(8,128)S(1)}, u32[]{:S(2)}, u32[]{:S(2)}) collective-permute-start(f32[16,1024]{1,0:T(8,128)S(1)} %get-tuple-element.38.refs_0_), channel_id=1, source_target_pairs={{0,4},{1,5},{2,6},{3,7},{4,8},{5,9},{6,10},{7,11},{8,12},{9,13},{1... | collective-permute-start | bytes 196616 | tf_op jit(solution)/shard_map/ppermute | solution.py:38
  55.3 11.9 %collective-permute-start.11 = (bf16[1,2,128,512]{3,2,1,0:T(8,128)(2,1)S(1)}, bf16[1,2,128,512]{3,2,1,0:T(8,128)(2,1)S(1)}, u32[]{:S(2)}, u32[]{:S(2)}) collective-permute-start(bf16[1,2,128,512]{3,2,1,0:T(8,128)(2,1)S(1)} %odd.2), channel_id=1, source_target_pairs={{4,8},{5,9},{8,12},{9,13},{20,24},{21,25},{24,28},{25,29}} | collective-permute-start | bytes 786440 | tf_op jit(solution)/shard_map/ppermute | solution.py:38
  57.2 10.1 %collective-permute-start.13 = (bf16[1,2,128,512]{3,2,1,0:T(8,128)(2,1)S(1)}, bf16[1,2,128,512]{3,2,1,0:T(8,128)(2,1)S(1)}, u32[]{:S(2)}, u32[]{:S(2)}) collective-permute-start(bf16[1,2,128,512]{3,2,1,0:T(8,128)(2,1)S(1)} %odd.3), channel_id=1, source_target_pairs={{6,10},{7,11},{10,14},{11,15},{22,26},{23,27},{26,30},{27,31}} | collective-permute-start | bytes 786440 | tf_op jit(solution)/shard_map/ppermute | solution.py:38
  57.9 15.8 %collective-permute-start.4 = (f32[16,1024]{1,0:T(8,128)S(1)}, f32[16,1024]{1,0:T(8,128)S(1)}, u32[]{:S(2)}, u32[]{:S(2)}) collective-permute-start(f32[16,1024]{1,0:T(8,128)S(1)} %shard_map.79), channel_id=1, source_target_pairs={{0,8},{1,9},{2,10},{3,11},{4,12},{5,13},{6,14},{7,15},{16,24},{17,... | collective-permute-start | bytes 196616 | tf_op jit(solution)/shard_map/ppermute | solution.py:38
  68.4 13.2 %collective-permute-start.15 = (bf16[128,512]{1,0:T(8,128)(2,1)S(1)}, bf16[128,512]{1,0:T(8,128)(2,1)S(1)}, u32[]{:S(2)}, u32[]{:S(2)}) collective-permute-start(bf16[128,512]{1,0:T(8,128)(2,1)S(1)} %get-tuple-element.52), channel_id=1, source_target_pairs={{0,2},{1,3},{2,0},{3,1},{4,6},{5,7},{6,4},{7,5},{8,10},{9,11},{10,... | collective-permute-start | bytes 393224 | tf_op jit(solution)/shard_map/ppermute | solution.py:24
  71.7 9.9 %collective-permute-start.16 = (bf16[128,512]{1,0:T(8,128)(2,1)S(1)}, bf16[128,512]{1,0:T(8,128)(2,1)S(1)}, u32[]{:S(2)}, u32[]{:S(2)}) collective-permute-start(bf16[128,512]{1,0:T(8,128)(2,1)S(1)} %get-tuple-element.53), channel_id=1, source_target_pairs={{0,3},{1,2},{2,1},{3,0},{4,7},{5,6},{6,5},{7,4},{8,11},{9,10},{10,... | collective-permute-start | bytes 393224 | tf_op jit(solution)/shard_map/ppermute | solution.py:24
  73.4 8.2 %collective-permute-start.14 = (bf16[128,512]{1,0:T(8,128)(2,1)S(1)}, bf16[128,512]{1,0:T(8,128)(2,1)S(1)}, u32[]{:S(2)}, u32[]{:S(2)}) collective-permute-start(bf16[128,512]{1,0:T(8,128)(2,1)S(1)} %get-tuple-element.51), channel_id=1, source_target_pairs={{0,1},{1,0},{2,3},{3,2},{4,5},{5,4},{6,7},{7,6},{8,9},{9,8},{10,11... | collective-permute-start | bytes 393224 | tf_op jit(solution)/shard_map/ppermute | solution.py:24
  73.7 5.4 %collective-permute-start.5 = (f32[16,1024]{1,0:T(8,128)S(1)}, f32[16,1024]{1,0:T(8,128)S(1)}, u32[]{:S(2)}, u32[]{:S(2)}) collective-permute-start(f32[16,1024]{1,0:T(8,128)S(1)} %get-tuple-element.43), channel_id=1, source_target_pairs={{0,1},{1,0},{2,3},{3,2},{4,5},{5,4},{6,7},{7,6},{8,9},{9,8},{10,11... | collective-permute-start | bytes 196616 | tf_op jit(solution)/shard_map/ppermute | solution.py:24

commit v3 on v2

--- a/solution.py
+++ b/solution.py
@@ -41,6 +41,11 @@
 def spot():
     index = lax.axis_index("ctx")
     return index & 1, lax.shift_right_logical(index, 1) & 1, index & (ROW - 1), index // ROW
+
+
+def next_block(value, axis, first):
+    count = lax.axis_size(axis)
+    return lax.ppermute(value, axis, [(at, at + 1) for at in range(first, count - 1, 2)])
 
 
 ALL_VMEM = 67043328
@@ -75,6 +80,10 @@
     return kept
 
 
+def either(one, other):
+    return one.astype(F32) + other.astype(F32)
+
+
 def feature(x, halo, w_ref, stream, at):
     here = x.astype(F32)
     halo = halo.astype(F32)
@@ -98,7 +107,7 @@
 
 
 def hyena_ends_body(
-    filters, x_ref, halo_ref, w_ref, rate_ref, res_ref, mixed_ref, keep_ref, away_ref, wide_ref, gain_ref, all_s
+    filters, x_ref, halo_ref, other_ref, w_ref, rate_ref, res_ref, mixed_ref, keep_ref, away_ref, wide_ref, gain_ref, all_s
 ):
     rows = x_ref.shape[1]
     modes, groups = rate_ref.shape
@@ -114,7 +123,9 @@
     step = pl.program_id(0)
     for part in range(parts):
         at = slice(part * lanes, (part + 1) * lanes)
-        key, value = (feature(x_ref[n, :, at], halo_ref[n, :, at], w_ref, n, at) for n in (1, 2))
+        key, value = (
+            feature(x_ref[n, :, at], either(halo_ref[n, :, at], other_ref[n, :, at]), w_ref, n, at) for n in (1, 2)
+        )
         mixed = (key * value).astype(BF16)
         mixed_ref[:, at] = mixed
         rate = down(rates, part, filters, rows)
@@ -142,9 +153,9 @@
 STEPS = 4
 
 
-def hyena_ends(streams, halo, short_weight, rates, residues):
+def hyena_ends(streams, halos, short_weight, rates, residues):
     _, rows, channels = streams.shape
-    edge = halo.shape[1]
+    edge = halos[0].shape[1]
     modes, groups = rates.shape
     filters = groups * LANES // channels
     terms = filters * modes
@@ -157,6 +168,7 @@
         grid=(STEPS,),
         in_specs=[
             pl.BlockSpec((3, rows, wide), lead),
+            pl.BlockSpec((3, edge, wide), lead),
             pl.BlockSpec((3, edge, wide), lead),
             pl.BlockSpec((3, 3, wide), lead),
             pl.BlockSpec((modes, groups), whole),
@@ -168,11 +180,11 @@
         compiler_params=limits(16),
         cost_estimate=cost(4 * rows * terms * channels, 8 * rows * channels),
         name="hyena_ends",
-    )(streams, halo, short_weight, rates, residues)
+    )(streams, *halos, short_weight, rates, residues)
 
 
 def hyena_near_body(
-    filters, x_ref, halo_ref, w_ref, mixed_ref, rate_ref, res_ref, near_ref, q_ref, high_ref, low_ref, taps_s, u_s
+    filters, x_ref, halo_ref, other_ref, w_ref, mixed_ref, rate_ref, res_ref, near_ref, q_ref, high_ref, low_ref, taps_s, u_s
 ):
     rows = mixed_ref.shape[0]
     modes, groups = rate_ref.shape
@@ -201,7 +213,7 @@
             mine = (lane_at >= g * width) & (lane_at < (g + 1) * width)
             u_s[part, g * rows : (g + 1) * rows, :] = jnp.where(mine, mixed, zero)
         near_ref[:, at] = jnp.dot(taps_s[part], u_s[part], preferred_element_type=F32)
-        q_ref[:, at] = feature(x_ref[0, :, at], halo_ref[0, :, at], w_ref, 0, at)
+        q_ref[:, at] = feature(x_ref[0, :, at], either(halo_ref[0, :, at], other_ref[0, :, at]), w_ref, 0, at)
         decays = jnp.exp(-rate * ahead_lag).T
         here = slice(part * terms, (part + 1) * terms)
         high = decays.astype(BF16)
@@ -209,9 +221,9 @@
         low_ref[:, here] = (decays - high.astype(F32)).astype(BF16)
 
 
-def hyena_near(streams, halo, short_weight, mixed, rates, residues):
+def hyena_near(streams, halos, short_weight, mixed, rates, residues):
     rows, channels = mixed.shape
-    edge = halo.shape[1]
+    edge = halos[0].shape[1]
     modes, groups = rates.shape
     lanes = LANES
     filters = groups * lanes // channels
@@ -226,6 +238,7 @@
         grid=(STEPS,),
         in_specs=[
             pl.BlockSpec((1, rows, wide), lead),
+            pl.BlockSpec((1, edge, wide), lead),
             pl.BlockSpec((1, edge, wide), lead),
             pl.BlockSpec((3, 3, wide), lead),
             pl.BlockSpec((rows, wide), by_block),
@@ -242,7 +255,7 @@
         compiler_params=limits(16),
         cost_estimate=cost(2 * rows * rows * filters * channels, 12 * rows * channels),
         name="hyena_near",
-    )(streams, halo, short_weight, mixed, rates, residues)
+    )(streams, *halos, short_weight, mixed, rates, residues)
 
 
 def hyena_out_body(modes, near_ref, q_ref, high_ref, low_ref, keep_ref, back_ref, out_ref):
@@ -668,7 +681,7 @@
     theirs, edge = front(streams, inner)
 
     theirs = flip(theirs, "ctx", 1)
-    edge = ahead(edge, "ctx", 1)
+    edges = (next_block(edge, "ctx", 0), next_block(edge, "ctx", 1))
     own, cross = pack(streams, theirs, 1, 2)
     cross = ahead(cross, "ctx", ROW, 2)
     own = ahead(own, "ctx", ROW)
@@ -681,8 +694,8 @@
         ahead(odd(cross, 1), "ctx", ROW, 0, ROW, 1),
     )
 
-    mixed, keep, away, wide, gain = hyena_ends(inner, edge, short_weight, rates, residues)
-    near, query, high, low = hyena_near(inner, edge, short_weight, mixed, rates, residues)
+    mixed, keep, away, wide, gain = hyena_ends(inner, edges, short_weight, rates, residues)
+    near, query, high, low = hyena_near(inner, edges, short_weight, mixed, rates, residues)
     keep, back = scan_states(keep, away, wide, gain, rows)
     hyena_out = hyena_finish(near, query, high, low, keep, back)
 

time: 82.8 us -> 81.8 us (0.988)
  starting transfers between devices: 39.4 us -> 37.5 us
    ppermute x9 -> x8, starting transfers between devices: 31.8 us -> 27.3 us  [ahead(): return lax.ppermute(value, axis, pairs)]
    ppermute x0 -> x2, starting transfers between devices: none -> 1.95 us  [next_block(): lax.ppermute(value, axis, [(at, at + 1) for at in range(first, count - 1,...]
    ppermute x9 -> x8, waiting for transfers between devices: 16.6 us -> 16.9 us  [ahead(): return lax.ppermute(value, axis, pairs)]
  transfers between devices with their start and end apart: 17 -> 18, of which waited for: 6 -> 6; matrix products, arithmetic and copies ran while one was open for 0% -> 0% of each run, Pallas kernels for 21% -> 22%
where the time goes in v3:
time: 81.8 us; the launch traced here: 81.4 us
  starting transfers between devices  37.5 us (46%)
  waiting for transfers between devices  23 us (28%)
  Pallas kernels  19.9 us (24%)
  between operations  0.97 us (1%)
    ppermute x8, starting transfers between devices, ahead(): return lax.ppermute(value, axis, pairs)  27.3 us
    ppermute x8, waiting for transfers between devices, ahead(): return lax.ppermute(value, axis, pairs)  16.9 us
    ppermute x8, starting transfers between devices, flip(): return lax.ppermute(value, axis, [(at, at ^ bit) for at in range(count)])  8.27 us
    ppermute x8, waiting for transfers between devices, flip(): return lax.ppermute(value, axis, [(at, at ^ bit) for at in range(count)])  6.1 us
    pallas_call x1, Pallas kernels, hyena_near(): pl.pallas_call(functools.partial(hyena_near_body, filters), grid=(STEPS,)...  5.07 us
    pallas_call x1, Pallas kernels, attend(): pl.pallas_call(attend_body, in_specs=[SMEM] + [VMEM] * 5, out_specs=[VMEM...  4.84 us
    pallas_call x2, Pallas kernels, attend_last(): pl.pallas_call(functools.partial(attend_last_body, pair), in_specs=[SMEM]...  2.78 us
    pallas_call x1, Pallas kernels, hyena_finish(): pl.pallas_call(functools.partial(hyena_out_body, modes), grid=(STEPS,), i...  2.44 us
  transfers between devices with their start and end apart: 18, of which 6 were waited for; matrix products, arithmetic and copies ran while one was open for 0% of the time, Pallas kernels for 22%

profile of v3, /device:TPU:0, one launch (start us, length us, event | category | flops | bytes accessed | tf_op | source)
XLA Modules:
  0.0 81.4 jit_solution(11130939448841539633)
XLA Ops:
  0.6 1.3 %front.1 = (bf16[3,128,1024]{2,1,0:T(8,128)(2,1)S(1)}, bf16[3,8,2048]{2,1,0:T(8,128)(2,1)S(1)}) custom-call(bf16[3,128,2048]{2,1,0:T(8,128)(2,1)} %bitcast.4, bf16[3,128,2048]{2,1,0:T(8,128)(2,1)} %bitcast.10), custom_call_target="tpu_custom_call" | custom-call | bytes 1572864 | tf_op jit(solution)/shard_map/front/pallas_call | solution.py:396
  1.9 0.6 collective-permute-start.7
  2.5 1.9 %collective-permute-done.7.theirs_ref.theirs = bf16[3,128,1024]{2,1,0:T(8,128)(2,1)S(1)} collective-permute-done((bf16[3,128,1024]{2,1,0:T(8,128)(2,1)S(1)}, bf16[3,128,1024]{2,1,0:T(8,128)(2,1)S(1)}, u32[]{:S(2)}, u32[]{:S(2)}) %collective-permute-start.7) | collective-permute-done | bytes 786464 | tf_op jit(solution)/shard_map/ppermute | solution.py:24
  4.4 0.1 pack.3
  4.5 5.8 %collective-permute-start.9 = (bf16[2,2,128,512]{3,2,1,0:T(8,128)(2,1)S(1)}, bf16[2,2,128,512]{3,2,1,0:T(8,128)(2,1)S(1)}, u32[]{:S(2)}, u32[]{:S(2)}) collective-permute-start(bf16[2,2,128,512]{3,2,1,0:T(8,128)(2,1)S(1)} %get-tuple-element.45), channel_id=1, source_target_pairs={{0,6},{1,7},{2,4},{3,5},{4,10},{5,11},{6,8},{7,9},{8,14},{9,15},{1... | collective-permute-start | bytes 1572872 | tf_op jit(solution)/shard_map/ppermute | solution.py:38
  10.4 3.6 %collective-permute-start.11 = (bf16[2,2,128,512]{3,2,1,0:T(8,128)(2,1)S(1)}, bf16[2,2,128,512]{3,2,1,0:T(8,128)(2,1)S(1)}, u32[]{:S(2)}, u32[]{:S(2)}) collective-permute-start(bf16[2,2,128,512]{3,2,1,0:T(8,128)(2,1)S(1)} %get-tuple-element.46), channel_id=1, source_target_pairs={{0,4},{1,5},{2,6},{3,7},{4,8},{5,9},{6,10},{7,11},{8,12},{9,13},{1... | collective-permute-start | bytes 1572872 | tf_op jit(solution)/shard_map/ppermute | solution.py:38
  14.1 0.6 collective-permute-start.8
  14.6 1.3 %collective-permute-start = (bf16[3,8,2048]{2,1,0:T(8,128)(2,1)S(1)}, bf16[3,8,2048]{2,1,0:T(8,128)(2,1)S(1)}, u32[]{:S(2)}, u32[]{:S(2)}) collective-permute-start(bf16[3,8,2048]{2,1,0:T(8,128)(2,1)S(1)} %get-tuple-element.28), channel_id=1, source_target_pairs={{0,1},{2,3},{4,5},{6,7},{8,9},{10,11},{12,13},{14,15},{16,17},{18,... | collective-permute-start | bytes 294920 | tf_op jit(solution)/shard_map/ppermute | solution.py:48
  15.9 0.7 collective-permute-start.1
  16.6 6.0 %collective-permute-done.9.pairs.cross = bf16[2,2,128,512]{3,2,1,0:T(8,128)(2,1)S(1)} collective-permute-done((bf16[2,2,128,512]{3,2,1,0:T(8,128)(2,1)S(1)}, bf16[2,2,128,512]{3,2,1,0:T(8,128)(2,1)S(1)}, u32[]{:S(2)}, u32[]{:S(2)}) %collective-permute-start.9) | collective-permute-done | bytes 524320 | tf_op jit(solution)/shard_map/ppermute | solution.py:38
  22.6 0.7 collective-permute-start.10
  23.3 9.7 %collective-permute-done.11.pairs.own = bf16[2,2,128,512]{3,2,1,0:T(8,128)(2,1)S(1)} collective-permute-done((bf16[2,2,128,512]{3,2,1,0:T(8,128)(2,1)S(1)}, bf16[2,2,128,512]{3,2,1,0:T(8,128)(2,1)S(1)}, u32[]{:S(2)}, u32[]{:S(2)}) %collective-permute-start.11) | collective-permute-done | bytes 524320 | tf_op jit(solution)/shard_map/ppermute | solution.py:38
  33.0 0.7 collective-permute-start.13
  33.8 2.3 %hyena_ends.1 = (bf16[128,2048]{1,0:T(8,128)(2,1)S(1)}, f32[16,1024]{1,0:T(8,128)S(1)}, f32[16,1024]{1,0:T(8,128)S(1)}, f32[16,1024]{1,0:T(8,128)S(1)}, f32[16,1024]{1,0:T(8,128)S(1)}) custom-call(bf16[3,128,2048]{2,1,0:T(8,128)(2,1)S(1)} %bitcast.11, bf16[3,8,2048]{2,1,0:T(8,128)(2,1)S(1)} %collective-permute-done.halo_ref, ...), custom_call_target="tpu_custom_call" | custom-call | flops 134217728 | bytes 2097152 | tf_op jit(solution)/shard_map/hyena_ends/pallas_call | solution.py:166
  36.1 0.1 collective-permute-start.2
  36.2 1.2 %collective-permute-done.2.refs_1_ = f32[16,1024]{1,0:T(8,128)S(1)} collective-permute-done((f32[16,1024]{1,0:T(8,128)S(1)}, f32[16,1024]{1,0:T(8,128)S(1)}, u32[]{:S(2)}, u32[]{:S(2)}) %collective-permute-start.2) | collective-permute-done | bytes 65568 | tf_op jit(solution)/shard_map/ppermute | solution.py:24
  37.5 1.4 %collective-permute-start.3 = (f32[16,1024]{1,0:T(8,128)S(1)}, f32[16,1024]{1,0:T(8,128)S(1)}, u32[]{:S(2)}, u32[]{:S(2)}) collective-permute-start(f32[16,1024]{1,0:T(8,128)S(1)} %get-tuple-element.37.refs_0_), channel_id=1, source_target_pairs={{0,2},{1,3},{2,0},{3,1},{4,6},{5,7},{6,4},{7,5},{8,10},{9,11},{10,... | collective-permute-start | bytes 196616 | tf_op jit(solution)/shard_map/ppermute | solution.py:24
  38.9 2.9 %collective-permute-done.3.refs_1_ = f32[16,1024]{1,0:T(8,128)S(1)} collective-permute-done((f32[16,1024]{1,0:T(8,128)S(1)}, f32[16,1024]{1,0:T(8,128)S(1)}, u32[]{:S(2)}, u32[]{:S(2)}) %collective-permute-start.3) | collective-permute-done | bytes 65568 | tf_op jit(solution)/shard_map/ppermute | solution.py:24
  41.8 9.9 %collective-permute-start.4 = (f32[16,1024]{1,0:T(8,128)S(1)}, f32[16,1024]{1,0:T(8,128)S(1)}, u32[]{:S(2)}, u32[]{:S(2)}) collective-permute-start(f32[16,1024]{1,0:T(8,128)S(1)} %get-tuple-element.38.refs_0_), channel_id=1, source_target_pairs={{0,4},{1,5},{2,6},{3,7},{4,8},{5,9},{6,10},{7,11},{8,12},{9,13},{1... | collective-permute-start | bytes 196616 | tf_op jit(solution)/shard_map/ppermute | solution.py:38
  51.8 0.7 collective-permute-start.12
  52.5 1.1 %collective-permute-done.4.refs_1_.refs_0_ = f32[16,1024]{1,0:T(8,128)S(1)} collective-permute-done((f32[16,1024]{1,0:T(8,128)S(1)}, f32[16,1024]{1,0:T(8,128)S(1)}, u32[]{:S(2)}, u32[]{:S(2)}) %collective-permute-start.4) | collective-permute-done | bytes 65568 | tf_op jit(solution)/shard_map/ppermute | solution.py:38
  53.6 0.7 collective-permute-start.14
  54.3 5.3 %collective-permute-start.5 = (f32[16,1024]{1,0:T(8,128)S(1)}, f32[16,1024]{1,0:T(8,128)S(1)}, u32[]{:S(2)}, u32[]{:S(2)}) collective-permute-start(f32[16,1024]{1,0:T(8,128)S(1)} %shard_map.79), channel_id=1, source_target_pairs={{0,8},{1,9},{2,10},{3,11},{4,12},{5,13},{6,14},{7,15},{16,24},{17,... | collective-permute-start | bytes 196616 | tf_op jit(solution)/shard_map/ppermute | solution.py:38
  59.6 4.8 %attend.1 = (f32[512,512]{1,0:T(8,128)S(1)}, f32[512,512]{1,0:T(8,128)S(1)}, f32[512,512]{1,0:T(8,128)S(1)}) custom-call(s32[4]{0:T(128)S(1)} %copy-done.5, bf16[3,128,2048]{2,1,0:T(8,128)(2,1)S(1)} %bitcast.7, bf16[3,128,1024]{2,1,0:T(8,128)(2,1)S(1)} %collective-permute-done.7.theirs_ref.theirs, bf16[2,3,128,512]{3,2,1,0:T(8,128)(2,1)S(1)} %collective-permute-done.8.swap, ...), custom_call_target="tpu_custom_call" | custom-call | flops 872415232 | bytes 3670016 | tf_op jit(solution)/shard_map/attend/pallas_call | solution.py:561
  64.5 1.1 %attend_last.3 = (bf16[128,512]{1,0:T(8,128)(2,1)S(1)}, bf16[128,512]{1,0:T(8,128)(2,1)S(1)}) custom-call(s32[4]{0:T(128)S(1)} %copy-done.5, bf16[3,128,2048]{2,1,0:T(8,128)(2,1)S(1)} %bitcast.8, bf16[3,128,1024]{2,1,0:T(8,128)(2,1)S(1)} %collective-permute-done.7.theirs_ref.theirs, bf16[2,3,128,512]{3,2,1,0:T(8,128)(2,1)S(1)} %collective-permute-done.8.swap, ...), custom_call_target="tpu_custom_call" | custom-call | flops 134217728 | bytes 1572864 | tf_op jit(solution)/shard_map/attend_last/pallas_call | solution.py:641
  65.7 5.0 %collective-permute-start.16 = (bf16[128,512]{1,0:T(8,128)(2,1)S(1)}, bf16[128,512]{1,0:T(8,128)(2,1)S(1)}, u32[]{:S(2)}, u32[]{:S(2)}) collective-permute-start(bf16[128,512]{1,0:T(8,128)(2,1)S(1)} %get-tuple-element.52), channel_id=1, source_target_pairs={{0,2},{1,3},{2,0},{3,1},{4,6},{5,7},{6,4},{7,5},{8,10},{9,11},{10,... | collective-permute-start | bytes 393224 | tf_op jit(solution)/shard_map/ppermute | solution.py:24
  70.7 1.6 %attend_last.2 = (bf16[128,512]{1,0:T(8,128)(2,1)S(1)}, bf16[128,512]{1,0:T(8,128)(2,1)S(1)}) custom-call(s32[4]{0:T(128)S(1)} %copy-done.5, bf16[3,128,2048]{2,1,0:T(8,128)(2,1)S(1)} %bitcast.9, bf16[3,128,1024]{2,1,0:T(8,128)(2,1)S(1)} %collective-permute-done.7.theirs_ref.theirs, bf16[2,3,128,512]{3,2,1,0:T(8,128)(2,1)S(1)} %collective-permute-done.8.swap, ...), custom_call_target="tpu_custom_call" | custom-call | flops 134217728 | bytes 1572864 | tf_op jit(solution)/shard_map/attend_last/pallas_call | solution.py:641
  72.4 0.3 collective-permute-start.15
  72.7 0.4 collective-permute-start.6
  73.1 5.1 %hyena_near.1 = (f32[128,2048]{1,0:T(8,128)S(1)}, f32[128,2048]{1,0:T(8,128)S(1)}, bf16[128,2048]{1,0:T(8,128)(2,1)S(1)}, bf16[128,2048]{1,0:T(8,128)(2,1)S(1)}) custom-call(bf16[3,128,2048]{2,1,0:T(8,128)(2,1)S(1)} %bitcast.12, bf16[3,8,2048]{2,1,0:T(8,128)(2,1)S(1)} %collective-permute-done.halo_ref, ...), custom_call_target="tpu_custom_call" | custom-call | flops 536870912 | bytes 3145728 | tf_op jit(solution)/shard_map/hyena_near/pallas_call | solution.py:236
  78.2 2.4 %hyena_finish.1 = bf16[128,2048]{1,0:T(8,128)(2,1)} custom-call(f32[128,2048]{1,0:T(8,128)S(1)} %get-tuple-element.30.near_ref, f32[128,2048]{1,0:T(8,128)S(1)} %get-tuple-element.31.q_ref, bf16[128,2048]{1,0:T(8,128)(2,1)S(1)} %get-tuple-element.32.high_ref, bf16[128,2048]{1,0:T(8,128)(2,1)S(1)} %get-tuple-element.33.low_ref, ...), custom_call_target="tpu_custom_call" | custom-call | flops 201326592 | bytes 2621440 | tf_op jit(solution)/shard_map/hyena_finish/pallas_call | solution.py:289
  80.6 0.8 %assemble.1 = bf16[128,2048]{1,0:T(8,128)(2,1)} custom-call(bf16[128,512]{1,0:T(8,128)(2,1)S(1)} %get-tuple-element.50.refs_0_, bf16[128,512]{1,0:T(8,128)(2,1)S(1)} %collective-permute-done.15.refs_1_, bf16[128,512]{1,0:T(8,128)(2,1)S(1)} %collective-permute-done.16.refs_2_, bf16[128,512]{1,0:T(8,128)(2,1)S(1)} %collective-permute-done.17.refs_3_), custom_call_target="tpu_custom_call" | custom-call | bytes 1048576 | tf_op jit(solution)/shard_map/assemble/pallas_call | solution.py:665
  (32 shorter events, 0.3 us)
Async XLA Ops:
  0.6 3.8 %copy-start = (bf16[128,3,2048]{2,0,1:T(8,128)(2,1)S(1)}, bf16[128,3,2048]{2,0,1:T(8,128)(2,1)}, u32[]{:S(2)}) copy-start(bf16[128,3,2048]{2,0,1:T(8,128)(2,1)} %param.10) | copy-start | bytes 4718596
  1.9 2.5 %collective-permute-start.7 = (bf16[3,128,1024]{2,1,0:T(8,128)(2,1)S(1)}, bf16[3,128,1024]{2,1,0:T(8,128)(2,1)S(1)}, u32[]{:S(2)}, u32[]{:S(2)}) collective-permute-start(bf16[3,128,1024]{2,1,0:T(8,128)(2,1)S(1)} %get-tuple-element.44), channel_id=1, source_target_pairs={{0,1},{1,0},{2,3},{3,2},{4,5},{5,4},{6,7},{7,6},{8,9},{9,8},{10,11... | collective-permute-start | bytes 2359304 | tf_op jit(solution)/shard_map/ppermute | solution.py:24
  4.5 18.1 %collective-permute-start.9 = (bf16[2,2,128,512]{3,2,1,0:T(8,128)(2,1)S(1)}, bf16[2,2,128,512]{3,2,1,0:T(8,128)(2,1)S(1)}, u32[]{:S(2)}, u32[]{:S(2)}) collective-permute-start(bf16[2,2,128,512]{3,2,1,0:T(8,128)(2,1)S(1)} %get-tuple-element.45), channel_id=1, source_target_pairs={{0,6},{1,7},{2,4},{3,5},{4,10},{5,11},{6,8},{7,9},{8,14},{9,15},{1... | collective-permute-start | bytes 1572872 | tf_op jit(solution)/shard_map/ppermute | solution.py:38
  10.3 23.4 %copy-start.1 = (bf16[128,3,2048]{2,0,1:T(8,128)(2,1)S(1)}, bf16[128,3,2048]{2,0,1:T(8,128)(2,1)}, u32[]{:S(2)}) copy-start(bf16[128,3,2048]{2,0,1:T(8,128)(2,1)} %param.6) | copy-start | bytes 4718596
  10.3 23.4 %copy-start.2 = (f32[3,3,2048]{2,1,0:T(4,128)S(1)}, f32[3,3,2048]{2,1,0:T(4,128)}, u32[]{:S(2)}) copy-start(f32[3,3,2048]{2,1,0:T(4,128)} %w_ref.3) | copy-start | bytes 221188
  10.3 23.4 %copy-start.3 = (f32[128,16]{0,1:T(8,128)S(1)}, f32[128,16]{0,1:T(8,128)}, u32[]{:S(2)}) copy-start(f32[128,16]{0,1:T(8,128)} %param.8) | copy-start | bytes 24580
  10.3 23.4 %copy-start.4 = (f32[128,16]{0,1:T(8,128)S(1)}, f32[128,16]{0,1:T(8,128)}, u32[]{:S(2)}) copy-start(f32[128,16]{0,1:T(8,128)} %param.9) | copy-start | bytes 24580
  10.4 22.7 %collective-permute-start.11 = (bf16[2,2,128,512]{3,2,1,0:T(8,128)(2,1)S(1)}, bf16[2,2,128,512]{3,2,1,0:T(8,128)(2,1)S(1)}, u32[]{:S(2)}, u32[]{:S(2)}) collective-permute-start(bf16[2,2,128,512]{3,2,1,0:T(8,128)(2,1)S(1)} %get-tuple-element.46), channel_id=1, source_target_pairs={{0,4},{1,5},{2,6},{3,7},{4,8},{5,9},{6,10},{7,11},{8,12},{9,13},{1... | collective-permute-start | bytes 1572872 | tf_op jit(solution)/shard_map/ppermute | solution.py:38
  14.1 40.3 %collective-permute-start.8 = (bf16[2,3,128,512]{3,2,1,0:T(8,128)(2,1)S(1)}, bf16[2,3,128,512]{3,2,1,0:T(8,128)(2,1)S(1)}, u32[]{:S(2)}, u32[]{:S(2)}) collective-permute-start(bf16[2,3,128,512]{3,2,1,0:T(8,128)(2,1)S(1)} %pack.2), channel_id=1, source_target_pairs={{0,2},{1,3},{2,0},{3,1},{4,6},{5,7},{6,4},{7,5},{8,10},{9,11},{10,... | collective-permute-start | bytes 2359304 | tf_op jit(solution)/shard_map/ppermute | solution.py:24
  14.6 19.1 %collective-permute-start = (bf16[3,8,2048]{2,1,0:T(8,128)(2,1)S(1)}, bf16[3,8,2048]{2,1,0:T(8,128)(2,1)S(1)}, u32[]{:S(2)}, u32[]{:S(2)}) collective-permute-start(bf16[3,8,2048]{2,1,0:T(8,128)(2,1)S(1)} %get-tuple-element.28), channel_id=1, source_target_pairs={{0,1},{2,3},{4,5},{6,7},{8,9},{10,11},{12,13},{14,15},{16,17},{18,... | collective-permute-start | bytes 294920 | tf_op jit(solution)/shard_map/ppermute | solution.py:48
  15.9 17.8 %collective-permute-start.1 = (bf16[3,8,2048]{2,1,0:T(8,128)(2,1)S(1)}, bf16[3,8,2048]{2,1,0:T(8,128)(2,1)S(1)}, u32[]{:S(2)}, u32[]{:S(2)}) collective-permute-start(bf16[3,8,2048]{2,1,0:T(8,128)(2,1)S(1)} %get-tuple-element.28), channel_id=1, source_target_pairs={{1,2},{3,4},{5,6},{7,8},{9,10},{11,12},{13,14},{17,18},{19,20},{21... | collective-permute-start | bytes 294920 | tf_op jit(solution)/shard_map/ppermute | solution.py:48
  22.6 41.9 %collective-permute-start.10 = (bf16[2,2,128,512]{3,2,1,0:T(8,128)(2,1)S(1)}, bf16[2,2,128,512]{3,2,1,0:T(8,128)(2,1)S(1)}, u32[]{:S(2)}, u32[]{:S(2)}) collective-permute-start(bf16[2,2,128,512]{3,2,1,0:T(8,128)(2,1)S(1)} %collective-permute-done.9.pairs.cross), channel_id=1, source_target_pairs={{4,8},{5,9},{8,12},{9,13},{20,24},{21,25},{24,28},{25,29}} | collective-permute-start | bytes 1572872 | tf_op jit(solution)/shard_map/ppermute | solution.py:38
  33.0 31.5 %collective-permute-start.13 = (bf16[2,2,128,512]{3,2,1,0:T(8,128)(2,1)S(1)}, bf16[2,2,128,512]{3,2,1,0:T(8,128)(2,1)S(1)}, u32[]{:S(2)}, u32[]{:S(2)}) collective-permute-start(bf16[2,2,128,512]{3,2,1,0:T(8,128)(2,1)S(1)} %collective-permute-done.11.pairs.own), channel_id=1, source_target_pairs={{6,10},{7,11},{10,14},{11,15},{22,26},{23,27},{26,30},{27,31}} | collective-permute-start | bytes 1572872 | tf_op jit(solution)/shard_map/ppermute | solution.py:38
  36.1 23.5 %copy-start.5 = (s32[4]{0:T(128)S(1)}, s32[4]{0:T(128)}, u32[]{:S(2)}) copy-start(s32[4]{0:T(128)} %docs_ref.5) | copy-start | bytes 52
  36.1 1.3 %collective-permute-start.2 = (f32[16,1024]{1,0:T(8,128)S(1)}, f32[16,1024]{1,0:T(8,128)S(1)}, u32[]{:S(2)}, u32[]{:S(2)}) collective-permute-start(f32[16,1024]{1,0:T(8,128)S(1)} %get-tuple-element.35), channel_id=1, source_target_pairs={{0,1},{1,0},{2,3},{3,2},{4,5},{5,4},{6,7},{7,6},{8,9},{9,8},{10,11... | collective-permute-start | bytes 196616 | tf_op jit(solution)/shard_map/ppermute | solution.py:24
  37.5 4.3 %collective-permute-start.3 = (f32[16,1024]{1,0:T(8,128)S(1)}, f32[16,1024]{1,0:T(8,128)S(1)}, u32[]{:S(2)}, u32[]{:S(2)}) collective-permute-start(f32[16,1024]{1,0:T(8,128)S(1)} %get-tuple-element.37.refs_0_), channel_id=1, source_target_pairs={{0,2},{1,3},{2,0},{3,1},{4,6},{5,7},{6,4},{7,5},{8,10},{9,11},{10,... | collective-permute-start | bytes 196616 | tf_op jit(solution)/shard_map/ppermute | solution.py:24
  41.8 11.8 %collective-permute-start.4 = (f32[16,1024]{1,0:T(8,128)S(1)}, f32[16,1024]{1,0:T(8,128)S(1)}, u32[]{:S(2)}, u32[]{:S(2)}) collective-permute-start(f32[16,1024]{1,0:T(8,128)S(1)} %get-tuple-element.38.refs_0_), channel_id=1, source_target_pairs={{0,4},{1,5},{2,6},{3,7},{4,8},{5,9},{6,10},{7,11},{8,12},{9,13},{1... | collective-permute-start | bytes 196616 | tf_op jit(solution)/shard_map/ppermute | solution.py:38
  51.8 12.7 %collective-permute-start.12 = (bf16[1,2,128,512]{3,2,1,0:T(8,128)(2,1)S(1)}, bf16[1,2,128,512]{3,2,1,0:T(8,128)(2,1)S(1)}, u32[]{:S(2)}, u32[]{:S(2)}) collective-permute-start(bf16[1,2,128,512]{3,2,1,0:T(8,128)(2,1)S(1)} %odd.2), channel_id=1, source_target_pairs={{4,8},{5,9},{8,12},{9,13},{20,24},{21,25},{24,28},{25,29}} | collective-permute-start | bytes 786440 | tf_op jit(solution)/shard_map/ppermute | solution.py:38
  53.6 10.9 %collective-permute-start.14 = (bf16[1,2,128,512]{3,2,1,0:T(8,128)(2,1)S(1)}, bf16[1,2,128,512]{3,2,1,0:T(8,128)(2,1)S(1)}, u32[]{:S(2)}, u32[]{:S(2)}) collective-permute-start(bf16[1,2,128,512]{3,2,1,0:T(8,128)(2,1)S(1)} %odd.3), channel_id=1, source_target_pairs={{6,10},{7,11},{10,14},{11,15},{22,26},{23,27},{26,30},{27,31}} | collective-permute-start | bytes 786440 | tf_op jit(solution)/shard_map/ppermute | solution.py:38
  54.3 18.3 %collective-permute-start.5 = (f32[16,1024]{1,0:T(8,128)S(1)}, f32[16,1024]{1,0:T(8,128)S(1)}, u32[]{:S(2)}, u32[]{:S(2)}) collective-permute-start(f32[16,1024]{1,0:T(8,128)S(1)} %shard_map.79), channel_id=1, source_target_pairs={{0,8},{1,9},{2,10},{3,11},{4,12},{5,13},{6,14},{7,15},{16,24},{17,... | collective-permute-start | bytes 196616 | tf_op jit(solution)/shard_map/ppermute | solution.py:38
  65.7 14.9 %collective-permute-start.16 = (bf16[128,512]{1,0:T(8,128)(2,1)S(1)}, bf16[128,512]{1,0:T(8,128)(2,1)S(1)}, u32[]{:S(2)}, u32[]{:S(2)}) collective-permute-start(bf16[128,512]{1,0:T(8,128)(2,1)S(1)} %get-tuple-element.52), channel_id=1, source_target_pairs={{0,2},{1,3},{2,0},{3,1},{4,6},{5,7},{6,4},{7,5},{8,10},{9,11},{10,... | collective-permute-start | bytes 393224 | tf_op jit(solution)/shard_map/ppermute | solution.py:24
  70.7 9.9 %collective-permute-start.17 = (bf16[128,512]{1,0:T(8,128)(2,1)S(1)}, bf16[128,512]{1,0:T(8,128)(2,1)S(1)}, u32[]{:S(2)}, u32[]{:S(2)}) collective-permute-start(bf16[128,512]{1,0:T(8,128)(2,1)S(1)} %get-tuple-element.53), channel_id=1, source_target_pairs={{0,3},{1,2},{2,1},{3,0},{4,7},{5,6},{6,5},{7,4},{8,11},{9,10},{10,... | collective-permute-start | bytes 393224 | tf_op jit(solution)/shard_map/ppermute | solution.py:24
  72.4 8.2 %collective-permute-start.15 = (bf16[128,512]{1,0:T(8,128)(2,1)S(1)}, bf16[128,512]{1,0:T(8,128)(2,1)S(1)}, u32[]{:S(2)}, u32[]{:S(2)}) collective-permute-start(bf16[128,512]{1,0:T(8,128)(2,1)S(1)} %get-tuple-element.51), channel_id=1, source_target_pairs={{0,1},{1,0},{2,3},{3,2},{4,5},{5,4},{6,7},{7,6},{8,9},{9,8},{10,11... | collective-permute-start | bytes 393224 | tf_op jit(solution)/shard_map/ppermute | solution.py:24
  72.7 5.5 %collective-permute-start.6 = (f32[16,1024]{1,0:T(8,128)S(1)}, f32[16,1024]{1,0:T(8,128)S(1)}, u32[]{:S(2)}, u32[]{:S(2)}) collective-permute-start(f32[16,1024]{1,0:T(8,128)S(1)} %get-tuple-element.43), channel_id=1, source_target_pairs={{0,1},{1,0},{2,3},{3,2},{4,5},{5,4},{6,7},{7,6},{8,9},{9,8},{10,11... | collective-permute-start | bytes 196616 | tf_op jit(solution)/shard_map/ppermute | solution.py:24

commit v4 on v2

--- a/solution.py
+++ b/solution.py
@@ -36,6 +36,11 @@
         if side is None or side_of(at) == side
     ]
     return lax.ppermute(value, axis, pairs)
+
+
+def to_side_0(value, axis):
+    count = lax.axis_size(axis)
+    return lax.ppermute(value, axis, [(at, at ^ 2) for at in range(count) if side_of(at)])
 
 
 def spot():
@@ -329,7 +334,9 @@
 
     other = flip(chip, "ctx", 2)
     total, left = small(whole, chip, other, rate, outs=2)
-    before = ahead(total, "ctx", ROW)
+    direct = ahead(total, "ctx", ROW, 0, 0, 1)
+    handed = to_side_0(direct, "ctx")
+    before = small(lambda one, other: one + other, direct, handed)
     reach = 2
     while reach < count:
         upto = small(lambda total, before, rate: total + decay(ROW, rate) * before, total, before, rate)

time: 82.8 us -> 91.5 us (1.11)
  starting transfers between devices: 39.4 us -> 46.8 us
  waiting for transfers between devices: 22.2 us -> 23.4 us
    ppermute x0 -> x1, waiting for transfers between devices: none -> 18.1 us  [to_side_0(): lax.ppermute(value, axis, [(at, at ^ 2) for at in range(count) if side_of...]
    ppermute x9, waiting for transfers between devices: 16.6 us -> 0.94 us  [ahead(): return lax.ppermute(value, axis, pairs)]
    ppermute x8, starting transfers between devices: 7.58 us -> 22.6 us  [flip(): return lax.ppermute(value, axis, [(at, at ^ bit) for at in range(count)])]
    ppermute x9, starting transfers between devices: 31.8 us -> 22.9 us  [ahead(): return lax.ppermute(value, axis, pairs)]
    ppermute x0 -> x1, starting transfers between devices: none -> 1.29 us  [to_side_0(): lax.ppermute(value, axis, [(at, at ^ 2) for at in range(count) if side_of...]
    ppermute x8, waiting for transfers between devices: 5.58 us -> 4.36 us  [flip(): return lax.ppermute(value, axis, [(at, at ^ bit) for at in range(count)])]
  transfers between devices with their start and end apart: 17 -> 18, of which waited for: 6 -> 4; matrix products, arithmetic and copies ran while one was open for 0% -> 0% of each run, Pallas kernels for 21% -> 19%
where the time goes in v4:
time: 91.5 us; the launch traced here: 91.1 us
  starting transfers between devices  46.8 us (51%)
  waiting for transfers between devices  23.4 us (26%)
  Pallas kernels  19.9 us (22%)
  between operations  0.96 us (1%)
    ppermute x9, starting transfers between devices, ahead(): return lax.ppermute(value, axis, pairs)  22.9 us
    ppermute x8, starting transfers between devices, flip(): return lax.ppermute(value, axis, [(at, at ^ bit) for at in range(count)])  22.6 us
    ppermute x1, waiting for transfers between devices, to_side_0(): lax.ppermute(value, axis, [(at, at ^ 2) for at in range(count) if side_of...  18.1 us
    pallas_call x1, Pallas kernels, hyena_near(): pl.pallas_call(functools.partial(hyena_near_body, filters), grid=(STEPS,)...  5.05 us
    pallas_call x1, Pallas kernels, attend(): pl.pallas_call(attend_body, in_specs=[SMEM] + [VMEM] * 5, out_specs=[VMEM...  4.85 us
    ppermute x8, waiting for transfers between devices, flip(): return lax.ppermute(value, axis, [(at, at ^ bit) for at in range(count)])  4.36 us
    pallas_call x2, Pallas kernels, attend_last(): pl.pallas_call(functools.partial(attend_last_body, pair), in_specs=[SMEM]...  2.78 us
    pallas_call x1, Pallas kernels, hyena_finish(): pl.pallas_call(functools.partial(hyena_out_body, modes), grid=(STEPS,), i...  2.44 us
  transfers between devices with their start and end apart: 18, of which 4 were waited for; matrix products, arithmetic and copies ran while one was open for 0% of the time, Pallas kernels for 19%

profile of v4, /device:TPU:0, one launch (start us, length us, event | category | flops | bytes accessed | tf_op | source)
XLA Modules:
  0.0 91.1 jit_solution(18281862506832745864)
XLA Ops:
  0.6 1.3 %front.1 = (bf16[3,128,1024]{2,1,0:T(8,128)(2,1)S(1)}, bf16[3,8,2048]{2,1,0:T(8,128)(2,1)S(1)}) custom-call(bf16[3,128,2048]{2,1,0:T(8,128)(2,1)} %bitcast.4, bf16[3,128,2048]{2,1,0:T(8,128)(2,1)} %bitcast.10), custom_call_target="tpu_custom_call" | custom-call | bytes 1572864 | tf_op jit(solution)/shard_map/front/pallas_call | solution.py:390
  1.9 0.6 collective-permute-start.7
  2.5 1.9 %collective-permute-done.7.theirs_ref.theirs = bf16[3,128,1024]{2,1,0:T(8,128)(2,1)S(1)} collective-permute-done((bf16[3,128,1024]{2,1,0:T(8,128)(2,1)S(1)}, bf16[3,128,1024]{2,1,0:T(8,128)(2,1)S(1)}, u32[]{:S(2)}, u32[]{:S(2)}) %collective-permute-start.7) | collective-permute-done | bytes 786464 | tf_op jit(solution)/shard_map/ppermute | solution.py:24
  4.4 0.1 pack.3
  4.5 5.8 %collective-permute-start.9 = (bf16[2,2,128,512]{3,2,1,0:T(8,128)(2,1)S(1)}, bf16[2,2,128,512]{3,2,1,0:T(8,128)(2,1)S(1)}, u32[]{:S(2)}, u32[]{:S(2)}) collective-permute-start(bf16[2,2,128,512]{3,2,1,0:T(8,128)(2,1)S(1)} %get-tuple-element.45), channel_id=1, source_target_pairs={{0,6},{1,7},{2,4},{3,5},{4,10},{5,11},{6,8},{7,9},{8,14},{9,15},{1... | collective-permute-start | bytes 1572872 | tf_op jit(solution)/shard_map/ppermute | solution.py:38
  10.4 3.6 %collective-permute-start.11 = (bf16[2,2,128,512]{3,2,1,0:T(8,128)(2,1)S(1)}, bf16[2,2,128,512]{3,2,1,0:T(8,128)(2,1)S(1)}, u32[]{:S(2)}, u32[]{:S(2)}) collective-permute-start(bf16[2,2,128,512]{3,2,1,0:T(8,128)(2,1)S(1)} %get-tuple-element.46), channel_id=1, source_target_pairs={{0,4},{1,5},{2,6},{3,7},{4,8},{5,9},{6,10},{7,11},{8,12},{9,13},{1... | collective-permute-start | bytes 1572872 | tf_op jit(solution)/shard_map/ppermute | solution.py:38
  14.0 0.1 pack.2
  14.1 0.6 collective-permute-start.8
  14.6 1.3 %collective-permute-start = (bf16[3,8,2048]{2,1,0:T(8,128)(2,1)S(1)}, bf16[3,8,2048]{2,1,0:T(8,128)(2,1)S(1)}, u32[]{:S(2)}, u32[]{:S(2)}) collective-permute-start(bf16[3,8,2048]{2,1,0:T(8,128)(2,1)S(1)} %get-tuple-element.28), channel_id=1, source_target_pairs={{0,1},{1,2},{2,3},{3,4},{4,5},{5,6},{6,7},{7,8},{8,9},{9,10},{10,1... | collective-permute-start | bytes 294920 | tf_op jit(solution)/shard_map/ppermute | solution.py:38
  15.9 0.9 %collective-permute-done.halo_ref = bf16[3,8,2048]{2,1,0:T(8,128)(2,1)S(1)} collective-permute-done((bf16[3,8,2048]{2,1,0:T(8,128)(2,1)S(1)}, bf16[3,8,2048]{2,1,0:T(8,128)(2,1)S(1)}, u32[]{:S(2)}, u32[]{:S(2)}) %collective-permute-start) | collective-permute-done | bytes 98336 | tf_op jit(solution)/shard_map/ppermute | solution.py:38
  16.9 2.3 %hyena_ends.1 = (bf16[128,2048]{1,0:T(8,128)(2,1)S(1)}, f32[16,1024]{1,0:T(8,128)S(1)}, f32[16,1024]{1,0:T(8,128)S(1)}, f32[16,1024]{1,0:T(8,128)S(1)}, f32[16,1024]{1,0:T(8,128)S(1)}) custom-call(bf16[3,128,2048]{2,1,0:T(8,128)(2,1)S(1)} %bitcast.11, bf16[3,8,2048]{2,1,0:T(8,128)(2,1)S(1)} %collective-permute-done.halo_ref, f32[3,3,2048]{2,1,0:T(4,128)S(1)} %copy-done.2, ...), custom_call_target="tpu_custom_call" | custom-call | flops 134217728 | bytes 2097152 | tf_op jit(solution)/shard_map/hyena_ends/pallas_call | solution.py:160
  19.2 15.2 %collective-permute-start.1 = (f32[16,1024]{1,0:T(8,128)S(1)}, f32[16,1024]{1,0:T(8,128)S(1)}, u32[]{:S(2)}, u32[]{:S(2)}) collective-permute-start(f32[16,1024]{1,0:T(8,128)S(1)} %get-tuple-element.35), channel_id=1, source_target_pairs={{0,1},{1,0},{2,3},{3,2},{4,5},{5,4},{6,7},{7,6},{8,9},{9,8},{10,11... | collective-permute-start | bytes 196616 | tf_op jit(solution)/shard_map/ppermute | solution.py:24
  34.4 0.7 collective-permute-start.10
  35.1 0.7 collective-permute-start.13
  35.9 2.8 %collective-permute-start.2 = (f32[16,1024]{1,0:T(8,128)S(1)}, f32[16,1024]{1,0:T(8,128)S(1)}, u32[]{:S(2)}, u32[]{:S(2)}) collective-permute-start(f32[16,1024]{1,0:T(8,128)S(1)} %get-tuple-element.37.refs_0_), channel_id=1, source_target_pairs={{0,2},{1,3},{2,0},{3,1},{4,6},{5,7},{6,4},{7,5},{8,10},{9,11},{10,... | collective-permute-start | bytes 196616 | tf_op jit(solution)/shard_map/ppermute | solution.py:24
  38.6 2.4 %collective-permute-done.2.refs_1_ = f32[16,1024]{1,0:T(8,128)S(1)} collective-permute-done((f32[16,1024]{1,0:T(8,128)S(1)}, f32[16,1024]{1,0:T(8,128)S(1)}, u32[]{:S(2)}, u32[]{:S(2)}) %collective-permute-start.2) | collective-permute-done | bytes 65568 | tf_op jit(solution)/shard_map/ppermute | solution.py:24
  41.1 0.7 collective-permute-start.3
  41.8 1.3 %collective-permute-start.4 = (f32[16,1024]{1,0:T(8,128)S(1)}, f32[16,1024]{1,0:T(8,128)S(1)}, u32[]{:S(2)}, u32[]{:S(2)}) collective-permute-start(f32[16,1024]{1,0:T(8,128)S(1)} %collective-permute-done.3.refs_0_), channel_id=1, source_target_pairs={{2,0},{3,1},{6,4},{7,5},{10,8},{11,9},{14,12},{15,13},{18,16},{19,... | collective-permute-start | bytes 196616 | tf_op jit(solution)/shard_map/ppermute | solution.py:43
  43.1 0.7 collective-permute-start.12
  43.8 18.1 %collective-permute-done.4.refs_1_ = f32[16,1024]{1,0:T(8,128)S(1)} collective-permute-done((f32[16,1024]{1,0:T(8,128)S(1)}, f32[16,1024]{1,0:T(8,128)S(1)}, u32[]{:S(2)}, u32[]{:S(2)}) %collective-permute-start.4) | collective-permute-done | bytes 65568 | tf_op jit(solution)/shard_map/ppermute | solution.py:43
  62.0 0.7 collective-permute-start.14
  62.7 8.8 %collective-permute-start.5 = (f32[16,1024]{1,0:T(8,128)S(1)}, f32[16,1024]{1,0:T(8,128)S(1)}, u32[]{:S(2)}, u32[]{:S(2)}) collective-permute-start(f32[16,1024]{1,0:T(8,128)S(1)} %shard_map.80), channel_id=1, source_target_pairs={{0,8},{1,9},{2,10},{3,11},{4,12},{5,13},{6,14},{7,15},{16,24},{17,... | collective-permute-start | bytes 196616 | tf_op jit(solution)/shard_map/ppermute | solution.py:38
  71.5 4.8 %attend.1 = (f32[512,512]{1,0:T(8,128)S(1)}, f32[512,512]{1,0:T(8,128)S(1)}, f32[512,512]{1,0:T(8,128)S(1)}) custom-call(s32[4]{0:T(128)S(1)} %copy-done.5, bf16[3,128,2048]{2,1,0:T(8,128)(2,1)S(1)} %bitcast.7, bf16[3,128,1024]{2,1,0:T(8,128)(2,1)S(1)} %collective-permute-done.7.theirs_ref.theirs, bf16[2,3,128,512]{3,2,1,0:T(8,128)(2,1)S(1)} %collective-permute-done.8.swap, ...), custom_call_target="tpu_custom_call" | custom-call | flops 872415232 | bytes 3670016 | tf_op jit(solution)/shard_map/attend/pallas_call | solution.py:555
  76.4 1.1 %attend_last.3 = (bf16[128,512]{1,0:T(8,128)(2,1)S(1)}, bf16[128,512]{1,0:T(8,128)(2,1)S(1)}) custom-call(s32[4]{0:T(128)S(1)} %copy-done.5, bf16[3,128,2048]{2,1,0:T(8,128)(2,1)S(1)} %bitcast.8, bf16[3,128,1024]{2,1,0:T(8,128)(2,1)S(1)} %collective-permute-done.7.theirs_ref.theirs, bf16[2,3,128,512]{3,2,1,0:T(8,128)(2,1)S(1)} %collective-permute-done.8.swap, ...), custom_call_target="tpu_custom_call" | custom-call | flops 134217728 | bytes 1572864 | tf_op jit(solution)/shard_map/attend_last/pallas_call | solution.py:635
  77.6 2.8 %collective-permute-start.16 = (bf16[128,512]{1,0:T(8,128)(2,1)S(1)}, bf16[128,512]{1,0:T(8,128)(2,1)S(1)}, u32[]{:S(2)}, u32[]{:S(2)}) collective-permute-start(bf16[128,512]{1,0:T(8,128)(2,1)S(1)} %get-tuple-element.52), channel_id=1, source_target_pairs={{0,2},{1,3},{2,0},{3,1},{4,6},{5,7},{6,4},{7,5},{8,10},{9,11},{10,... | collective-permute-start | bytes 393224 | tf_op jit(solution)/shard_map/ppermute | solution.py:24
  80.4 1.6 %attend_last.2 = (bf16[128,512]{1,0:T(8,128)(2,1)S(1)}, bf16[128,512]{1,0:T(8,128)(2,1)S(1)}) custom-call(s32[4]{0:T(128)S(1)} %copy-done.5, bf16[3,128,2048]{2,1,0:T(8,128)(2,1)S(1)} %bitcast.9, bf16[3,128,1024]{2,1,0:T(8,128)(2,1)S(1)} %collective-permute-done.7.theirs_ref.theirs, bf16[2,3,128,512]{3,2,1,0:T(8,128)(2,1)S(1)} %collective-permute-done.8.swap, ...), custom_call_target="tpu_custom_call" | custom-call | flops 134217728 | bytes 1572864 | tf_op jit(solution)/shard_map/attend_last/pallas_call | solution.py:635
  82.1 0.3 collective-permute-start.15
  82.3 0.1 shard_map.81
  82.4 0.4 collective-permute-start.6
  82.8 5.1 %hyena_near.1 = (f32[128,2048]{1,0:T(8,128)S(1)}, f32[128,2048]{1,0:T(8,128)S(1)}, bf16[128,2048]{1,0:T(8,128)(2,1)S(1)}, bf16[128,2048]{1,0:T(8,128)(2,1)S(1)}) custom-call(bf16[3,128,2048]{2,1,0:T(8,128)(2,1)S(1)} %bitcast.12, bf16[3,8,2048]{2,1,0:T(8,128)(2,1)S(1)} %collective-permute-done.halo_ref, f32[3,3,2048]{2,1,0:T(4,128)S(1)} %copy-done.2, ...), custom_call_target="tpu_custom_call" | custom-call | flops 536870912 | bytes 3145728 | tf_op jit(solution)/shard_map/hyena_near/pallas_call | solution.py:229
  87.8 2.4 %hyena_finish.1 = bf16[128,2048]{1,0:T(8,128)(2,1)} custom-call(f32[128,2048]{1,0:T(8,128)S(1)} %get-tuple-element.30.near_ref, f32[128,2048]{1,0:T(8,128)S(1)} %get-tuple-element.31.q_ref, bf16[128,2048]{1,0:T(8,128)(2,1)S(1)} %get-tuple-element.32.high_ref, bf16[128,2048]{1,0:T(8,128)(2,1)S(1)} %get-tuple-element.33.low_ref, ...), custom_call_target="tpu_custom_call" | custom-call | flops 201326592 | bytes 2621440 | tf_op jit(solution)/shard_map/hyena_finish/pallas_call | solution.py:281
  90.3 0.8 assemble.1
  (33 shorter events, 0.2 us)
Async XLA Ops:
  0.6 3.8 %copy-start = (bf16[128,3,2048]{2,0,1:T(8,128)(2,1)S(1)}, bf16[128,3,2048]{2,0,1:T(8,128)(2,1)}, u32[]{:S(2)}) copy-start(bf16[128,3,2048]{2,0,1:T(8,128)(2,1)} %param.10) | copy-start | bytes 4718596
  1.9 2.5 %collective-permute-start.7 = (bf16[3,128,1024]{2,1,0:T(8,128)(2,1)S(1)}, bf16[3,128,1024]{2,1,0:T(8,128)(2,1)S(1)}, u32[]{:S(2)}, u32[]{:S(2)}) collective-permute-start(bf16[3,128,1024]{2,1,0:T(8,128)(2,1)S(1)} %get-tuple-element.44), channel_id=1, source_target_pairs={{0,1},{1,0},{2,3},{3,2},{4,5},{5,4},{6,7},{7,6},{8,9},{9,8},{10,11... | collective-permute-start | bytes 2359304 | tf_op jit(solution)/shard_map/ppermute | solution.py:24
  4.5 29.9 %collective-permute-start.9 = (bf16[2,2,128,512]{3,2,1,0:T(8,128)(2,1)S(1)}, bf16[2,2,128,512]{3,2,1,0:T(8,128)(2,1)S(1)}, u32[]{:S(2)}, u32[]{:S(2)}) collective-permute-start(bf16[2,2,128,512]{3,2,1,0:T(8,128)(2,1)S(1)} %get-tuple-element.45), channel_id=1, source_target_pairs={{0,6},{1,7},{2,4},{3,5},{4,10},{5,11},{6,8},{7,9},{8,14},{9,15},{1... | collective-permute-start | bytes 1572872 | tf_op jit(solution)/shard_map/ppermute | solution.py:38
  10.3 6.5 %copy-start.1 = (bf16[128,3,2048]{2,0,1:T(8,128)(2,1)S(1)}, bf16[128,3,2048]{2,0,1:T(8,128)(2,1)}, u32[]{:S(2)}) copy-start(bf16[128,3,2048]{2,0,1:T(8,128)(2,1)} %param.6) | copy-start | bytes 4718596
  10.3 6.5 %copy-start.2 = (f32[3,3,2048]{2,1,0:T(4,128)S(1)}, f32[3,3,2048]{2,1,0:T(4,128)}, u32[]{:S(2)}) copy-start(f32[3,3,2048]{2,1,0:T(4,128)} %w_ref.3) | copy-start | bytes 221188
  10.3 6.5 %copy-start.3 = (f32[128,16]{0,1:T(8,128)S(1)}, f32[128,16]{0,1:T(8,128)}, u32[]{:S(2)}) copy-start(f32[128,16]{0,1:T(8,128)} %param.8) | copy-start | bytes 24580
  10.3 6.5 %copy-start.4 = (f32[128,16]{0,1:T(8,128)S(1)}, f32[128,16]{0,1:T(8,128)}, u32[]{:S(2)}) copy-start(f32[128,16]{0,1:T(8,128)} %param.9) | copy-start | bytes 24580
  10.4 24.7 %collective-permute-start.11 = (bf16[2,2,128,512]{3,2,1,0:T(8,128)(2,1)S(1)}, bf16[2,2,128,512]{3,2,1,0:T(8,128)(2,1)S(1)}, u32[]{:S(2)}, u32[]{:S(2)}) collective-permute-start(bf16[2,2,128,512]{3,2,1,0:T(8,128)(2,1)S(1)} %get-tuple-element.46), channel_id=1, source_target_pairs={{0,4},{1,5},{2,6},{3,7},{4,8},{5,9},{6,10},{7,11},{8,12},{9,13},{1... | collective-permute-start | bytes 1572872 | tf_op jit(solution)/shard_map/ppermute | solution.py:38
  14.1 48.7 %collective-permute-start.8 = (bf16[2,3,128,512]{3,2,1,0:T(8,128)(2,1)S(1)}, bf16[2,3,128,512]{3,2,1,0:T(8,128)(2,1)S(1)}, u32[]{:S(2)}, u32[]{:S(2)}) collective-permute-start(bf16[2,3,128,512]{3,2,1,0:T(8,128)(2,1)S(1)} %pack.2), channel_id=1, source_target_pairs={{0,2},{1,3},{2,0},{3,1},{4,6},{5,7},{6,4},{7,5},{8,10},{9,11},{10,... | collective-permute-start | bytes 2359304 | tf_op jit(solution)/shard_map/ppermute | solution.py:24
  14.6 2.2 %collective-permute-start = (bf16[3,8,2048]{2,1,0:T(8,128)(2,1)S(1)}, bf16[3,8,2048]{2,1,0:T(8,128)(2,1)S(1)}, u32[]{:S(2)}, u32[]{:S(2)}) collective-permute-start(bf16[3,8,2048]{2,1,0:T(8,128)(2,1)S(1)} %get-tuple-element.28), channel_id=1, source_target_pairs={{0,1},{1,2},{2,3},{3,4},{4,5},{5,6},{6,7},{7,8},{8,9},{9,10},{10,1... | collective-permute-start | bytes 294920 | tf_op jit(solution)/shard_map/ppermute | solution.py:38
  19.2 52.4 %copy-start.5 = (s32[4]{0:T(128)S(1)}, s32[4]{0:T(128)}, u32[]{:S(2)}) copy-start(s32[4]{0:T(128)} %docs_ref.5) | copy-start | bytes 52
  19.2 16.6 %collective-permute-start.1 = (f32[16,1024]{1,0:T(8,128)S(1)}, f32[16,1024]{1,0:T(8,128)S(1)}, u32[]{:S(2)}, u32[]{:S(2)}) collective-permute-start(f32[16,1024]{1,0:T(8,128)S(1)} %get-tuple-element.35), channel_id=1, source_target_pairs={{0,1},{1,0},{2,3},{3,2},{4,5},{5,4},{6,7},{7,6},{8,9},{9,8},{10,11... | collective-permute-start | bytes 196616 | tf_op jit(solution)/shard_map/ppermute | solution.py:24
  34.4 42.0 %collective-permute-start.10 = (bf16[2,2,128,512]{3,2,1,0:T(8,128)(2,1)S(1)}, bf16[2,2,128,512]{3,2,1,0:T(8,128)(2,1)S(1)}, u32[]{:S(2)}, u32[]{:S(2)}) collective-permute-start(bf16[2,2,128,512]{3,2,1,0:T(8,128)(2,1)S(1)} %collective-permute-done.9.pairs.cross), channel_id=1, source_target_pairs={{4,8},{5,9},{8,12},{9,13},{20,24},{21,25},{24,28},{25,29}} | collective-permute-start | bytes 1572872 | tf_op jit(solution)/shard_map/ppermute | solution.py:38
  35.1 41.3 %collective-permute-start.13 = (bf16[2,2,128,512]{3,2,1,0:T(8,128)(2,1)S(1)}, bf16[2,2,128,512]{3,2,1,0:T(8,128)(2,1)S(1)}, u32[]{:S(2)}, u32[]{:S(2)}) collective-permute-start(bf16[2,2,128,512]{3,2,1,0:T(8,128)(2,1)S(1)} %collective-permute-done.11.pairs.own), channel_id=1, source_target_pairs={{6,10},{7,11},{10,14},{11,15},{22,26},{23,27},{26,30},{27,31}} | collective-permute-start | bytes 1572872 | tf_op jit(solution)/shard_map/ppermute | solution.py:38
  35.9 5.2 %collective-permute-start.2 = (f32[16,1024]{1,0:T(8,128)S(1)}, f32[16,1024]{1,0:T(8,128)S(1)}, u32[]{:S(2)}, u32[]{:S(2)}) collective-permute-start(f32[16,1024]{1,0:T(8,128)S(1)} %get-tuple-element.37.refs_0_), channel_id=1, source_target_pairs={{0,2},{1,3},{2,0},{3,1},{4,6},{5,7},{6,4},{7,5},{8,10},{9,11},{10,... | collective-permute-start | bytes 196616 | tf_op jit(solution)/shard_map/ppermute | solution.py:24
  41.1 0.7 collective-permute-start.3
  41.8 20.2 %collective-permute-start.4 = (f32[16,1024]{1,0:T(8,128)S(1)}, f32[16,1024]{1,0:T(8,128)S(1)}, u32[]{:S(2)}, u32[]{:S(2)}) collective-permute-start(f32[16,1024]{1,0:T(8,128)S(1)} %collective-permute-done.3.refs_0_), channel_id=1, source_target_pairs={{2,0},{3,1},{6,4},{7,5},{10,8},{11,9},{14,12},{15,13},{18,16},{19,... | collective-permute-start | bytes 196616 | tf_op jit(solution)/shard_map/ppermute | solution.py:43
  43.1 33.3 %collective-permute-start.12 = (bf16[1,2,128,512]{3,2,1,0:T(8,128)(2,1)S(1)}, bf16[1,2,128,512]{3,2,1,0:T(8,128)(2,1)S(1)}, u32[]{:S(2)}, u32[]{:S(2)}) collective-permute-start(bf16[1,2,128,512]{3,2,1,0:T(8,128)(2,1)S(1)} %odd.2), channel_id=1, source_target_pairs={{4,8},{5,9},{8,12},{9,13},{20,24},{21,25},{24,28},{25,29}} | collective-permute-start | bytes 786440 | tf_op jit(solution)/shard_map/ppermute | solution.py:38
  62.0 14.4 %collective-permute-start.14 = (bf16[1,2,128,512]{3,2,1,0:T(8,128)(2,1)S(1)}, bf16[1,2,128,512]{3,2,1,0:T(8,128)(2,1)S(1)}, u32[]{:S(2)}, u32[]{:S(2)}) collective-permute-start(bf16[1,2,128,512]{3,2,1,0:T(8,128)(2,1)S(1)} %odd.3), channel_id=1, source_target_pairs={{6,10},{7,11},{10,14},{11,15},{22,26},{23,27},{26,30},{27,31}} | collective-permute-start | bytes 786440 | tf_op jit(solution)/shard_map/ppermute | solution.py:38
  62.7 19.6 %collective-permute-start.5 = (f32[16,1024]{1,0:T(8,128)S(1)}, f32[16,1024]{1,0:T(8,128)S(1)}, u32[]{:S(2)}, u32[]{:S(2)}) collective-permute-start(f32[16,1024]{1,0:T(8,128)S(1)} %shard_map.80), channel_id=1, source_target_pairs={{0,8},{1,9},{2,10},{3,11},{4,12},{5,13},{6,14},{7,15},{16,24},{17,... | collective-permute-start | bytes 196616 | tf_op jit(solution)/shard_map/ppermute | solution.py:38
  77.6 12.7 %collective-permute-start.16 = (bf16[128,512]{1,0:T(8,128)(2,1)S(1)}, bf16[128,512]{1,0:T(8,128)(2,1)S(1)}, u32[]{:S(2)}, u32[]{:S(2)}) collective-permute-start(bf16[128,512]{1,0:T(8,128)(2,1)S(1)} %get-tuple-element.52), channel_id=1, source_target_pairs={{0,2},{1,3},{2,0},{3,1},{4,6},{5,7},{6,4},{7,5},{8,10},{9,11},{10,... | collective-permute-start | bytes 393224 | tf_op jit(solution)/shard_map/ppermute | solution.py:24
  80.4 9.9 %collective-permute-start.17 = (bf16[128,512]{1,0:T(8,128)(2,1)S(1)}, bf16[128,512]{1,0:T(8,128)(2,1)S(1)}, u32[]{:S(2)}, u32[]{:S(2)}) collective-permute-start(bf16[128,512]{1,0:T(8,128)(2,1)S(1)} %get-tuple-element.53), channel_id=1, source_target_pairs={{0,3},{1,2},{2,1},{3,0},{4,7},{5,6},{6,5},{7,4},{8,11},{9,10},{10,... | collective-permute-start | bytes 393224 | tf_op jit(solution)/shard_map/ppermute | solution.py:24
  82.1 8.2 %collective-permute-start.15 = (bf16[128,512]{1,0:T(8,128)(2,1)S(1)}, bf16[128,512]{1,0:T(8,128)(2,1)S(1)}, u32[]{:S(2)}, u32[]{:S(2)}) collective-permute-start(bf16[128,512]{1,0:T(8,128)(2,1)S(1)} %get-tuple-element.51), channel_id=1, source_target_pairs={{0,1},{1,0},{2,3},{3,2},{4,5},{5,4},{6,7},{7,6},{8,9},{9,8},{10,11... | collective-permute-start | bytes 393224 | tf_op jit(solution)/shard_map/ppermute | solution.py:24
  82.4 5.4 %collective-permute-start.6 = (f32[16,1024]{1,0:T(8,128)S(1)}, f32[16,1024]{1,0:T(8,128)S(1)}, u32[]{:S(2)}, u32[]{:S(2)}) collective-permute-start(f32[16,1024]{1,0:T(8,128)S(1)} %get-tuple-element.43), channel_id=1, source_target_pairs={{0,1},{1,0},{2,3},{3,2},{4,5},{5,4},{6,7},{7,6},{8,9},{9,8},{10,11... | collective-permute-start | bytes 196616 | tf_op jit(solution)/shard_map/ppermute | solution.py:24

commit v5 on v4

--- a/solution.py
+++ b/solution.py
@@ -645,13 +645,16 @@
 
 def assemble_body(*refs):
     place = spot()[2]
-    *pieces, out_ref = refs
-    turns = len(pieces) // ROW
+    *pieces, out_ref, sems = refs
     lanes = pieces[0].shape[1]
+    copies = []
     for n, piece in enumerate(pieces):
-        maker = place ^ (n % ROW)
+        maker = place ^ n
         which = 2 * (maker & 1) + lax.shift_right_logical(maker, 1)
-        out_ref[:, lanes_from(which * turns + n // ROW, lanes)] = piece[...]
+        copies.append(pltpu.make_async_copy(piece, out_ref.at[:, lanes_from(which, lanes)], sems.at[n]))
+        copies[-1].start()
+    for copy in copies:
+        copy.wait()
 
 
 def assemble(pieces):
@@ -659,7 +662,8 @@
     return pl.pallas_call(
         assemble_body,
         in_specs=[VMEM] * len(pieces),
-        out_specs=VMEM,
+        out_specs=ANY,
+        scratch_shapes=[pltpu.SemaphoreType.DMA((ROW,))],
         out_shape=jax.ShapeDtypeStruct((rows, len(pieces) * lanes), BF16),
         compiler_params=limits(6),
         cost_estimate=cost(0, 4 * rows * lanes * len(pieces)),

time: 91.5 us -> 91.6 us (level)
  no operation moved by 1% of the time
where the time goes in v5:
time: 91.6 us; the launch traced here: 91.3 us
  starting transfers between devices  46.8 us (51%)
  waiting for transfers between devices  23.4 us (26%)
  Pallas kernels  19.9 us (22%)
  between operations  1.12 us (1%)
    ppermute x9, starting transfers between devices, ahead(): return lax.ppermute(value, axis, pairs)  22.9 us
    ppermute x8, starting transfers between devices, flip(): return lax.ppermute(value, axis, [(at, at ^ bit) for at in range(count)])  22.6 us
    ppermute x1, waiting for transfers between devices, to_side_0(): lax.ppermute(value, axis, [(at, at ^ 2) for at in range(count) if side_of...  18.1 us
    pallas_call x1, Pallas kernels, hyena_near(): pl.pallas_call(functools.partial(hyena_near_body, filters), grid=(STEPS,)...  5.05 us
    pallas_call x1, Pallas kernels, attend(): pl.pallas_call(attend_body, in_specs=[SMEM] + [VMEM] * 5, out_specs=[VMEM...  4.85 us
    ppermute x8, waiting for transfers between devices, flip(): return lax.ppermute(value, axis, [(at, at ^ bit) for at in range(count)])  4.36 us
    pallas_call x2, Pallas kernels, attend_last(): pl.pallas_call(functools.partial(attend_last_body, pair), in_specs=[SMEM]...  2.78 us
    pallas_call x1, Pallas kernels, hyena_finish(): pl.pallas_call(functools.partial(hyena_out_body, modes), grid=(STEPS,), i...  2.44 us
  transfers between devices with their start and end apart: 18, of which 4 were waited for; matrix products, arithmetic and copies ran while one was open for 0% of the time, Pallas kernels for 19%

profile of v5, /device:TPU:0, one launch (start us, length us, event | category | flops | bytes accessed | tf_op | source)
XLA Modules:
  0.0 91.3 jit_solution(2605516341357280076)
XLA Ops:
  0.6 1.3 %front.1 = (bf16[3,128,1024]{2,1,0:T(8,128)(2,1)S(1)}, bf16[3,8,2048]{2,1,0:T(8,128)(2,1)S(1)}) custom-call(bf16[3,128,2048]{2,1,0:T(8,128)(2,1)} %bitcast.4, bf16[3,128,2048]{2,1,0:T(8,128)(2,1)} %bitcast.10), custom_call_target="tpu_custom_call" | custom-call | bytes 1572864 | tf_op jit(solution)/shard_map/front/pallas_call | solution.py:390
  1.9 0.6 collective-permute-start.7
  2.5 1.9 %collective-permute-done.7.theirs_ref.theirs = bf16[3,128,1024]{2,1,0:T(8,128)(2,1)S(1)} collective-permute-done((bf16[3,128,1024]{2,1,0:T(8,128)(2,1)S(1)}, bf16[3,128,1024]{2,1,0:T(8,128)(2,1)S(1)}, u32[]{:S(2)}, u32[]{:S(2)}) %collective-permute-start.7) | collective-permute-done | bytes 786464 | tf_op jit(solution)/shard_map/ppermute | solution.py:24
  4.4 0.1 pack.3
  4.5 5.8 %collective-permute-start.9 = (bf16[2,2,128,512]{3,2,1,0:T(8,128)(2,1)S(1)}, bf16[2,2,128,512]{3,2,1,0:T(8,128)(2,1)S(1)}, u32[]{:S(2)}, u32[]{:S(2)}) collective-permute-start(bf16[2,2,128,512]{3,2,1,0:T(8,128)(2,1)S(1)} %get-tuple-element.45), channel_id=1, source_target_pairs={{0,6},{1,7},{2,4},{3,5},{4,10},{5,11},{6,8},{7,9},{8,14},{9,15},{1... | collective-permute-start | bytes 1572872 | tf_op jit(solution)/shard_map/ppermute | solution.py:38
  10.4 3.6 %collective-permute-start.11 = (bf16[2,2,128,512]{3,2,1,0:T(8,128)(2,1)S(1)}, bf16[2,2,128,512]{3,2,1,0:T(8,128)(2,1)S(1)}, u32[]{:S(2)}, u32[]{:S(2)}) collective-permute-start(bf16[2,2,128,512]{3,2,1,0:T(8,128)(2,1)S(1)} %get-tuple-element.46), channel_id=1, source_target_pairs={{0,4},{1,5},{2,6},{3,7},{4,8},{5,9},{6,10},{7,11},{8,12},{9,13},{1... | collective-permute-start | bytes 1572872 | tf_op jit(solution)/shard_map/ppermute | solution.py:38
  14.0 0.1 pack.2
  14.1 0.6 collective-permute-start.8
  14.6 1.3 %collective-permute-start = (bf16[3,8,2048]{2,1,0:T(8,128)(2,1)S(1)}, bf16[3,8,2048]{2,1,0:T(8,128)(2,1)S(1)}, u32[]{:S(2)}, u32[]{:S(2)}) collective-permute-start(bf16[3,8,2048]{2,1,0:T(8,128)(2,1)S(1)} %get-tuple-element.28), channel_id=1, source_target_pairs={{0,1},{1,2},{2,3},{3,4},{4,5},{5,6},{6,7},{7,8},{8,9},{9,10},{10,1... | collective-permute-start | bytes 294920 | tf_op jit(solution)/shard_map/ppermute | solution.py:38
  15.9 0.9 %collective-permute-done.halo_ref = bf16[3,8,2048]{2,1,0:T(8,128)(2,1)S(1)} collective-permute-done((bf16[3,8,2048]{2,1,0:T(8,128)(2,1)S(1)}, bf16[3,8,2048]{2,1,0:T(8,128)(2,1)S(1)}, u32[]{:S(2)}, u32[]{:S(2)}) %collective-permute-start) | collective-permute-done | bytes 98336 | tf_op jit(solution)/shard_map/ppermute | solution.py:38
  16.9 2.3 %hyena_ends.1 = (bf16[128,2048]{1,0:T(8,128)(2,1)S(1)}, f32[16,1024]{1,0:T(8,128)S(1)}, f32[16,1024]{1,0:T(8,128)S(1)}, f32[16,1024]{1,0:T(8,128)S(1)}, f32[16,1024]{1,0:T(8,128)S(1)}) custom-call(bf16[3,128,2048]{2,1,0:T(8,128)(2,1)S(1)} %bitcast.11, bf16[3,8,2048]{2,1,0:T(8,128)(2,1)S(1)} %collective-permute-done.halo_ref, f32[3,3,2048]{2,1,0:T(4,128)S(1)} %copy-done.2, ...), custom_call_target="tpu_custom_call" | custom-call | flops 134217728 | bytes 2097152 | tf_op jit(solution)/shard_map/hyena_ends/pallas_call | solution.py:160
  19.2 15.2 %collective-permute-start.1 = (f32[16,1024]{1,0:T(8,128)S(1)}, f32[16,1024]{1,0:T(8,128)S(1)}, u32[]{:S(2)}, u32[]{:S(2)}) collective-permute-start(f32[16,1024]{1,0:T(8,128)S(1)} %get-tuple-element.35), channel_id=1, source_target_pairs={{0,1},{1,0},{2,3},{3,2},{4,5},{5,4},{6,7},{7,6},{8,9},{9,8},{10,11... | collective-permute-start | bytes 196616 | tf_op jit(solution)/shard_map/ppermute | solution.py:24
  34.4 0.7 collective-permute-start.10
  35.1 0.7 collective-permute-start.13
  35.9 2.8 %collective-permute-start.2 = (f32[16,1024]{1,0:T(8,128)S(1)}, f32[16,1024]{1,0:T(8,128)S(1)}, u32[]{:S(2)}, u32[]{:S(2)}) collective-permute-start(f32[16,1024]{1,0:T(8,128)S(1)} %get-tuple-element.37.refs_0_), channel_id=1, source_target_pairs={{0,2},{1,3},{2,0},{3,1},{4,6},{5,7},{6,4},{7,5},{8,10},{9,11},{10,... | collective-permute-start | bytes 196616 | tf_op jit(solution)/shard_map/ppermute | solution.py:24
  38.6 2.4 %collective-permute-done.2.refs_1_ = f32[16,1024]{1,0:T(8,128)S(1)} collective-permute-done((f32[16,1024]{1,0:T(8,128)S(1)}, f32[16,1024]{1,0:T(8,128)S(1)}, u32[]{:S(2)}, u32[]{:S(2)}) %collective-permute-start.2) | collective-permute-done | bytes 65568 | tf_op jit(solution)/shard_map/ppermute | solution.py:24
  41.1 0.7 collective-permute-start.3
  41.8 1.3 %collective-permute-start.4 = (f32[16,1024]{1,0:T(8,128)S(1)}, f32[16,1024]{1,0:T(8,128)S(1)}, u32[]{:S(2)}, u32[]{:S(2)}) collective-permute-start(f32[16,1024]{1,0:T(8,128)S(1)} %collective-permute-done.3.refs_0_), channel_id=1, source_target_pairs={{2,0},{3,1},{6,4},{7,5},{10,8},{11,9},{14,12},{15,13},{18,16},{19,... | collective-permute-start | bytes 196616 | tf_op jit(solution)/shard_map/ppermute | solution.py:43
  43.1 0.7 collective-permute-start.12
  43.8 18.1 %collective-permute-done.4.refs_1_ = f32[16,1024]{1,0:T(8,128)S(1)} collective-permute-done((f32[16,1024]{1,0:T(8,128)S(1)}, f32[16,1024]{1,0:T(8,128)S(1)}, u32[]{:S(2)}, u32[]{:S(2)}) %collective-permute-start.4) | collective-permute-done | bytes 65568 | tf_op jit(solution)/shard_map/ppermute | solution.py:43
  62.0 0.7 collective-permute-start.14
  62.7 8.8 %collective-permute-start.5 = (f32[16,1024]{1,0:T(8,128)S(1)}, f32[16,1024]{1,0:T(8,128)S(1)}, u32[]{:S(2)}, u32[]{:S(2)}) collective-permute-start(f32[16,1024]{1,0:T(8,128)S(1)} %shard_map.80), channel_id=1, source_target_pairs={{0,8},{1,9},{2,10},{3,11},{4,12},{5,13},{6,14},{7,15},{16,24},{17,... | collective-permute-start | bytes 196616 | tf_op jit(solution)/shard_map/ppermute | solution.py:38
  71.5 4.8 %attend.1 = (f32[512,512]{1,0:T(8,128)S(1)}, f32[512,512]{1,0:T(8,128)S(1)}, f32[512,512]{1,0:T(8,128)S(1)}) custom-call(s32[4]{0:T(128)S(1)} %copy-done.5, bf16[3,128,2048]{2,1,0:T(8,128)(2,1)S(1)} %bitcast.7, bf16[3,128,1024]{2,1,0:T(8,128)(2,1)S(1)} %collective-permute-done.7.theirs_ref.theirs, bf16[2,3,128,512]{3,2,1,0:T(8,128)(2,1)S(1)} %collective-permute-done.8.swap, ...), custom_call_target="tpu_custom_call" | custom-call | flops 872415232 | bytes 3670016 | tf_op jit(solution)/shard_map/attend/pallas_call | solution.py:555
  76.4 1.1 %attend_last.3 = (bf16[128,512]{1,0:T(8,128)(2,1)S(1)}, bf16[128,512]{1,0:T(8,128)(2,1)S(1)}) custom-call(s32[4]{0:T(128)S(1)} %copy-done.5, bf16[3,128,2048]{2,1,0:T(8,128)(2,1)S(1)} %bitcast.8, bf16[3,128,1024]{2,1,0:T(8,128)(2,1)S(1)} %collective-permute-done.7.theirs_ref.theirs, bf16[2,3,128,512]{3,2,1,0:T(8,128)(2,1)S(1)} %collective-permute-done.8.swap, ...), custom_call_target="tpu_custom_call" | custom-call | flops 134217728 | bytes 1572864 | tf_op jit(solution)/shard_map/attend_last/pallas_call | solution.py:635
  77.6 2.8 %collective-permute-start.16 = (bf16[128,512]{1,0:T(8,128)(2,1)S(1)}, bf16[128,512]{1,0:T(8,128)(2,1)S(1)}, u32[]{:S(2)}, u32[]{:S(2)}) collective-permute-start(bf16[128,512]{1,0:T(8,128)(2,1)S(1)} %get-tuple-element.52), channel_id=1, source_target_pairs={{0,2},{1,3},{2,0},{3,1},{4,6},{5,7},{6,4},{7,5},{8,10},{9,11},{10,... | collective-permute-start | bytes 393224 | tf_op jit(solution)/shard_map/ppermute | solution.py:24
  80.4 1.6 %attend_last.2 = (bf16[128,512]{1,0:T(8,128)(2,1)S(1)}, bf16[128,512]{1,0:T(8,128)(2,1)S(1)}) custom-call(s32[4]{0:T(128)S(1)} %copy-done.5, bf16[3,128,2048]{2,1,0:T(8,128)(2,1)S(1)} %bitcast.9, bf16[3,128,1024]{2,1,0:T(8,128)(2,1)S(1)} %collective-permute-done.7.theirs_ref.theirs, bf16[2,3,128,512]{3,2,1,0:T(8,128)(2,1)S(1)} %collective-permute-done.8.swap, ...), custom_call_target="tpu_custom_call" | custom-call | flops 134217728 | bytes 1572864 | tf_op jit(solution)/shard_map/attend_last/pallas_call | solution.py:635
  82.1 0.3 collective-permute-start.15
  82.3 0.1 shard_map.81
  82.4 0.4 collective-permute-start.6
  82.8 5.1 %hyena_near.1 = (f32[128,2048]{1,0:T(8,128)S(1)}, f32[128,2048]{1,0:T(8,128)S(1)}, bf16[128,2048]{1,0:T(8,128)(2,1)S(1)}, bf16[128,2048]{1,0:T(8,128)(2,1)S(1)}) custom-call(bf16[3,128,2048]{2,1,0:T(8,128)(2,1)S(1)} %bitcast.12, bf16[3,8,2048]{2,1,0:T(8,128)(2,1)S(1)} %collective-permute-done.halo_ref, f32[3,3,2048]{2,1,0:T(4,128)S(1)} %copy-done.2, ...), custom_call_target="tpu_custom_call" | custom-call | flops 536870912 | bytes 3145728 | tf_op jit(solution)/shard_map/hyena_near/pallas_call | solution.py:229
  87.8 2.4 %hyena_finish.1 = bf16[128,2048]{1,0:T(8,128)(2,1)} custom-call(f32[128,2048]{1,0:T(8,128)S(1)} %get-tuple-element.30.near_ref, f32[128,2048]{1,0:T(8,128)S(1)} %get-tuple-element.31.q_ref, bf16[128,2048]{1,0:T(8,128)(2,1)S(1)} %get-tuple-element.32.high_ref, bf16[128,2048]{1,0:T(8,128)(2,1)S(1)} %get-tuple-element.33.low_ref, ...), custom_call_target="tpu_custom_call" | custom-call | flops 201326592 | bytes 2621440 | tf_op jit(solution)/shard_map/hyena_finish/pallas_call | solution.py:281
  90.3 0.8 assemble.1
  (33 shorter events, 0.2 us)
Async XLA Ops:
  0.6 3.8 %copy-start = (bf16[128,3,2048]{2,0,1:T(8,128)(2,1)S(1)}, bf16[128,3,2048]{2,0,1:T(8,128)(2,1)}, u32[]{:S(2)}) copy-start(bf16[128,3,2048]{2,0,1:T(8,128)(2,1)} %param.10) | copy-start | bytes 4718596
  1.9 2.5 %collective-permute-start.7 = (bf16[3,128,1024]{2,1,0:T(8,128)(2,1)S(1)}, bf16[3,128,1024]{2,1,0:T(8,128)(2,1)S(1)}, u32[]{:S(2)}, u32[]{:S(2)}) collective-permute-start(bf16[3,128,1024]{2,1,0:T(8,128)(2,1)S(1)} %get-tuple-element.44), channel_id=1, source_target_pairs={{0,1},{1,0},{2,3},{3,2},{4,5},{5,4},{6,7},{7,6},{8,9},{9,8},{10,11... | collective-permute-start | bytes 2359304 | tf_op jit(solution)/shard_map/ppermute | solution.py:24
  4.5 29.9 %collective-permute-start.9 = (bf16[2,2,128,512]{3,2,1,0:T(8,128)(2,1)S(1)}, bf16[2,2,128,512]{3,2,1,0:T(8,128)(2,1)S(1)}, u32[]{:S(2)}, u32[]{:S(2)}) collective-permute-start(bf16[2,2,128,512]{3,2,1,0:T(8,128)(2,1)S(1)} %get-tuple-element.45), channel_id=1, source_target_pairs={{0,6},{1,7},{2,4},{3,5},{4,10},{5,11},{6,8},{7,9},{8,14},{9,15},{1... | collective-permute-start | bytes 1572872 | tf_op jit(solution)/shard_map/ppermute | solution.py:38
  10.3 6.5 %copy-start.1 = (bf16[128,3,2048]{2,0,1:T(8,128)(2,1)S(1)}, bf16[128,3,2048]{2,0,1:T(8,128)(2,1)}, u32[]{:S(2)}) copy-start(bf16[128,3,2048]{2,0,1:T(8,128)(2,1)} %param.6) | copy-start | bytes 4718596
  10.3 6.5 %copy-start.2 = (f32[3,3,2048]{2,1,0:T(4,128)S(1)}, f32[3,3,2048]{2,1,0:T(4,128)}, u32[]{:S(2)}) copy-start(f32[3,3,2048]{2,1,0:T(4,128)} %w_ref.3) | copy-start | bytes 221188
  10.3 6.5 %copy-start.3 = (f32[128,16]{0,1:T(8,128)S(1)}, f32[128,16]{0,1:T(8,128)}, u32[]{:S(2)}) copy-start(f32[128,16]{0,1:T(8,128)} %param.8) | copy-start | bytes 24580
  10.3 6.5 %copy-start.4 = (f32[128,16]{0,1:T(8,128)S(1)}, f32[128,16]{0,1:T(8,128)}, u32[]{:S(2)}) copy-start(f32[128,16]{0,1:T(8,128)} %param.9) | copy-start | bytes 24580
  10.4 24.7 %collective-permute-start.11 = (bf16[2,2,128,512]{3,2,1,0:T(8,128)(2,1)S(1)}, bf16[2,2,128,512]{3,2,1,0:T(8,128)(2,1)S(1)}, u32[]{:S(2)}, u32[]{:S(2)}) collective-permute-start(bf16[2,2,128,512]{3,2,1,0:T(8,128)(2,1)S(1)} %get-tuple-element.46), channel_id=1, source_target_pairs={{0,4},{1,5},{2,6},{3,7},{4,8},{5,9},{6,10},{7,11},{8,12},{9,13},{1... | collective-permute-start | bytes 1572872 | tf_op jit(solution)/shard_map/ppermute | solution.py:38
  14.1 48.7 %collective-permute-start.8 = (bf16[2,3,128,512]{3,2,1,0:T(8,128)(2,1)S(1)}, bf16[2,3,128,512]{3,2,1,0:T(8,128)(2,1)S(1)}, u32[]{:S(2)}, u32[]{:S(2)}) collective-permute-start(bf16[2,3,128,512]{3,2,1,0:T(8,128)(2,1)S(1)} %pack.2), channel_id=1, source_target_pairs={{0,2},{1,3},{2,0},{3,1},{4,6},{5,7},{6,4},{7,5},{8,10},{9,11},{10,... | collective-permute-start | bytes 2359304 | tf_op jit(solution)/shard_map/ppermute | solution.py:24
  14.6 2.2 %collective-permute-start = (bf16[3,8,2048]{2,1,0:T(8,128)(2,1)S(1)}, bf16[3,8,2048]{2,1,0:T(8,128)(2,1)S(1)}, u32[]{:S(2)}, u32[]{:S(2)}) collective-permute-start(bf16[3,8,2048]{2,1,0:T(8,128)(2,1)S(1)} %get-tuple-element.28), channel_id=1, source_target_pairs={{0,1},{1,2},{2,3},{3,4},{4,5},{5,6},{6,7},{7,8},{8,9},{9,10},{10,1... | collective-permute-start | bytes 294920 | tf_op jit(solution)/shard_map/ppermute | solution.py:38
  19.2 52.4 %copy-start.5 = (s32[4]{0:T(128)S(1)}, s32[4]{0:T(128)}, u32[]{:S(2)}) copy-start(s32[4]{0:T(128)} %docs_ref.5) | copy-start | bytes 52
  19.2 16.6 %collective-permute-start.1 = (f32[16,1024]{1,0:T(8,128)S(1)}, f32[16,1024]{1,0:T(8,128)S(1)}, u32[]{:S(2)}, u32[]{:S(2)}) collective-permute-start(f32[16,1024]{1,0:T(8,128)S(1)} %get-tuple-element.35), channel_id=1, source_target_pairs={{0,1},{1,0},{2,3},{3,2},{4,5},{5,4},{6,7},{7,6},{8,9},{9,8},{10,11... | collective-permute-start | bytes 196616 | tf_op jit(solution)/shard_map/ppermute | solution.py:24
  34.4 42.0 %collective-permute-start.10 = (bf16[2,2,128,512]{3,2,1,0:T(8,128)(2,1)S(1)}, bf16[2,2,128,512]{3,2,1,0:T(8,128)(2,1)S(1)}, u32[]{:S(2)}, u32[]{:S(2)}) collective-permute-start(bf16[2,2,128,512]{3,2,1,0:T(8,128)(2,1)S(1)} %collective-permute-done.9.pairs.cross), channel_id=1, source_target_pairs={{4,8},{5,9},{8,12},{9,13},{20,24},{21,25},{24,28},{25,29}} | collective-permute-start | bytes 1572872 | tf_op jit(solution)/shard_map/ppermute | solution.py:38
  35.1 41.3 %collective-permute-start.13 = (bf16[2,2,128,512]{3,2,1,0:T(8,128)(2,1)S(1)}, bf16[2,2,128,512]{3,2,1,0:T(8,128)(2,1)S(1)}, u32[]{:S(2)}, u32[]{:S(2)}) collective-permute-start(bf16[2,2,128,512]{3,2,1,0:T(8,128)(2,1)S(1)} %collective-permute-done.11.pairs.own), channel_id=1, source_target_pairs={{6,10},{7,11},{10,14},{11,15},{22,26},{23,27},{26,30},{27,31}} | collective-permute-start | bytes 1572872 | tf_op jit(solution)/shard_map/ppermute | solution.py:38
  35.9 5.2 %collective-permute-start.2 = (f32[16,1024]{1,0:T(8,128)S(1)}, f32[16,1024]{1,0:T(8,128)S(1)}, u32[]{:S(2)}, u32[]{:S(2)}) collective-permute-start(f32[16,1024]{1,0:T(8,128)S(1)} %get-tuple-element.37.refs_0_), channel_id=1, source_target_pairs={{0,2},{1,3},{2,0},{3,1},{4,6},{5,7},{6,4},{7,5},{8,10},{9,11},{10,... | collective-permute-start | bytes 196616 | tf_op jit(solution)/shard_map/ppermute | solution.py:24
  41.1 0.7 collective-permute-start.3
  41.8 20.2 %collective-permute-start.4 = (f32[16,1024]{1,0:T(8,128)S(1)}, f32[16,1024]{1,0:T(8,128)S(1)}, u32[]{:S(2)}, u32[]{:S(2)}) collective-permute-start(f32[16,1024]{1,0:T(8,128)S(1)} %collective-permute-done.3.refs_0_), channel_id=1, source_target_pairs={{2,0},{3,1},{6,4},{7,5},{10,8},{11,9},{14,12},{15,13},{18,16},{19,... | collective-permute-start | bytes 196616 | tf_op jit(solution)/shard_map/ppermute | solution.py:43
  43.1 33.3 %collective-permute-start.12 = (bf16[1,2,128,512]{3,2,1,0:T(8,128)(2,1)S(1)}, bf16[1,2,128,512]{3,2,1,0:T(8,128)(2,1)S(1)}, u32[]{:S(2)}, u32[]{:S(2)}) collective-permute-start(bf16[1,2,128,512]{3,2,1,0:T(8,128)(2,1)S(1)} %odd.2), channel_id=1, source_target_pairs={{4,8},{5,9},{8,12},{9,13},{20,24},{21,25},{24,28},{25,29}} | collective-permute-start | bytes 786440 | tf_op jit(solution)/shard_map/ppermute | solution.py:38
  62.0 14.4 %collective-permute-start.14 = (bf16[1,2,128,512]{3,2,1,0:T(8,128)(2,1)S(1)}, bf16[1,2,128,512]{3,2,1,0:T(8,128)(2,1)S(1)}, u32[]{:S(2)}, u32[]{:S(2)}) collective-permute-start(bf16[1,2,128,512]{3,2,1,0:T(8,128)(2,1)S(1)} %odd.3), channel_id=1, source_target_pairs={{6,10},{7,11},{10,14},{11,15},{22,26},{23,27},{26,30},{27,31}} | collective-permute-start | bytes 786440 | tf_op jit(solution)/shard_map/ppermute | solution.py:38
  62.7 19.6 %collective-permute-start.5 = (f32[16,1024]{1,0:T(8,128)S(1)}, f32[16,1024]{1,0:T(8,128)S(1)}, u32[]{:S(2)}, u32[]{:S(2)}) collective-permute-start(f32[16,1024]{1,0:T(8,128)S(1)} %shard_map.80), channel_id=1, source_target_pairs={{0,8},{1,9},{2,10},{3,11},{4,12},{5,13},{6,14},{7,15},{16,24},{17,... | collective-permute-start | bytes 196616 | tf_op jit(solution)/shard_map/ppermute | solution.py:38
  77.6 12.7 %collective-permute-start.16 = (bf16[128,512]{1,0:T(8,128)(2,1)S(1)}, bf16[128,512]{1,0:T(8,128)(2,1)S(1)}, u32[]{:S(2)}, u32[]{:S(2)}) collective-permute-start(bf16[128,512]{1,0:T(8,128)(2,1)S(1)} %get-tuple-element.52), channel_id=1, source_target_pairs={{0,2},{1,3},{2,0},{3,1},{4,6},{5,7},{6,4},{7,5},{8,10},{9,11},{10,... | collective-permute-start | bytes 393224 | tf_op jit(solution)/shard_map/ppermute | solution.py:24
  80.4 9.9 %collective-permute-start.17 = (bf16[128,512]{1,0:T(8,128)(2,1)S(1)}, bf16[128,512]{1,0:T(8,128)(2,1)S(1)}, u32[]{:S(2)}, u32[]{:S(2)}) collective-permute-start(bf16[128,512]{1,0:T(8,128)(2,1)S(1)} %get-tuple-element.53), channel_id=1, source_target_pairs={{0,3},{1,2},{2,1},{3,0},{4,7},{5,6},{6,5},{7,4},{8,11},{9,10},{10,... | collective-permute-start | bytes 393224 | tf_op jit(solution)/shard_map/ppermute | solution.py:24
  82.1 8.2 %collective-permute-start.15 = (bf16[128,512]{1,0:T(8,128)(2,1)S(1)}, bf16[128,512]{1,0:T(8,128)(2,1)S(1)}, u32[]{:S(2)}, u32[]{:S(2)}) collective-permute-start(bf16[128,512]{1,0:T(8,128)(2,1)S(1)} %get-tuple-element.51), channel_id=1, source_target_pairs={{0,1},{1,0},{2,3},{3,2},{4,5},{5,4},{6,7},{7,6},{8,9},{9,8},{10,11... | collective-permute-start | bytes 393224 | tf_op jit(solution)/shard_map/ppermute | solution.py:24
  82.4 5.4 %collective-permute-start.6 = (f32[16,1024]{1,0:T(8,128)S(1)}, f32[16,1024]{1,0:T(8,128)S(1)}, u32[]{:S(2)}, u32[]{:S(2)}) collective-permute-start(f32[16,1024]{1,0:T(8,128)S(1)} %get-tuple-element.43), channel_id=1, source_target_pairs={{0,1},{1,0},{2,3},{3,2},{4,5},{5,4},{6,7},{7,6},{8,9},{9,8},{10,11... | collective-permute-start | bytes 196616 | tf_op jit(solution)/shard_map/ppermute | solution.py:24
